TPU v7x, 32 devices: a whole 2x2x4 slice. The times are simulated.
32 devices in a mesh: mem: 4 (over z), space: 8 (over y, x, core).
Axes of the slice: x: 2, y: 2, z: 4, core: 2. Of those that a mesh axis runs over, the one named last changes fastest.
Arguments:
- ensemble: float32 [128, 16, 2048], P('mem', 'space'), may hold values from -6 to 6
- forcing: float32 [16, 2048], P('space'), may hold values from 2 to 8
- obs_cell: int32 [1024], P('space'), may hold values from 0 to 32767, as said below
- obs_value: float32 [1024], P('space'), may hold values from -8 to 8
- obs_var: float32 [1024], P('space'), may hold values from 0.5 to 2
- obs_noise: float32 [128, 1024], P('mem', 'space'), may hold values from -5 to 5
Outputs:
- analysis: float32 [128, 16, 2048], P('mem', 'space')
Inputs may be any that keep to these rules, and one draw needn't show every extreme that they name: `obs_cell`: entries 128 * s to 128 * (s + 1) - 1 name cells of planes 2 * s to 2 * (s + 1) - 1, a cell of plane x and position p having index x * 2048 + p.
All inputs are finite; a program needn't handle non-finite values.
Results may differ from a plain program's by a relative error of at most 0.00018.
Values sent between devices are 32-bit elements; how exact they have to be, the bound alone decides.
No kernel may reach another device: no remote copies, remote signals or barrier semaphores. Data moves between devices by JAX's collectives and lax.ppermute only.
A program may use at most 64 MiB of HBM per device.

v0:
```python
import functools

import jax
import jax.numpy as jnp
from jax import lax
from jax.experimental import pallas as pl
from jax.experimental.pallas import tpu as pltpu
from jax.sharding import PartitionSpec as P


FSTEPS = 4
ITERS = 6
LANES = 128
SUBLANES = 8

time_step = 0.05
highest = lax.Precision.HIGHEST


def from_behind(value, axis, steps):
    count = lax.axis_size(axis)
    pairs = [(source, (source + steps) % count) for source in range(count)]
    return lax.ppermute(value, axis, pairs)


def flipped(value, axis, mask):
    count = lax.axis_size(axis)
    return lax.ppermute(value, axis, [(i, i ^ mask) for i in range(count)])


def padded_2(x, sides, width):
    for axis, dim in sides:
        size, length = (lax.axis_size(axis), x.shape[dim])
        up = [(i, (i + 1) % size) for i in range(size)]
        down = [(j, i) for i, j in up]
        last = lax.slice_in_dim(x, length - width, length, axis=dim)
        initial = lax.slice_in_dim(x, 0, width, axis=dim)
        before = lax.ppermute(last, axis, up)
        after = lax.ppermute(initial, axis, down)
        x = jnp.concatenate([before, x, after], axis=dim)
    return x


def taper_of(planes_a, planes_b, planes_all, reach_planes):
    spread = jnp.abs(planes_a[:, None] - planes_b[None, :])
    spread = jnp.minimum(spread, planes_all - spread)
    return jnp.maximum(0.0, 1.0 - spread.astype(jnp.float32) / reach_planes)


def collect_band(values, along, reach_slabs):
    pieces = []
    for offset in range(-reach_slabs, reach_slabs + 1):
        if offset == 0:
            pieces.append(values)
        else:
            pieces.append(from_behind(values, "space", -offset))
    return jnp.concatenate(pieces, axis=along)


def banded(ensemble, forcing, obs_cell, obs_value, obs_var, obs_noise):
    members_dev, planes_dev, plane_cells = ensemble.shape
    obs_dev = obs_cell.shape[0]
    space_count = lax.axis_size("space")
    mem_count = lax.axis_size("mem")
    space_index = lax.axis_index("space")
    mem_index = lax.axis_index("mem")
    members = members_dev * mem_count
    planes_all = planes_dev * space_count
    reach_slabs = min(8, space_count // 4)
    reach_planes = planes_dev * reach_slabs
    band_width = reach_slabs * obs_dev
    states = ensemble
    for _ in range(FSTEPS):
        padded = padded_2(states, (("space", 1),), 2)
        forward_one = padded[:, 3 : 3 + planes_dev]
        back_one = padded[:, 1 : 1 + planes_dev]
        back_two = padded[:, 0:planes_dev]
        states = states + time_step * ((forward_one - back_two) * back_one - states + forcing)
    slab_cells = planes_dev * plane_cells
    local_cells = obs_cell - space_index * slab_cells
    observed = jnp.take(states.reshape(members_dev, slab_cells), local_cells, axis=1)
    own_planes = obs_cell // plane_cells
    own_rows = lax.all_gather(observed, "mem", axis=0, tiled=True)
    own_mean = jnp.sum(own_rows, axis=0) / members
    own_anom = own_rows - own_mean
    stacked = jnp.concatenate([own_anom, own_planes.astype(jnp.float32)[None, :]], axis=0)
    band = collect_band(stacked, 1, reach_slabs)
    context_anom = band[:members]
    context_planes = band[members].astype(jnp.int32)
    context_count = context_anom.shape[1]
    taper_block = taper_of(own_planes, context_planes, planes_all, reach_planes)
    gram_block = jnp.dot(own_anom.T, context_anom, precision=highest) / (members - 1)
    diagonal = jnp.arange(context_count)[None, :] == (band_width + jnp.arange(obs_dev))[:, None]
    covariance = taper_block * gram_block + jnp.where(diagonal, obs_var[:, None], 0.0)
    row_max = jnp.max(jnp.sum(jnp.abs(covariance), axis=1))
    var_min = jnp.min(obs_var)
    both = lax.pmax((row_max, -var_min), "space")
    upper_bound = both[0]
    lower_bound = -both[1]
    mean_rhs = obs_value - own_mean
    member_anom = lax.dynamic_slice_in_dim(own_anom, mem_index * members_dev, members_dev, 0)
    anom_rhs = (jnp.sqrt(obs_var)[None, :] * obs_noise - member_anom).T
    center = (upper_bound + lower_bound) / 2.0
    radius = (upper_bound - lower_bound) / 2.0
    sigma_ratio = center / radius
    rho_now = 1.0 / sigma_ratio
    resid_anom, resid_mean = (anom_rhs, mean_rhs)
    dir_anom, dir_mean = (anom_rhs / center, mean_rhs / center)
    anom_weight = jnp.zeros_like(anom_rhs)
    mean_weight = jnp.zeros_like(mean_rhs)
    for iteration in range(ITERS):
        anom_weight = anom_weight + dir_anom
        mean_weight = mean_weight + dir_mean
        if iteration < ITERS - 1:
            joined = jnp.concatenate([dir_anom, dir_mean[:, None]], axis=1)
            band_dirs = collect_band(joined, 0, reach_slabs)
            image = jnp.dot(covariance, band_dirs, precision=highest)
            image_anom = image[:, :-1]
            image_mean = image[:, -1]
            resid_anom = resid_anom - image_anom
            resid_mean = resid_mean - image_mean
            rho_next = 1.0 / (2.0 * sigma_ratio - rho_now)
            dir_anom = rho_next * rho_now * dir_anom + 2.0 * rho_next / radius * resid_anom
            dir_mean = rho_next * rho_now * dir_mean + 2.0 * rho_next / radius * resid_mean
            rho_now = rho_next
    weight = anom_weight + mean_weight[:, None]
    owned_cells = lax.all_to_all(states, "mem", split_axis=2, concat_axis=0, tiled=True)
    weight_rows = lax.all_gather(weight, "mem", axis=1, tiled=True)
    weight_context = collect_band(weight_rows, 0, reach_slabs)
    own_plane_ids = space_index * planes_dev + jnp.arange(planes_dev, dtype=jnp.int32)
    plane_taper = taper_of(own_plane_ids, context_planes, planes_all, reach_planes)

    def plane_gain(taper_row):
        return jnp.dot(context_anom * taper_row[None, :], weight_context, precision=highest)

    gain_blocks = lax.map(plane_gain, plane_taper)
    state_mean = jnp.sum(owned_cells, axis=0) / members
    state_anom = owned_cells - state_mean
    update = jnp.einsum("jxp,xjk->kxp", state_anom, gain_blocks, precision=highest) / (members - 1)
    analysis = owned_cells + update
    return lax.all_to_all(analysis, "mem", split_axis=0, concat_axis=2, tiled=True)


def halves(x):
    high = x.astype(jnp.bfloat16)
    low = (x - high.astype(jnp.float32)).astype(jnp.bfloat16)
    return high, low


def mxu(a, b):
    return jnp.dot(a, b, preferred_element_type=jnp.float32)


def round_up(value, unit):
    return -(-value // unit) * unit


def pack_kernel(ens_hbm, forcing_hbm, cell_ref, value_ref, var_ref, noise_ref, *rest, slabs):
    give_ref, keep_ref, side_ref, local_ref, ens, forcing, sems = rest
    members_dev, planes_dev, cells = ens.shape
    blocks, rows, width = give_ref.shape
    state_rows = planes_dev * members_dev
    me = lax.axis_index("space")
    smalls = pltpu.make_async_copy(forcing_hbm, forcing, sems.at[0])
    smalls.start()
    copies = []
    for _ in range(1):
        copy = pltpu.make_async_copy(ens_hbm, ens, sems.at[1])
        copy.start()
        copies.append(copy)
    local_ref[...] = cell_ref[...] - me * (planes_dev * cells)
    side_ref[:members_dev] = value_ref[...] + jnp.sqrt(var_ref[...]) * noise_ref[...]
    base = me * planes_dev
    place = jnp.zeros(cell_ref.shape, jnp.float32) + base.astype(jnp.float32)
    for plane in range(1, planes_dev):
        place = place + jnp.where(local_ref[...] >= plane * cells, 1.0, 0.0)
    fill = jnp.zeros((SUBLANES - 2, cell_ref.shape[1]), jnp.float32)
    side_ref[members_dev:] = jnp.concatenate([var_ref[...], place, fill], axis=0)
    smalls.wait()
    for copy in copies:
        copy.wait()
    tail = jnp.zeros((rows - state_rows - planes_dev, width), jnp.float32)
    for hop in range(blocks):
        for ref, flip in ((give_ref, 1), (keep_ref, 0)):
            first = jnp.bitwise_xor(me, 2 * hop + flip) * width
            span = pl.ds(pl.multiple_of(first, width), width)
            for plane in range(planes_dev):
                top = plane * members_dev
                ref[hop, top : top + members_dev, :] = ens[:, plane, span]
            ref[hop, state_rows:, :] = jnp.concatenate([forcing[:, span], tail], axis=0)


def join_kernel(keep_ref, got_ref, *outs):
    skip = keep_ref.shape[0] - len(outs)
    for hop, out in enumerate(outs):
        out[0] = keep_ref[hop + skip]
        out[1] = got_ref[hop + skip]


def forecast_kernel(*refs, planes_dev, members_dev, slabs):
    keep_ref, got_ref, others = refs[0], refs[1], refs[2 : 1 + slabs // 2]
    own_ref, cross_ref, grid_ref = refs[1 + slabs // 2 :]
    width = own_ref.shape[2]
    state_rows = planes_dev * members_dev
    count = slabs * planes_dev
    me = lax.axis_index("space")
    grid_ref[me] = keep_ref[0]
    grid_ref[jnp.bitwise_xor(me, 1)] = got_ref[0]
    for hop, other in enumerate(others):
        for flip in range(2):
            grid_ref[jnp.bitwise_xor(me, 2 * hop + 2 + flip)] = other[flip]
    for lane in range(0, width, LANES):
        lanes = slice(lane, lane + LANES)
        drive = []
        for plane in range(count):
            row = state_rows + plane % planes_dev
            drive.append(grid_ref[plane // planes_dev, row : row + 1, lanes])
        for member in range(0, members_dev, SUBLANES):
            column = []
            for plane in range(count):
                top = (plane % planes_dev) * members_dev + member
                column.append(grid_ref[plane // planes_dev, top : top + SUBLANES, lanes])
            for _ in range(FSTEPS):
                column = [
                    column[n]
                    + time_step
                    * (
                        (column[(n + 1) % count] - column[n - 2]) * column[n - 1]
                        - column[n]
                        + drive[n]
                    )
                    for n in range(count)
                ]
            for plane in range(count):
                top = (plane % planes_dev) * members_dev + member
                grid_ref[plane // planes_dev, top : top + SUBLANES, lanes] = column[plane]
    for hop in range(slabs // 2):
        own_ref[hop] = grid_ref[jnp.bitwise_xor(me, 2 * hop), :state_rows]
        cross_ref[hop] = grid_ref[jnp.bitwise_xor(me, 2 * hop + 1), :state_rows]


def observe_kernel(*refs, planes_dev, members_dev, plane_cells):
    pieces, (local_ref, out_ref, rest_ref, whole_ref) = refs[:-4], refs[-4:]
    width = rest_ref.shape[2]
    obs_dev = local_ref.shape[1]
    me = lax.axis_index("space")
    local = local_ref[...]
    total = jnp.zeros((3 * members_dev, obs_dev), jnp.float32)
    for hop, piece in enumerate(pieces):
        for flip in range(2):
            block = jnp.bitwise_xor(me, 2 * hop + flip)
            if hop:
                rest_ref[2 * hop - 2 + flip] = piece[flip]
            whole_ref[2 * hop + flip] = piece[flip]
            for plane in range(planes_dev):
                base = plane * plane_cells + block * width
                index = lax.broadcasted_iota(jnp.int32, (width, obs_dev), 0)
                pick = (index == local - base).astype(jnp.float32).astype(jnp.bfloat16)
                top = plane * members_dev
                values = piece[flip, top : top + members_dev, :]
                high = values.astype(jnp.bfloat16)
                middle, low = halves(values - high.astype(jnp.float32))
                total += mxu(jnp.concatenate([high, middle, low], axis=0), pick)
    out_ref[...] = (
        total[:members_dev]
        + total[members_dev : 2 * members_dev]
        + total[2 * members_dev :]
    )


def stack_kernel(*refs):
    out_ref = refs[-1]
    row = 0
    for ref in refs[:-1]:
        out_ref[row : row + ref.shape[0], :] = ref[...]
        row += ref.shape[0]


def solve_kernel(*refs, members, members_dev, planes_dev, pair, reach_slabs):
    slabs = len(refs) - 10
    ins, gain_ref = refs[:slabs], refs[slabs]
    anom_ref, flip_ref, side_ref, cov_hi, cov_lo, dir_ref, res_ref, sol_ref, split_ref = refs[
        slabs + 1 :
    ]
    obs_dev = ins[0].shape[1]
    planes_all = planes_dev * slabs
    reach_planes = planes_dev * reach_slabs
    me = lax.axis_index("space")
    member_count = jnp.float32(members)

    for offset in range(slabs):
        slab = jnp.bitwise_xor(me, offset)
        block = ins[offset][...]
        observed = block[:members]
        mean = jnp.sum(observed, axis=0, keepdims=True) / member_count
        anom = observed - mean
        high, low = halves(anom)
        anom_ref[slab, :members] = high
        anom_ref[slab, members : 2 * members] = high
        anom_ref[slab, 2 * members :] = low
        turned = anom.T
        turned_hi, turned_lo = halves(turned)
        flip_ref[slab, :, :members] = turned_hi
        flip_ref[slab, :, members:] = turned_lo
        res_ref[slab] = block[members : members + members_dev] - observed[:members_dev]
        side_ref[slab] = block[members + members_dev : members + members_dev + SUBLANES]

    lower = None
    variances, places, columns = [], [], []
    for slab in range(slabs):
        side = side_ref[slab]
        variances.append(side[0:1])
        places.append(side[1:2])
        columns.append(side.T[:, 1:2])
    var_row = jnp.concatenate(variances, axis=1)
    place_row = jnp.concatenate(places, axis=1)
    lower = jnp.min(var_row, axis=1, keepdims=True)

    tile = pair * obs_dev
    tiles = slabs // pair
    reach_tiles = -(-reach_slabs // pair)
    near = {}
    for right in range(tiles):
        near[right] = sorted({(right + step) % tiles for step in range(-reach_tiles, reach_tiles + 1)})
    scale = jnp.float32(1.0 / (members - 1))
    upper = None
    for right in range(tiles):
        span = slice(right * tile, (right + 1) * tile)
        tops = jnp.concatenate(
            [anom_ref[right * pair + n, : 2 * members] for n in range(pair)], axis=1
        )
        lows = jnp.concatenate(
            [anom_ref[right * pair + n, 2 * members :] for n in range(pair)], axis=1
        )
        along = place_row[:, span]
        sums = None
        for order, left in enumerate(near[right]):
            for part in range(pair):
                slab = left * pair + part
                rows = flip_ref[slab]
                gram = mxu(rows, tops) + mxu(rows[:, :members], lows)
                spread = jnp.abs(columns[slab] - along)
                spread = jnp.minimum(spread, planes_all - spread)
                taper = jnp.maximum(0.0, 1.0 - spread / reach_planes)
                cov = taper * (gram * scale)
                if left == right:
                    below = lax.broadcasted_iota(jnp.int32, (obs_dev, tile), 0) + part * obs_dev
                    across = lax.broadcasted_iota(jnp.int32, (obs_dev, tile), 1)
                    cov = cov + jnp.where(below == across, var_row[:, span], 0.0)
                size = jnp.sum(jnp.abs(cov), axis=0, keepdims=True)
                sums = size if sums is None else sums + size
                high, low = halves(cov)
                top = (order * pair + part) * obs_dev
                cov_hi[right, top : top + obs_dev, :] = high
                cov_lo[right, top : top + obs_dev, :] = low
        biggest = jnp.max(sums, axis=1, keepdims=True)
        upper = biggest if upper is None else jnp.maximum(upper, biggest)

    center = (upper + lower) / 2.0
    radius = (upper - lower) / 2.0
    sigma_ratio = center / radius
    rho_now = 1.0 / sigma_ratio
    for slab in range(slabs):
        span = slice(slab * obs_dev, (slab + 1) * obs_dev)
        start = res_ref[slab] / center
        dir_ref[slab] = start
        sol_ref[slab] = start
        high, low = halves(start)
        split_ref[:members_dev, span] = high
        split_ref[members_dev:, span] = low
    for iteration in range(ITERS - 1):
        rho_next = 1.0 / (2.0 * sigma_ratio - rho_now)
        keep = rho_next * rho_now
        take = 2.0 * rho_next / radius
        images = []
        for right in range(tiles):
            lefts = jnp.concatenate(
                [split_ref[:, left * tile : (left + 1) * tile] for left in near[right]], axis=1
            )
            both = mxu(lefts, cov_hi[right])
            images.append(
                both[:members_dev]
                + both[members_dev:]
                + mxu(lefts[:members_dev], cov_lo[right])
            )
        for slab in range(slabs):
            span = slice(slab * obs_dev, (slab + 1) * obs_dev)
            part = slab % pair
            image = images[slab // pair][:, part * obs_dev : (part + 1) * obs_dev]
            residual = res_ref[slab] - image
            res_ref[slab] = residual
            ahead = keep * dir_ref[slab] + take * residual
            dir_ref[slab] = ahead
            sol_ref[slab] += ahead
            if iteration < ITERS - 2:
                high, low = halves(ahead)
                split_ref[:members_dev, span] = high
                split_ref[members_dev:, span] = low
        rho_now = rho_next

    total = jnp.zeros((2 * planes_dev * members_dev, members), jnp.float32)
    extra = jnp.zeros((planes_dev * members_dev, members), jnp.float32)
    for slab in range(slabs):
        weight = sol_ref[slab]
        tapered = []
        for plane in range(planes_dev):
            own = (me * planes_dev + plane).astype(jnp.float32)
            spread = jnp.abs(own - place_row[:, slab * obs_dev : (slab + 1) * obs_dev])
            spread = jnp.minimum(spread, planes_all - spread)
            tapered.append(weight * jnp.maximum(0.0, 1.0 - spread / reach_planes))
        high, low = halves(jnp.concatenate(tapered, axis=0))
        rows = flip_ref[slab]
        total += mxu(jnp.concatenate([high, low], axis=0), rows[:, :members])
        extra += mxu(high, rows[:, members:])
    half = planes_dev * members_dev
    gain = (total[:half] + total[half:] + extra) * scale
    for plane in range(planes_dev):
        gain_ref[plane] = gain[plane * members_dev : (plane + 1) * members_dev]


def update_kernel(
    whole_ref, home_ref, rest_ref, far_ref, inner_ref, outer_ref, gain_ref, out_ref, *, members, planes_dev
):
    blocks, rows, width = whole_ref.shape
    members_dev = rows // planes_dev
    split = home_ref.shape[0]
    member_count = jnp.float32(members)
    me = lax.axis_index("space")
    for plane in range(planes_dev):
        high, low = halves(gain_ref[plane])
        both = jnp.concatenate([high, low], axis=0)
        span = slice(plane * members_dev, (plane + 1) * members_dev)
        for block in range(blocks):
            own = whole_ref[block, span, :]
            one = home_ref[block, span, :] if block < split else rest_ref[block - split, span, :]
            last = inner_ref[block, span, :] + outer_ref[block, span, :]
            values = jnp.concatenate([own, one, far_ref[block, span, :], last], axis=0)
            anom = values - jnp.sum(values, axis=0, keepdims=True) / member_count
            anom_hi, anom_lo = halves(anom)
            change = mxu(both, anom_hi)
            change = change[:members_dev] + change[members_dev:] + mxu(high, anom_lo)
            start = jnp.bitwise_xor(me, block) * width
            out_ref[:, plane, pl.ds(pl.multiple_of(start, width), width)] = own + change


def on_core(kernel, shapes, flops, moved, scratch=(), room=8, in_specs=None):
    single = not isinstance(shapes, list)
    many = [shapes] if single else shapes
    out = [x if hasattr(x, "dtype") else jax.ShapeDtypeStruct(x, jnp.float32) for x in many]
    extra = {} if in_specs is None else {"in_specs": in_specs}
    return pl.pallas_call(
        kernel,
        compiler_params=pltpu.CompilerParams(vmem_limit_bytes=room * 2**20),
        out_shape=out[0] if single else out,
        scratch_shapes=list(scratch),
        cost_estimate=pl.CostEstimate(flops=flops, bytes_accessed=moved, transcendentals=0),
        **extra,
    )


def replicated(ensemble, forcing, obs_cell, obs_value, obs_var, obs_noise):
    members_dev, planes_dev, plane_cells = ensemble.shape
    obs_dev = obs_cell.shape[0]
    slabs = lax.axis_size("space")
    mem_count = lax.axis_size("mem")
    members = members_dev * mem_count
    reach_slabs = min(8, slabs // 4)
    width = plane_cells // slabs
    state_rows = planes_dev * members_dev
    sent_rows = round_up(state_rows + planes_dev, SUBLANES)
    state_bytes = 4 * ensemble.size
    hops = slabs // 2
    sizes = dict(planes_dev=planes_dev, members_dev=members_dev)
    in_hbm = pl.BlockSpec(memory_space=pltpu.HBM)
    in_vmem = pl.BlockSpec(memory_space=pltpu.VMEM)

    give, keep, side, local = on_core(
        functools.partial(pack_kernel, slabs=slabs),
        [
            (hops, sent_rows, width),
            (hops, sent_rows, width),
            (members_dev + SUBLANES, obs_dev),
            jax.ShapeDtypeStruct((1, obs_dev), jnp.int32),
        ],
        ensemble.size,
        2 * state_bytes,
        scratch=[
            pltpu.VMEM(ensemble.shape, jnp.float32),
            pltpu.VMEM(forcing.shape, jnp.float32),
            pltpu.SemaphoreType.DMA((2,)),
        ],
        in_specs=[in_hbm, in_hbm] + [in_vmem] * 4,
    )(ensemble, forcing, obs_cell[None], obs_value[None], obs_var[None], obs_noise)
    got = flipped(give, "space", 1)
    sent = on_core(join_kernel, [(2, sent_rows, width)] * (hops - 1), 1, 2 * state_bytes)(keep, got)
    come = [flipped(sent[n - 1], "space", 2 * n) for n in range(1, hops)]
    own, cross = on_core(
        functools.partial(forecast_kernel, slabs=slabs, **sizes),
        [(hops, state_rows, width)] * 2,
        24 * ensemble.size,
        2 * state_bytes,
        scratch=[pltpu.VMEM((slabs, sent_rows, width), jnp.float32)],
    )(keep, got, *come)

    crossed = flipped(cross, "space", 1)
    back = on_core(join_kernel, [(2, state_rows, width)] * hops, 1, 2 * state_bytes)(own, crossed)
    home = back[0]
    pieces = [home] + [flipped(back[n], "space", 2 * n) for n in range(1, hops)]
    home_two = flipped(home, "mem", 2)
    home_one = flipped(home, "mem", 1)
    observed, rest, whole = on_core(
        functools.partial(observe_kernel, plane_cells=plane_cells, **sizes),
        [
            (members_dev, obs_dev),
            (slabs - 2, state_rows, width),
            (slabs, state_rows, width),
        ],
        6 * ensemble.size * obs_dev,
        state_bytes,
    )(*pieces, local)

    seen = [observed] + [flipped(observed, "mem", n) for n in range(1, mem_count)]
    rest_two = flipped(rest, "mem", 2)
    rest_one = flipped(rest, "mem", 1)
    block = on_core(
        stack_kernel, (members + members_dev + SUBLANES, obs_dev), 1, 8 * members * obs_dev
    )(*seen, side)
    near = [flipped(block, "space", n) if n else block for n in range(0, slabs, 2)]
    gathered = []
    for n in range(slabs // 2):
        gathered += [near[n], flipped(near[n], "space", 1)]

    whole, gathered = lax.optimization_barrier((whole, gathered))
    inner = lax.ppermute(whole, "mem", [(1, 2), (2, 1)])

    pair = 2
    tiles = slabs // pair
    near_tiles = min(tiles, 1 + 2 * (-(-reach_slabs // pair)))
    tile = pair * obs_dev
    count = slabs * obs_dev
    low_type = jnp.bfloat16
    gain = on_core(
        functools.partial(
            solve_kernel, members=members, pair=pair, reach_slabs=reach_slabs, **sizes
        ),
        (planes_dev, members_dev, members),
        6 * count * count * (members + 2 * ITERS * members_dev),
        4 * count * (members + members_dev),
        [
            pltpu.VMEM((slabs, 3 * members, obs_dev), low_type),
            pltpu.VMEM((slabs, obs_dev, 2 * members), low_type),
            pltpu.VMEM((slabs, SUBLANES, obs_dev), jnp.float32),
            pltpu.VMEM((tiles, near_tiles * tile, tile), low_type),
            pltpu.VMEM((tiles, near_tiles * tile, tile), low_type),
            pltpu.VMEM((slabs, members_dev, obs_dev), jnp.float32),
            pltpu.VMEM((slabs, members_dev, obs_dev), jnp.float32),
            pltpu.VMEM((slabs, members_dev, obs_dev), jnp.float32),
            pltpu.VMEM((2 * members_dev, count), low_type),
        ],
        room=20,
    )(*gathered)

    home_two, rest_two, gain = lax.optimization_barrier((home_two, rest_two, gain))
    far = on_core(stack_kernel, (slabs, state_rows, width), 1, 2 * state_bytes)(home_two, rest_two)
    outer = lax.ppermute(far, "mem", [(2, 3), (1, 0)])
    return on_core(
        functools.partial(
            update_kernel,
            members=members,
            planes_dev=planes_dev,
        ),
        ensemble.shape,
        6 * ensemble.size * members,
        6 * state_bytes,
        room=12,
    )(whole, home_one, rest_one, far, inner, outer, gain)


def shards(ensemble, forcing, obs_cell, obs_value, obs_var, obs_noise):
    args = (ensemble, forcing, obs_cell, obs_value, obs_var, obs_noise)
    members_dev, _, plane_cells = ensemble.shape
    slabs, groups, obs_dev = (lax.axis_size("space"), lax.axis_size("mem"), obs_cell.shape[0])
    aligned = (
        obs_dev % LANES == 0
        and plane_cells % (slabs * LANES) == 0
        and members_dev % SUBLANES == 0
        and (members_dev * groups) % LANES == 0
    )
    small = 4 * (slabs * obs_dev) ** 2 <= 2**24
    paired = slabs & (slabs - 1) == 0 and slabs >= 4
    if aligned and small and paired and groups == 4:
        return replicated(*args)
    return banded(*args)


def solution(mesh):
    placed = (
        P("mem", "space", None),
        P("space", None),
        P("space"),
        P("space"),
        P("space"),
        P("mem", "space"),
    )
    return jax.shard_map(
        shards, mesh=mesh, in_specs=placed, out_specs=P("mem", "space", None), check_vma=False
    )
```

profile of v0, /device:TPU:0, one launch (start us, length us, event | category | flops | bytes accessed | tf_op | source)
XLA Modules:
  0.0 91.6 jit_solution(12269505890699276622)
XLA Ops:
  0.0 0.6 copy-done.3
  0.7 0.0 copy-done.4
  0.7 0.0 copy-done.5
  0.7 1.0 %copy-done = f32[32,2,2048]{2,1,0:T(2,128)S(1)} copy-done((f32[32,2,2048]{2,1,0:T(2,128)S(1)}, f32[32,2,2048]{2,1,0:T(2,128)}, u32[]{:S(2)}) %copy-start) | copy-done | bytes 524312
  1.7 0.7 copy-done.1
  2.5 0.7 copy-done.2
  3.2 0.3 shard_map.64
  3.4 0.6 collective-permute-start
  4.0 1.2 %collective-permute-done.got_ref.refs_1_ = f32[4,72,256]{2,1,0:T(8,128)S(1)} collective-permute-done((f32[4,72,256]{2,1,0:T(8,128)S(1)}, f32[4,72,256]{2,1,0:T(8,128)S(1)}, u32[]{:S(2)}, u32[]{:S(2)}) %collective-permute-start) | collective-permute-done | bytes 294944 | tf_op jit(solution)/shard_map/ppermute | solution.py:28
  5.2 2.9 %collective-permute-start.1 = (f32[2,72,256]{2,1,0:T(8,128)S(1)}, f32[2,72,256]{2,1,0:T(8,128)S(1)}, u32[]{:S(2)}, u32[]{:S(2)}) collective-permute-start(f32[2,72,256]{2,1,0:T(8,128)S(1)} %get-tuple-element.35), channel_id=1, source_target_pairs={{0,2},{1,3},{2,0},{3,1},{4,6},{5,7},{6,4},{7,5},{8,10},{9,11},{10,... | collective-permute-start | bytes 442376 | tf_op jit(solution)/shard_map/ppermute | solution.py:28
  8.1 1.5 %collective-permute-start.2 = (f32[2,72,256]{2,1,0:T(8,128)S(1)}, f32[2,72,256]{2,1,0:T(8,128)S(1)}, u32[]{:S(2)}, u32[]{:S(2)}) collective-permute-start(f32[2,72,256]{2,1,0:T(8,128)S(1)} %get-tuple-element.36), channel_id=1, source_target_pairs={{0,4},{1,5},{2,6},{3,7},{4,0},{5,1},{6,2},{7,3},{8,12},{9,13},{10,... | collective-permute-start | bytes 442376 | tf_op jit(solution)/shard_map/ppermute | solution.py:28
  9.7 0.0 collective-permute-start.3
  9.7 3.1 %collective-permute-done.1.refs_2_ = f32[2,72,256]{2,1,0:T(8,128)S(1)} collective-permute-done((f32[2,72,256]{2,1,0:T(8,128)S(1)}, f32[2,72,256]{2,1,0:T(8,128)S(1)}, u32[]{:S(2)}, u32[]{:S(2)}) %collective-permute-start.1) | collective-permute-done | bytes 147488 | tf_op jit(solution)/shard_map/ppermute | solution.py:28
  12.8 4.1 %collective-permute-done.2.refs_3_ = f32[2,72,256]{2,1,0:T(8,128)S(1)} collective-permute-done((f32[2,72,256]{2,1,0:T(8,128)S(1)}, f32[2,72,256]{2,1,0:T(8,128)S(1)}, u32[]{:S(2)}, u32[]{:S(2)}) %collective-permute-start.2) | collective-permute-done | bytes 147488 | tf_op jit(solution)/shard_map/ppermute | solution.py:28
  16.9 0.5 shard_map.66
  17.4 0.1 collective-permute-start.4
  17.5 1.5 %collective-permute-done.4.got_ref = f32[4,64,256]{2,1,0:T(8,128)S(1)} collective-permute-done((f32[4,64,256]{2,1,0:T(8,128)S(1)}, f32[4,64,256]{2,1,0:T(8,128)S(1)}, u32[]{:S(2)}, u32[]{:S(2)}) %collective-permute-start.4) | collective-permute-done | bytes 262176 | tf_op jit(solution)/shard_map/ppermute | solution.py:28
  19.1 1.3 %collective-permute-start.5 = (f32[2,64,256]{2,1,0:T(8,128)S(1)}, f32[2,64,256]{2,1,0:T(8,128)S(1)}, u32[]{:S(2)}, u32[]{:S(2)}) collective-permute-start(f32[2,64,256]{2,1,0:T(8,128)S(1)} %get-tuple-element.41), channel_id=1, source_target_pairs={{0,2},{1,3},{2,0},{3,1},{4,6},{5,7},{6,4},{7,5},{8,10},{9,11},{10,... | collective-permute-start | bytes 393224 | tf_op jit(solution)/shard_map/ppermute | solution.py:28
  20.4 0.8 collective-permute-start.6
  21.2 1.4 %collective-permute-start.7 = (f32[2,64,256]{2,1,0:T(8,128)S(1)}, f32[2,64,256]{2,1,0:T(8,128)S(1)}, u32[]{:S(2)}, u32[]{:S(2)}) collective-permute-start(f32[2,64,256]{2,1,0:T(8,128)S(1)} %get-tuple-element.43), channel_id=1, source_target_pairs={{0,6},{1,7},{2,4},{3,5},{4,2},{5,3},{6,0},{7,1},{8,14},{9,15},{10,... | collective-permute-start | bytes 393224 | tf_op jit(solution)/shard_map/ppermute | solution.py:28
  22.6 2.7 %collective-permute-done.5.refs_1_ = f32[2,64,256]{2,1,0:T(8,128)S(1)} collective-permute-done((f32[2,64,256]{2,1,0:T(8,128)S(1)}, f32[2,64,256]{2,1,0:T(8,128)S(1)}, u32[]{:S(2)}, u32[]{:S(2)}) %collective-permute-start.5) | collective-permute-done | bytes 131104 | tf_op jit(solution)/shard_map/ppermute | solution.py:28
  25.3 1.5 %collective-permute-done.6.refs_2_ = f32[2,64,256]{2,1,0:T(8,128)S(1)} collective-permute-done((f32[2,64,256]{2,1,0:T(8,128)S(1)}, f32[2,64,256]{2,1,0:T(8,128)S(1)}, u32[]{:S(2)}, u32[]{:S(2)}) %collective-permute-start.6) | collective-permute-done | bytes 131104 | tf_op jit(solution)/shard_map/ppermute | solution.py:28
  26.8 1.6 %collective-permute-done.7.refs_3_ = f32[2,64,256]{2,1,0:T(8,128)S(1)} collective-permute-done((f32[2,64,256]{2,1,0:T(8,128)S(1)}, f32[2,64,256]{2,1,0:T(8,128)S(1)}, u32[]{:S(2)}, u32[]{:S(2)}) %collective-permute-start.7) | collective-permute-done | bytes 131104 | tf_op jit(solution)/shard_map/ppermute | solution.py:28
  28.4 0.5 shard_map.68
  28.9 3.7 %collective-permute-start.10 = (f32[32,128]{1,0:T(8,128)S(1)}, f32[32,128]{1,0:T(8,128)S(1)}, u32[]{:S(2)}, u32[]{:S(2)}) collective-permute-start(f32[32,128]{1,0:T(8,128)S(1)} %get-tuple-element.46.refs_0_), channel_id=1, source_target_pairs={{0,24},{8,16},{16,8},{24,0},{1,25},{9,17},{17,9},{25,1},{2,26},{10... | collective-permute-start | bytes 49160 | tf_op jit(solution)/shard_map/ppermute | solution.py:28
  32.6 0.8 collective-permute-start.8
  33.4 1.2 %collective-permute-done.10.refs_3_ = f32[32,128]{1,0:T(8,128)S(1)} collective-permute-done((f32[32,128]{1,0:T(8,128)S(1)}, f32[32,128]{1,0:T(8,128)S(1)}, u32[]{:S(2)}, u32[]{:S(2)}) %collective-permute-start.10) | collective-permute-done | bytes 16416 | tf_op jit(solution)/shard_map/ppermute | solution.py:28
  34.5 2.7 %collective-permute-done.9.refs_2_ = f32[32,128]{1,0:T(8,128)S(1)} collective-permute-done((f32[32,128]{1,0:T(8,128)S(1)}, f32[32,128]{1,0:T(8,128)S(1)}, u32[]{:S(2)}, u32[]{:S(2)}) %collective-permute-start.9) | collective-permute-done | bytes 16416 | tf_op jit(solution)/shard_map/ppermute | solution.py:28
  37.2 1.8 %collective-permute-start.16 = (f32[168,128]{1,0:T(8,128)S(1)}, f32[168,128]{1,0:T(8,128)S(1)}, u32[]{:S(2)}, u32[]{:S(2)}) collective-permute-start(f32[168,128]{1,0:T(8,128)S(1)} %shard_map.69.refs_0_), channel_id=1, source_target_pairs={{0,6},{1,7},{2,4},{3,5},{4,2},{5,3},{6,0},{7,1},{8,14},{9,15},{10,... | collective-permute-start | bytes 258056 | tf_op jit(solution)/shard_map/ppermute | solution.py:28
  39.1 0.5 collective-permute-start.14
  39.6 1.2 %collective-permute-start.12 = (f32[168,128]{1,0:T(8,128)S(1)}, f32[168,128]{1,0:T(8,128)S(1)}, u32[]{:S(2)}, u32[]{:S(2)}) collective-permute-start(f32[168,128]{1,0:T(8,128)S(1)} %shard_map.69.refs_0_), channel_id=1, source_target_pairs={{0,2},{1,3},{2,0},{3,1},{4,6},{5,7},{6,4},{7,5},{8,10},{9,11},{10,... | collective-permute-start | bytes 258056 | tf_op jit(solution)/shard_map/ppermute | solution.py:28
  40.8 2.0 %collective-permute-start.21 = (f32[6,64,256]{2,1,0:T(8,128)S(1)}, f32[6,64,256]{2,1,0:T(8,128)S(1)}, u32[]{:S(2)}, u32[]{:S(2)}) collective-permute-start(f32[6,64,256]{2,1,0:T(8,128)S(1)} %get-tuple-element.49), channel_id=1, source_target_pairs={{0,16},{8,24},{16,0},{24,8},{1,17},{9,25},{17,1},{25,9},{2,18},{10... | collective-permute-start | bytes 1179656 | tf_op jit(solution)/shard_map/ppermute | solution.py:28
  42.8 0.0 collective-permute-start.11
  42.8 0.0 collective-permute-done.16.refs_6_
  42.8 0.5 collective-permute-start.17
  43.3 0.3 collective-permute-done.14.refs_4_
  43.6 0.4 collective-permute-done.12.refs_2_
  44.1 0.1 collective-permute-start.13
  44.1 2.0 %collective-permute-start.20 = (f32[2,64,256]{2,1,0:T(8,128)S(1)}, f32[2,64,256]{2,1,0:T(8,128)S(1)}, u32[]{:S(2)}, u32[]{:S(2)}) collective-permute-start(f32[2,64,256]{2,1,0:T(8,128)S(1)} %get-tuple-element.40.refs_0_), channel_id=1, source_target_pairs={{0,16},{8,24},{16,0},{24,8},{1,17},{9,25},{17,1},{25,9},{2,18},{10... | collective-permute-start | bytes 393224 | tf_op jit(solution)/shard_map/ppermute | solution.py:28
  46.2 0.0 collective-permute-done.17.refs_7_
  46.2 0.7 collective-permute-start.22
  46.9 5.3 %shard_map.70.gain_ref = f32[2,32,128]{2,1,0:T(8,128)S(1)} custom-call(f32[168,128]{1,0:T(8,128)S(1)} %shard_map.69.refs_0_, f32[168,128]{1,0:T(8,128)S(1)} %collective-permute-done.11.refs_1_, f32[168,128]{1,0:T(8,128)S(1)} %collective-permute-done.12.refs_2_, f32[168,128]{1,0:T(8,128)S(1)} %collective-permute-done.13.refs_3_, ...), custom_call_target="tpu_custom_call" | custom-call | flops 3221225472 | bytes 655360 | tf_op jit(solution)/shard_map/pallas_call | solution.py:542
  52.2 10.8 %collective-permute-done.20.refs_0_ = f32[2,64,256]{2,1,0:T(8,128)S(1)} collective-permute-done((f32[2,64,256]{2,1,0:T(8,128)S(1)}, f32[2,64,256]{2,1,0:T(8,128)S(1)}, u32[]{:S(2)}, u32[]{:S(2)}) %collective-permute-start.20) | collective-permute-done | bytes 131104 | tf_op jit(solution)/shard_map/ppermute | solution.py:28
  63.1 1.3 %collective-permute-start.23 = (f32[8,64,256]{2,1,0:T(8,128)S(1)}, f32[8,64,256]{2,1,0:T(8,128)S(1)}, u32[]{:S(2)}, u32[]{:S(2)}) collective-permute-start(f32[8,64,256]{2,1,0:T(8,128)S(1)} %shard_map.71.far_ref), channel_id=1, source_target_pairs={{16,24},{8,0},{17,25},{9,1},{18,26},{10,2},{19,27},{11,3},{20,28},... | collective-permute-start | bytes 1572872 | tf_op jit(solution)/shard_map/ppermute | solution.py:565
  64.4 2.7 %collective-permute-start.19 = (f32[6,64,256]{2,1,0:T(8,128)S(1)}, f32[6,64,256]{2,1,0:T(8,128)S(1)}, u32[]{:S(2)}, u32[]{:S(2)}) collective-permute-start(f32[6,64,256]{2,1,0:T(8,128)S(1)} %get-tuple-element.49), channel_id=1, source_target_pairs={{0,8},{8,0},{16,24},{24,16},{1,9},{9,1},{17,25},{25,17},{2,10},{10... | collective-permute-start | bytes 1179656 | tf_op jit(solution)/shard_map/ppermute | solution.py:28
  67.1 0.1 collective-permute-start.18
  67.2 22.8 %collective-permute-done.18.home_ref = f32[2,64,256]{2,1,0:T(8,128)S(1)} collective-permute-done((f32[2,64,256]{2,1,0:T(8,128)S(1)}, f32[2,64,256]{2,1,0:T(8,128)S(1)}, u32[]{:S(2)}, u32[]{:S(2)}) %collective-permute-start.18) | collective-permute-done | bytes 131104 | tf_op jit(solution)/shard_map/ppermute | solution.py:28
  90.0 1.7 %shard_map.72 = f32[32,2,2048]{2,1,0:T(2,128)} custom-call(f32[8,64,256]{2,1,0:T(8,128)S(1)} %get-tuple-element.48.whole_ref, f32[2,64,256]{2,1,0:T(8,128)S(1)} %collective-permute-done.18.home_ref, f32[6,64,256]{2,1,0:T(8,128)S(1)} %collective-permute-done.19.rest_ref, f32[8,64,256]{2,1,0:T(8,128)S(1)} %shard_map.71.far_ref, ...), custom_call_target="tpu_custom_call" | custom-call | flops 100663296 | bytes 3145728 | tf_op jit(solution)/shard_map/pallas_call | solution.py:566
  (21 shorter events, 0.1 us)
Async XLA Ops:
  0.0 0.7 copy-start.3
  0.0 0.7 copy-start.4
  0.0 0.7 copy-start.5
  0.7 1.0 %copy-start = (f32[32,2,2048]{2,1,0:T(2,128)S(1)}, f32[32,2,2048]{2,1,0:T(2,128)}, u32[]{:S(2)}) copy-start(f32[32,2,2048]{2,1,0:T(2,128)} %ens_hbm.1) | copy-start | bytes 1572868
  1.7 0.7 copy-start.1
  2.4 0.7 copy-start.2
  3.4 1.8 %collective-permute-start = (f32[4,72,256]{2,1,0:T(8,128)S(1)}, f32[4,72,256]{2,1,0:T(8,128)S(1)}, u32[]{:S(2)}, u32[]{:S(2)}) collective-permute-start(f32[4,72,256]{2,1,0:T(8,128)S(1)} %get-tuple-element.34), channel_id=1, source_target_pairs={{0,1},{1,0},{2,3},{3,2},{4,5},{5,4},{6,7},{7,6},{8,9},{9,8},{10,11... | collective-permute-start | bytes 884744 | tf_op jit(solution)/shard_map/ppermute | solution.py:28
  5.2 7.6 %collective-permute-start.1 = (f32[2,72,256]{2,1,0:T(8,128)S(1)}, f32[2,72,256]{2,1,0:T(8,128)S(1)}, u32[]{:S(2)}, u32[]{:S(2)}) collective-permute-start(f32[2,72,256]{2,1,0:T(8,128)S(1)} %get-tuple-element.35), channel_id=1, source_target_pairs={{0,2},{1,3},{2,0},{3,1},{4,6},{5,7},{6,4},{7,5},{8,10},{9,11},{10,... | collective-permute-start | bytes 442376 | tf_op jit(solution)/shard_map/ppermute | solution.py:28
  8.1 8.8 %collective-permute-start.2 = (f32[2,72,256]{2,1,0:T(8,128)S(1)}, f32[2,72,256]{2,1,0:T(8,128)S(1)}, u32[]{:S(2)}, u32[]{:S(2)}) collective-permute-start(f32[2,72,256]{2,1,0:T(8,128)S(1)} %get-tuple-element.36), channel_id=1, source_target_pairs={{0,4},{1,5},{2,6},{3,7},{4,0},{5,1},{6,2},{7,3},{8,12},{9,13},{10,... | collective-permute-start | bytes 442376 | tf_op jit(solution)/shard_map/ppermute | solution.py:28
  9.7 7.3 %collective-permute-start.3 = (f32[2,72,256]{2,1,0:T(8,128)S(1)}, f32[2,72,256]{2,1,0:T(8,128)S(1)}, u32[]{:S(2)}, u32[]{:S(2)}) collective-permute-start(f32[2,72,256]{2,1,0:T(8,128)S(1)} %get-tuple-element.37), channel_id=1, source_target_pairs={{0,6},{1,7},{2,4},{3,5},{4,2},{5,3},{6,0},{7,1},{8,14},{9,15},{10,... | collective-permute-start | bytes 442376 | tf_op jit(solution)/shard_map/ppermute | solution.py:28
  17.4 1.6 %collective-permute-start.4 = (f32[4,64,256]{2,1,0:T(8,128)S(1)}, f32[4,64,256]{2,1,0:T(8,128)S(1)}, u32[]{:S(2)}, u32[]{:S(2)}) collective-permute-start(f32[4,64,256]{2,1,0:T(8,128)S(1)} %get-tuple-element.39), channel_id=1, source_target_pairs={{0,1},{1,0},{2,3},{3,2},{4,5},{5,4},{6,7},{7,6},{8,9},{9,8},{10,11... | collective-permute-start | bytes 786440 | tf_op jit(solution)/shard_map/ppermute | solution.py:28
  19.1 6.3 %collective-permute-start.5 = (f32[2,64,256]{2,1,0:T(8,128)S(1)}, f32[2,64,256]{2,1,0:T(8,128)S(1)}, u32[]{:S(2)}, u32[]{:S(2)}) collective-permute-start(f32[2,64,256]{2,1,0:T(8,128)S(1)} %get-tuple-element.41), channel_id=1, source_target_pairs={{0,2},{1,3},{2,0},{3,1},{4,6},{5,7},{6,4},{7,5},{8,10},{9,11},{10,... | collective-permute-start | bytes 393224 | tf_op jit(solution)/shard_map/ppermute | solution.py:28
  20.4 6.4 %collective-permute-start.6 = (f32[2,64,256]{2,1,0:T(8,128)S(1)}, f32[2,64,256]{2,1,0:T(8,128)S(1)}, u32[]{:S(2)}, u32[]{:S(2)}) collective-permute-start(f32[2,64,256]{2,1,0:T(8,128)S(1)} %get-tuple-element.42), channel_id=1, source_target_pairs={{0,4},{1,5},{2,6},{3,7},{4,0},{5,1},{6,2},{7,3},{8,12},{9,13},{10,... | collective-permute-start | bytes 393224 | tf_op jit(solution)/shard_map/ppermute | solution.py:28
  21.2 7.2 %collective-permute-start.7 = (f32[2,64,256]{2,1,0:T(8,128)S(1)}, f32[2,64,256]{2,1,0:T(8,128)S(1)}, u32[]{:S(2)}, u32[]{:S(2)}) collective-permute-start(f32[2,64,256]{2,1,0:T(8,128)S(1)} %get-tuple-element.43), channel_id=1, source_target_pairs={{0,6},{1,7},{2,4},{3,5},{4,2},{5,3},{6,0},{7,1},{8,14},{9,15},{10,... | collective-permute-start | bytes 393224 | tf_op jit(solution)/shard_map/ppermute | solution.py:28
  28.9 5.6 %collective-permute-start.10 = (f32[32,128]{1,0:T(8,128)S(1)}, f32[32,128]{1,0:T(8,128)S(1)}, u32[]{:S(2)}, u32[]{:S(2)}) collective-permute-start(f32[32,128]{1,0:T(8,128)S(1)} %get-tuple-element.46.refs_0_), channel_id=1, source_target_pairs={{0,24},{8,16},{16,8},{24,0},{1,25},{9,17},{17,9},{25,1},{2,26},{10... | collective-permute-start | bytes 49160 | tf_op jit(solution)/shard_map/ppermute | solution.py:28
  32.6 4.6 %collective-permute-start.9 = (f32[32,128]{1,0:T(8,128)S(1)}, f32[32,128]{1,0:T(8,128)S(1)}, u32[]{:S(2)}, u32[]{:S(2)}) collective-permute-start(f32[32,128]{1,0:T(8,128)S(1)} %get-tuple-element.46.refs_0_), channel_id=1, source_target_pairs={{0,16},{8,24},{16,0},{24,8},{1,17},{9,25},{17,1},{25,9},{2,18},{10... | collective-permute-start | bytes 49160 | tf_op jit(solution)/shard_map/ppermute | solution.py:28
  32.6 4.6 %collective-permute-start.8 = (f32[32,128]{1,0:T(8,128)S(1)}, f32[32,128]{1,0:T(8,128)S(1)}, u32[]{:S(2)}, u32[]{:S(2)}) collective-permute-start(f32[32,128]{1,0:T(8,128)S(1)} %get-tuple-element.46.refs_0_), channel_id=1, source_target_pairs={{0,8},{8,0},{16,24},{24,16},{1,9},{9,1},{17,25},{25,17},{2,10},{10... | collective-permute-start | bytes 49160 | tf_op jit(solution)/shard_map/ppermute | solution.py:28
  37.2 5.6 %collective-permute-start.16 = (f32[168,128]{1,0:T(8,128)S(1)}, f32[168,128]{1,0:T(8,128)S(1)}, u32[]{:S(2)}, u32[]{:S(2)}) collective-permute-start(f32[168,128]{1,0:T(8,128)S(1)} %shard_map.69.refs_0_), channel_id=1, source_target_pairs={{0,6},{1,7},{2,4},{3,5},{4,2},{5,3},{6,0},{7,1},{8,14},{9,15},{10,... | collective-permute-start | bytes 258056 | tf_op jit(solution)/shard_map/ppermute | solution.py:28
  39.1 4.6 %collective-permute-start.14 = (f32[168,128]{1,0:T(8,128)S(1)}, f32[168,128]{1,0:T(8,128)S(1)}, u32[]{:S(2)}, u32[]{:S(2)}) collective-permute-start(f32[168,128]{1,0:T(8,128)S(1)} %shard_map.69.refs_0_), channel_id=1, source_target_pairs={{0,4},{1,5},{2,6},{3,7},{4,0},{5,1},{6,2},{7,3},{8,12},{9,13},{10,... | collective-permute-start | bytes 258056 | tf_op jit(solution)/shard_map/ppermute | solution.py:28
  39.6 4.5 %collective-permute-start.12 = (f32[168,128]{1,0:T(8,128)S(1)}, f32[168,128]{1,0:T(8,128)S(1)}, u32[]{:S(2)}, u32[]{:S(2)}) collective-permute-start(f32[168,128]{1,0:T(8,128)S(1)} %shard_map.69.refs_0_), channel_id=1, source_target_pairs={{0,2},{1,3},{2,0},{3,1},{4,6},{5,7},{6,4},{7,5},{8,10},{9,11},{10,... | collective-permute-start | bytes 258056 | tf_op jit(solution)/shard_map/ppermute | solution.py:28
  40.8 22.2 %collective-permute-start.21 = (f32[6,64,256]{2,1,0:T(8,128)S(1)}, f32[6,64,256]{2,1,0:T(8,128)S(1)}, u32[]{:S(2)}, u32[]{:S(2)}) collective-permute-start(f32[6,64,256]{2,1,0:T(8,128)S(1)} %get-tuple-element.49), channel_id=1, source_target_pairs={{0,16},{8,24},{16,0},{24,8},{1,17},{9,25},{17,1},{25,9},{2,18},{10... | collective-permute-start | bytes 1179656 | tf_op jit(solution)/shard_map/ppermute | solution.py:28
  42.8 1.3 %collective-permute-start.11 = (f32[168,128]{1,0:T(8,128)S(1)}, f32[168,128]{1,0:T(8,128)S(1)}, u32[]{:S(2)}, u32[]{:S(2)}) collective-permute-start(f32[168,128]{1,0:T(8,128)S(1)} %shard_map.69.refs_0_), channel_id=1, source_target_pairs={{0,1},{1,0},{2,3},{3,2},{4,5},{5,4},{6,7},{7,6},{8,9},{9,8},{10,11... | collective-permute-start | bytes 258056 | tf_op jit(solution)/shard_map/ppermute | solution.py:28
  42.8 3.3 %collective-permute-start.17 = (f32[168,128]{1,0:T(8,128)S(1)}, f32[168,128]{1,0:T(8,128)S(1)}, u32[]{:S(2)}, u32[]{:S(2)}) collective-permute-start(f32[168,128]{1,0:T(8,128)S(1)} %collective-permute-done.16.refs_6_), channel_id=1, source_target_pairs={{0,1},{1,0},{2,3},{3,2},{4,5},{5,4},{6,7},{7,6},{8,9},{9,8},{10,11... | collective-permute-start | bytes 258056 | tf_op jit(solution)/shard_map/ppermute | solution.py:28
  43.6 2.5 %collective-permute-start.15 = (f32[168,128]{1,0:T(8,128)S(1)}, f32[168,128]{1,0:T(8,128)S(1)}, u32[]{:S(2)}, u32[]{:S(2)}) collective-permute-start(f32[168,128]{1,0:T(8,128)S(1)} %collective-permute-done.14.refs_4_), channel_id=1, source_target_pairs={{0,1},{1,0},{2,3},{3,2},{4,5},{5,4},{6,7},{7,6},{8,9},{9,8},{10,11... | collective-permute-start | bytes 258056 | tf_op jit(solution)/shard_map/ppermute | solution.py:28
  44.1 2.1 %collective-permute-start.13 = (f32[168,128]{1,0:T(8,128)S(1)}, f32[168,128]{1,0:T(8,128)S(1)}, u32[]{:S(2)}, u32[]{:S(2)}) collective-permute-start(f32[168,128]{1,0:T(8,128)S(1)} %collective-permute-done.12.refs_2_), channel_id=1, source_target_pairs={{0,1},{1,0},{2,3},{3,2},{4,5},{5,4},{6,7},{7,6},{8,9},{9,8},{10,11... | collective-permute-start | bytes 258056 | tf_op jit(solution)/shard_map/ppermute | solution.py:28
  44.1 18.9 %collective-permute-start.20 = (f32[2,64,256]{2,1,0:T(8,128)S(1)}, f32[2,64,256]{2,1,0:T(8,128)S(1)}, u32[]{:S(2)}, u32[]{:S(2)}) collective-permute-start(f32[2,64,256]{2,1,0:T(8,128)S(1)} %get-tuple-element.40.refs_0_), channel_id=1, source_target_pairs={{0,16},{8,24},{16,0},{24,8},{1,17},{9,25},{17,1},{25,9},{2,18},{10... | collective-permute-start | bytes 393224 | tf_op jit(solution)/shard_map/ppermute | solution.py:28
  46.2 43.8 %collective-permute-start.22 = (f32[8,64,256]{2,1,0:T(8,128)S(1)}, f32[8,64,256]{2,1,0:T(8,128)S(1)}, u32[]{:S(2)}, u32[]{:S(2)}) collective-permute-start(f32[8,64,256]{2,1,0:T(8,128)S(1)} %get-tuple-element.48.whole_ref), channel_id=1, source_target_pairs={{8,16},{16,8},{9,17},{17,9},{10,18},{18,10},{11,19},{19,11},{12,20... | collective-permute-start | bytes 1572872 | tf_op jit(solution)/shard_map/ppermute | solution.py:534
  63.1 26.9 %collective-permute-start.23 = (f32[8,64,256]{2,1,0:T(8,128)S(1)}, f32[8,64,256]{2,1,0:T(8,128)S(1)}, u32[]{:S(2)}, u32[]{:S(2)}) collective-permute-start(f32[8,64,256]{2,1,0:T(8,128)S(1)} %shard_map.71.far_ref), channel_id=1, source_target_pairs={{16,24},{8,0},{17,25},{9,1},{18,26},{10,2},{19,27},{11,3},{20,28},... | collective-permute-start | bytes 1572872 | tf_op jit(solution)/shard_map/ppermute | solution.py:565
  64.4 25.6 %collective-permute-start.19 = (f32[6,64,256]{2,1,0:T(8,128)S(1)}, f32[6,64,256]{2,1,0:T(8,128)S(1)}, u32[]{:S(2)}, u32[]{:S(2)}) collective-permute-start(f32[6,64,256]{2,1,0:T(8,128)S(1)} %get-tuple-element.49), channel_id=1, source_target_pairs={{0,8},{8,0},{16,24},{24,16},{1,9},{9,1},{17,25},{25,17},{2,10},{10... | collective-permute-start | bytes 1179656 | tf_op jit(solution)/shard_map/ppermute | solution.py:28
  67.1 22.8 %collective-permute-start.18 = (f32[2,64,256]{2,1,0:T(8,128)S(1)}, f32[2,64,256]{2,1,0:T(8,128)S(1)}, u32[]{:S(2)}, u32[]{:S(2)}) collective-permute-start(f32[2,64,256]{2,1,0:T(8,128)S(1)} %get-tuple-element.40.refs_0_), channel_id=1, source_target_pairs={{0,8},{8,0},{16,24},{24,16},{1,9},{9,1},{17,25},{25,17},{2,10},{10... | collective-permute-start | bytes 393224 | tf_op jit(solution)/shard_map/ppermute | solution.py:28
where the time goes:
time: 92 us; the launch traced here: 91.6 us
  waiting for transfers between devices  54 us (59%)
  starting transfers between devices  26.1 us (28%)
  Pallas kernels  8.33 us (9%)
  local copies, waits for them, and re-layouts  3.16 us (3%)
    ppermute x22, waiting for transfers between devices, flipped(): return lax.ppermute(value, axis, [(i, i ^ mask) for i in range(count)])  54 us
    ppermute x22, starting transfers between devices, flipped(): return lax.ppermute(value, axis, [(i, i ^ mask) for i in range(count)])  24.1 us
    pallas_call x1, Pallas kernels, replicated(): on_core(functools.partial(solve_kernel, members=members, pair=pair, reach...  5.33 us
    unnamed x12, local copies, waits for them, and re-layouts  3.16 us
  transfers between devices with their start and end apart: 24, of which 13 were waited for; matrix products, arithmetic and copies ran while one was open for 0% of the time, Pallas kernels for 6%

commit v1 on v0

--- a/solution.py
+++ b/solution.py
@@ -155,30 +155,11 @@
     return -(-value // unit) * unit
 
 
-def pack_kernel(ens_hbm, forcing_hbm, cell_ref, value_ref, var_ref, noise_ref, *rest, slabs):
-    give_ref, keep_ref, side_ref, local_ref, ens, forcing, sems = rest
-    members_dev, planes_dev, cells = ens.shape
+def pack_kernel(ens_ref, forcing_ref, give_ref, keep_ref):
+    members_dev, planes_dev, _ = ens_ref.shape
     blocks, rows, width = give_ref.shape
     state_rows = planes_dev * members_dev
     me = lax.axis_index("space")
-    smalls = pltpu.make_async_copy(forcing_hbm, forcing, sems.at[0])
-    smalls.start()
-    copies = []
-    for _ in range(1):
-        copy = pltpu.make_async_copy(ens_hbm, ens, sems.at[1])
-        copy.start()
-        copies.append(copy)
-    local_ref[...] = cell_ref[...] - me * (planes_dev * cells)
-    side_ref[:members_dev] = value_ref[...] + jnp.sqrt(var_ref[...]) * noise_ref[...]
-    base = me * planes_dev
-    place = jnp.zeros(cell_ref.shape, jnp.float32) + base.astype(jnp.float32)
-    for plane in range(1, planes_dev):
-        place = place + jnp.where(local_ref[...] >= plane * cells, 1.0, 0.0)
-    fill = jnp.zeros((SUBLANES - 2, cell_ref.shape[1]), jnp.float32)
-    side_ref[members_dev:] = jnp.concatenate([var_ref[...], place, fill], axis=0)
-    smalls.wait()
-    for copy in copies:
-        copy.wait()
     tail = jnp.zeros((rows - state_rows - planes_dev, width), jnp.float32)
     for hop in range(blocks):
         for ref, flip in ((give_ref, 1), (keep_ref, 0)):
@@ -186,8 +167,8 @@
             span = pl.ds(pl.multiple_of(first, width), width)
             for plane in range(planes_dev):
                 top = plane * members_dev
-                ref[hop, top : top + members_dev, :] = ens[:, plane, span]
-            ref[hop, state_rows:, :] = jnp.concatenate([forcing[:, span], tail], axis=0)
+                ref[hop, top : top + members_dev, :] = ens_ref[:, plane, span]
+            ref[hop, state_rows:, :] = jnp.concatenate([forcing_ref[:, span], tail], axis=0)
 
 
 def join_kernel(keep_ref, got_ref, *outs):
@@ -244,7 +225,7 @@
     width = rest_ref.shape[2]
     obs_dev = local_ref.shape[1]
     me = lax.axis_index("space")
-    local = local_ref[...]
+    local = local_ref[...] - me * (planes_dev * plane_cells)
     total = jnp.zeros((3 * members_dev, obs_dev), jnp.float32)
     for hop, piece in enumerate(pieces):
         for flip in range(2):
@@ -268,12 +249,27 @@
     )
 
 
-def stack_kernel(*refs):
-    out_ref = refs[-1]
+def stack_kernel(*refs, planes_dev, plane_cells):
+    seen, (cell_ref, value_ref, var_ref, noise_ref, out_ref) = refs[:-5], refs[-5:]
     row = 0
-    for ref in refs[:-1]:
-        out_ref[row : row + ref.shape[0], :] = ref[...]
+    for ref in seen:
+        out_ref[row : row + ref.shape[0]] = ref[...]
         row += ref.shape[0]
+    wanted = value_ref[...] + jnp.sqrt(var_ref[...]) * noise_ref[...]
+    out_ref[row : row + wanted.shape[0]] = wanted
+    base = lax.axis_index("space") * planes_dev
+    local = cell_ref[...] - base * plane_cells
+    place = jnp.zeros(local.shape, jnp.float32) + base.astype(jnp.float32)
+    for plane in range(1, planes_dev):
+        place = place + jnp.where(local >= plane * plane_cells, 1.0, 0.0)
+    fill = jnp.zeros((SUBLANES - 2, local.shape[1]), jnp.float32)
+    out_ref[row + wanted.shape[0] :] = jnp.concatenate([var_ref[...], place, fill], axis=0)
+
+
+def merge_kernel(home_ref, rest_ref, out_ref):
+    split = home_ref.shape[0]
+    out_ref[:split] = home_ref[...]
+    out_ref[split:] = rest_ref[...]
 
 
 def solve_kernel(*refs, members, members_dev, planes_dev, pair, reach_slabs):
@@ -418,22 +414,20 @@
         gain_ref[plane] = gain[plane * members_dev : (plane + 1) * members_dev]
 
 
-def update_kernel(
-    whole_ref, home_ref, rest_ref, far_ref, inner_ref, outer_ref, gain_ref, out_ref, *, members, planes_dev
-):
-    blocks, rows, width = whole_ref.shape
-    members_dev = rows // planes_dev
+def update_kernel(own_ref, home_ref, rest_ref, far_ref, middle_ref, end_ref, gain_ref, out_ref):
+    blocks, _, width = own_ref.shape
+    members_dev, planes_dev = out_ref.shape[:2]
     split = home_ref.shape[0]
-    member_count = jnp.float32(members)
+    member_count = jnp.float32(gain_ref.shape[2])
     me = lax.axis_index("space")
     for plane in range(planes_dev):
         high, low = halves(gain_ref[plane])
         both = jnp.concatenate([high, low], axis=0)
         span = slice(plane * members_dev, (plane + 1) * members_dev)
         for block in range(blocks):
-            own = whole_ref[block, span, :]
+            own = own_ref[block, span, :]
             one = home_ref[block, span, :] if block < split else rest_ref[block - split, span, :]
-            last = inner_ref[block, span, :] + outer_ref[block, span, :]
+            last = middle_ref[block, span, :] + end_ref[block, span, :]
             values = jnp.concatenate([own, one, far_ref[block, span, :], last], axis=0)
             anom = values - jnp.sum(values, axis=0, keepdims=True) / member_count
             anom_hi, anom_lo = halves(anom)
@@ -471,26 +465,10 @@
     state_bytes = 4 * ensemble.size
     hops = slabs // 2
     sizes = dict(planes_dev=planes_dev, members_dev=members_dev)
-    in_hbm = pl.BlockSpec(memory_space=pltpu.HBM)
-    in_vmem = pl.BlockSpec(memory_space=pltpu.VMEM)
-
-    give, keep, side, local = on_core(
-        functools.partial(pack_kernel, slabs=slabs),
-        [
-            (hops, sent_rows, width),
-            (hops, sent_rows, width),
-            (members_dev + SUBLANES, obs_dev),
-            jax.ShapeDtypeStruct((1, obs_dev), jnp.int32),
-        ],
-        ensemble.size,
-        2 * state_bytes,
-        scratch=[
-            pltpu.VMEM(ensemble.shape, jnp.float32),
-            pltpu.VMEM(forcing.shape, jnp.float32),
-            pltpu.SemaphoreType.DMA((2,)),
-        ],
-        in_specs=[in_hbm, in_hbm] + [in_vmem] * 4,
-    )(ensemble, forcing, obs_cell[None], obs_value[None], obs_var[None], obs_noise)
+
+    give, keep = on_core(
+        pack_kernel, [(hops, sent_rows, width)] * 2, ensemble.size, 2 * state_bytes
+    )(ensemble, forcing)
     got = flipped(give, "space", 1)
     sent = on_core(join_kernel, [(2, sent_rows, width)] * (hops - 1), 1, 2 * state_bytes)(keep, got)
     come = [flipped(sent[n - 1], "space", 2 * n) for n in range(1, hops)]
@@ -506,8 +484,8 @@
     back = on_core(join_kernel, [(2, state_rows, width)] * hops, 1, 2 * state_bytes)(own, crossed)
     home = back[0]
     pieces = [home] + [flipped(back[n], "space", 2 * n) for n in range(1, hops)]
+    home_one = flipped(home, "mem", 1)
     home_two = flipped(home, "mem", 2)
-    home_one = flipped(home, "mem", 1)
     observed, rest, whole = on_core(
         functools.partial(observe_kernel, plane_cells=plane_cells, **sizes),
         [
@@ -517,21 +495,25 @@
         ],
         6 * ensemble.size * obs_dev,
         state_bytes,
-    )(*pieces, local)
+    )(*pieces, obs_cell[None])
 
     seen = [observed] + [flipped(observed, "mem", n) for n in range(1, mem_count)]
+    rest_one = flipped(rest, "mem", 1)
     rest_two = flipped(rest, "mem", 2)
-    rest_one = flipped(rest, "mem", 1)
     block = on_core(
-        stack_kernel, (members + members_dev + SUBLANES, obs_dev), 1, 8 * members * obs_dev
-    )(*seen, side)
-    near = [flipped(block, "space", n) if n else block for n in range(0, slabs, 2)]
+        functools.partial(stack_kernel, planes_dev=planes_dev, plane_cells=plane_cells),
+        (members + members_dev + SUBLANES, obs_dev),
+        1,
+        8 * members * obs_dev,
+    )(*seen, obs_cell[None], obs_value[None], obs_var[None], obs_noise)
+    near = [block] + [flipped(block, "space", 2 * n) for n in range(1, hops)]
     gathered = []
-    for n in range(slabs // 2):
+    for n in range(hops):
         gathered += [near[n], flipped(near[n], "space", 1)]
 
-    whole, gathered = lax.optimization_barrier((whole, gathered))
-    inner = lax.ppermute(whole, "mem", [(1, 2), (2, 1)])
+    all_middle = lax.ppermute(whole, "mem", [(1, 2), (2, 1)])
+    far = on_core(merge_kernel, (slabs, state_rows, width), 1, 2 * state_bytes)(home_two, rest_two)
+    all_out = lax.ppermute(far, "mem", [(2, 3), (1, 0)])
 
     pair = 2
     tiles = slabs // pair
@@ -560,20 +542,9 @@
         room=20,
     )(*gathered)
 
-    home_two, rest_two, gain = lax.optimization_barrier((home_two, rest_two, gain))
-    far = on_core(stack_kernel, (slabs, state_rows, width), 1, 2 * state_bytes)(home_two, rest_two)
-    outer = lax.ppermute(far, "mem", [(2, 3), (1, 0)])
     return on_core(
-        functools.partial(
-            update_kernel,
-            members=members,
-            planes_dev=planes_dev,
-        ),
-        ensemble.shape,
-        6 * ensemble.size * members,
-        6 * state_bytes,
-        room=12,
-    )(whole, home_one, rest_one, far, inner, outer, gain)
+        update_kernel, ensemble.shape, 6 * ensemble.size * members, 6 * state_bytes, room=12
+    )(whole, home_one, rest_one, far, all_middle, all_out, gain)
 
 
 def shards(ensemble, forcing, obs_cell, obs_value, obs_var, obs_noise):

time: 92 us -> 88 us (0.957)
  waiting for transfers between devices: 54 us -> 50 us
    ppermute x22, waiting for transfers between devices: 54 us -> 50 us  [flipped(): return lax.ppermute(value, axis, [(i, i ^ mask) for i in range(count)])]
  transfers between devices with their start and end apart: 24 -> 24, of which waited for: 13 -> 14; matrix products, arithmetic and copies ran while one was open for 0% -> 0% of each run, Pallas kernels for 6% -> 6%
where the time goes in v1:
time: 88 us; the launch traced here: 87.7 us
  waiting for transfers between devices  50 us (57%)
  starting transfers between devices  26.3 us (30%)
  Pallas kernels  8.28 us (9%)
  local copies, waits for them, and re-layouts  3.08 us (4%)
    ppermute x22, waiting for transfers between devices, flipped(): return lax.ppermute(value, axis, [(i, i ^ mask) for i in range(count)])  50 us
    ppermute x22, starting transfers between devices, flipped(): return lax.ppermute(value, axis, [(i, i ^ mask) for i in range(count)])  24.3 us
    pallas_call x1, Pallas kernels, replicated(): on_core(functools.partial(solve_kernel, members=members, pair=pair, reach...  5.33 us
    unnamed x12, local copies, waits for them, and re-layouts  3.08 us
  transfers between devices with their start and end apart: 24, of which 14 were waited for; matrix products, arithmetic and copies ran while one was open for 0% of the time, Pallas kernels for 6%

profile of v1, /device:TPU:0, one launch (start us, length us, event | category | flops | bytes accessed | tf_op | source)
XLA Modules:
  0.0 87.7 jit_solution(10382055396564887355)
XLA Ops:
  0.0 1.0 %copy-done = f32[32,2,2048]{2,1,0:T(2,128)S(1)} copy-done((f32[32,2,2048]{2,1,0:T(2,128)S(1)}, f32[32,2,2048]{2,1,0:T(2,128)}, u32[]{:S(2)}) %copy-start) | copy-done | bytes 524312
  1.0 0.7 copy-done.1
  1.8 0.2 shard_map.64
  1.9 0.6 collective-permute-start
  2.5 1.2 %collective-permute-done.got_ref.refs_1_ = f32[4,72,256]{2,1,0:T(8,128)S(1)} collective-permute-done((f32[4,72,256]{2,1,0:T(8,128)S(1)}, f32[4,72,256]{2,1,0:T(8,128)S(1)}, u32[]{:S(2)}, u32[]{:S(2)}) %collective-permute-start) | collective-permute-done | bytes 294944 | tf_op jit(solution)/shard_map/ppermute | solution.py:28
  3.7 2.9 %collective-permute-start.1 = (f32[2,72,256]{2,1,0:T(8,128)S(1)}, f32[2,72,256]{2,1,0:T(8,128)S(1)}, u32[]{:S(2)}, u32[]{:S(2)}) collective-permute-start(f32[2,72,256]{2,1,0:T(8,128)S(1)} %get-tuple-element.21), channel_id=1, source_target_pairs={{0,2},{1,3},{2,0},{3,1},{4,6},{5,7},{6,4},{7,5},{8,10},{9,11},{10,... | collective-permute-start | bytes 442376 | tf_op jit(solution)/shard_map/ppermute | solution.py:28
  6.7 1.5 %collective-permute-start.2 = (f32[2,72,256]{2,1,0:T(8,128)S(1)}, f32[2,72,256]{2,1,0:T(8,128)S(1)}, u32[]{:S(2)}, u32[]{:S(2)}) collective-permute-start(f32[2,72,256]{2,1,0:T(8,128)S(1)} %get-tuple-element.22), channel_id=1, source_target_pairs={{0,4},{1,5},{2,6},{3,7},{4,0},{5,1},{6,2},{7,3},{8,12},{9,13},{10,... | collective-permute-start | bytes 442376 | tf_op jit(solution)/shard_map/ppermute | solution.py:28
  8.2 0.0 collective-permute-start.3
  8.2 3.1 %collective-permute-done.1.refs_2_ = f32[2,72,256]{2,1,0:T(8,128)S(1)} collective-permute-done((f32[2,72,256]{2,1,0:T(8,128)S(1)}, f32[2,72,256]{2,1,0:T(8,128)S(1)}, u32[]{:S(2)}, u32[]{:S(2)}) %collective-permute-start.1) | collective-permute-done | bytes 147488 | tf_op jit(solution)/shard_map/ppermute | solution.py:28
  11.3 4.1 %collective-permute-done.2.refs_3_ = f32[2,72,256]{2,1,0:T(8,128)S(1)} collective-permute-done((f32[2,72,256]{2,1,0:T(8,128)S(1)}, f32[2,72,256]{2,1,0:T(8,128)S(1)}, u32[]{:S(2)}, u32[]{:S(2)}) %collective-permute-start.2) | collective-permute-done | bytes 147488 | tf_op jit(solution)/shard_map/ppermute | solution.py:28
  15.4 0.0 collective-permute-done.3.refs_4_
  15.4 0.5 shard_map.66
  15.9 0.1 collective-permute-start.4
  16.0 1.5 %collective-permute-done.4.got_ref = f32[4,64,256]{2,1,0:T(8,128)S(1)} collective-permute-done((f32[4,64,256]{2,1,0:T(8,128)S(1)}, f32[4,64,256]{2,1,0:T(8,128)S(1)}, u32[]{:S(2)}, u32[]{:S(2)}) %collective-permute-start.4) | collective-permute-done | bytes 262176 | tf_op jit(solution)/shard_map/ppermute | solution.py:28
  17.6 1.3 %collective-permute-start.5 = (f32[2,64,256]{2,1,0:T(8,128)S(1)}, f32[2,64,256]{2,1,0:T(8,128)S(1)}, u32[]{:S(2)}, u32[]{:S(2)}) collective-permute-start(f32[2,64,256]{2,1,0:T(8,128)S(1)} %get-tuple-element.27), channel_id=1, source_target_pairs={{0,2},{1,3},{2,0},{3,1},{4,6},{5,7},{6,4},{7,5},{8,10},{9,11},{10,... | collective-permute-start | bytes 393224 | tf_op jit(solution)/shard_map/ppermute | solution.py:28
  18.9 0.8 collective-permute-start.6
  19.7 1.4 %collective-permute-start.7 = (f32[2,64,256]{2,1,0:T(8,128)S(1)}, f32[2,64,256]{2,1,0:T(8,128)S(1)}, u32[]{:S(2)}, u32[]{:S(2)}) collective-permute-start(f32[2,64,256]{2,1,0:T(8,128)S(1)} %get-tuple-element.29), channel_id=1, source_target_pairs={{0,6},{1,7},{2,4},{3,5},{4,2},{5,3},{6,0},{7,1},{8,14},{9,15},{10,... | collective-permute-start | bytes 393224 | tf_op jit(solution)/shard_map/ppermute | solution.py:28
  21.1 2.7 %collective-permute-done.5.refs_1_ = f32[2,64,256]{2,1,0:T(8,128)S(1)} collective-permute-done((f32[2,64,256]{2,1,0:T(8,128)S(1)}, f32[2,64,256]{2,1,0:T(8,128)S(1)}, u32[]{:S(2)}, u32[]{:S(2)}) %collective-permute-start.5) | collective-permute-done | bytes 131104 | tf_op jit(solution)/shard_map/ppermute | solution.py:28
  23.8 1.5 %collective-permute-done.6.refs_2_ = f32[2,64,256]{2,1,0:T(8,128)S(1)} collective-permute-done((f32[2,64,256]{2,1,0:T(8,128)S(1)}, f32[2,64,256]{2,1,0:T(8,128)S(1)}, u32[]{:S(2)}, u32[]{:S(2)}) %collective-permute-start.6) | collective-permute-done | bytes 131104 | tf_op jit(solution)/shard_map/ppermute | solution.py:28
  25.3 1.6 %collective-permute-done.7.refs_3_ = f32[2,64,256]{2,1,0:T(8,128)S(1)} collective-permute-done((f32[2,64,256]{2,1,0:T(8,128)S(1)}, f32[2,64,256]{2,1,0:T(8,128)S(1)}, u32[]{:S(2)}, u32[]{:S(2)}) %collective-permute-start.7) | collective-permute-done | bytes 131104 | tf_op jit(solution)/shard_map/ppermute | solution.py:28
  26.9 0.7 copy-done.3
  27.6 0.5 shard_map.68
  28.1 2.7 %collective-permute-start.11 = (f32[6,64,256]{2,1,0:T(8,128)S(1)}, f32[6,64,256]{2,1,0:T(8,128)S(1)}, u32[]{:S(2)}, u32[]{:S(2)}) collective-permute-start(f32[6,64,256]{2,1,0:T(8,128)S(1)} %get-tuple-element.31), channel_id=1, source_target_pairs={{0,16},{8,24},{16,0},{24,8},{1,17},{9,25},{17,1},{25,9},{2,18},{10... | collective-permute-start | bytes 1179656 | tf_op jit(solution)/shard_map/ppermute | solution.py:28
  30.8 0.3 collective-permute-start.10
  31.1 3.6 %collective-permute-start.16 = (f32[32,128]{1,0:T(8,128)S(1)}, f32[32,128]{1,0:T(8,128)S(1)}, u32[]{:S(2)}, u32[]{:S(2)}) collective-permute-start(f32[32,128]{1,0:T(8,128)S(1)} %get-tuple-element.32.refs_0_), channel_id=1, source_target_pairs={{0,24},{8,16},{16,8},{24,0},{1,25},{9,17},{17,9},{25,1},{2,26},{10... | collective-permute-start | bytes 49160 | tf_op jit(solution)/shard_map/ppermute | solution.py:28
  34.7 0.0 collective-permute-start.15
  34.7 0.8 collective-permute-start.14
  35.5 8.5 %collective-permute-done.16.refs_3_ = f32[32,128]{1,0:T(8,128)S(1)} collective-permute-done((f32[32,128]{1,0:T(8,128)S(1)}, f32[32,128]{1,0:T(8,128)S(1)}, u32[]{:S(2)}, u32[]{:S(2)}) %collective-permute-start.16) | collective-permute-done | bytes 16416 | tf_op jit(solution)/shard_map/ppermute | solution.py:28
  44.0 10.9 %collective-permute-done.15.refs_2_ = f32[32,128]{1,0:T(8,128)S(1)} collective-permute-done((f32[32,128]{1,0:T(8,128)S(1)}, f32[32,128]{1,0:T(8,128)S(1)}, u32[]{:S(2)}, u32[]{:S(2)}) %collective-permute-start.15) | collective-permute-done | bytes 16416 | tf_op jit(solution)/shard_map/ppermute | solution.py:28
  54.8 0.0 collective-permute-done.14.refs_1_
  54.8 0.6 copy-done.4
  55.5 0.0 copy-done.5
  55.5 1.3 %collective-permute-start.22 = (f32[168,128]{1,0:T(8,128)S(1)}, f32[168,128]{1,0:T(8,128)S(1)}, u32[]{:S(2)}, u32[]{:S(2)}) collective-permute-start(f32[168,128]{1,0:T(8,128)S(1)} %shard_map.70.refs_0_), channel_id=1, source_target_pairs={{0,6},{1,7},{2,4},{3,5},{4,2},{5,3},{6,0},{7,1},{8,14},{9,15},{10,... | collective-permute-start | bytes 258056 | tf_op jit(solution)/shard_map/ppermute | solution.py:28
  56.8 0.7 collective-permute-start.20
  57.5 0.7 collective-permute-start.12
  58.2 0.0 collective-permute-done.11.rest_ref
  58.3 1.3 %collective-permute-start.13 = (f32[8,64,256]{2,1,0:T(8,128)S(1)}, f32[8,64,256]{2,1,0:T(8,128)S(1)}, u32[]{:S(2)}, u32[]{:S(2)}) collective-permute-start(f32[8,64,256]{2,1,0:T(8,128)S(1)} %shard_map.69.far_ref), channel_id=1, source_target_pairs={{16,24},{8,0},{17,25},{9,1},{18,26},{10,2},{19,27},{11,3},{20,28},... | collective-permute-start | bytes 1572872 | tf_op jit(solution)/shard_map/ppermute | solution.py:516
  59.6 1.6 %collective-permute-start.18 = (f32[168,128]{1,0:T(8,128)S(1)}, f32[168,128]{1,0:T(8,128)S(1)}, u32[]{:S(2)}, u32[]{:S(2)}) collective-permute-start(f32[168,128]{1,0:T(8,128)S(1)} %shard_map.70.refs_0_), channel_id=1, source_target_pairs={{0,2},{1,3},{2,0},{3,1},{4,6},{5,7},{6,4},{7,5},{8,10},{9,11},{10,... | collective-permute-start | bytes 258056 | tf_op jit(solution)/shard_map/ppermute | solution.py:28
  61.2 0.7 collective-permute-done.20.refs_4_
  61.9 2.2 %collective-permute-done.18.refs_2_ = f32[168,128]{1,0:T(8,128)S(1)} collective-permute-done((f32[168,128]{1,0:T(8,128)S(1)}, f32[168,128]{1,0:T(8,128)S(1)}, u32[]{:S(2)}, u32[]{:S(2)}) %collective-permute-start.18) | collective-permute-done | bytes 86048 | tf_op jit(solution)/shard_map/ppermute | solution.py:28
  64.1 4.1 %collective-permute-start.9 = (f32[6,64,256]{2,1,0:T(8,128)S(1)}, f32[6,64,256]{2,1,0:T(8,128)S(1)}, u32[]{:S(2)}, u32[]{:S(2)}) collective-permute-start(f32[6,64,256]{2,1,0:T(8,128)S(1)} %get-tuple-element.31), channel_id=1, source_target_pairs={{0,8},{8,0},{16,24},{24,16},{1,9},{9,1},{17,25},{25,17},{2,10},{10... | collective-permute-start | bytes 1179656 | tf_op jit(solution)/shard_map/ppermute | solution.py:28
  68.3 0.5 collective-permute-start.19
  68.8 0.8 collective-permute-done.21.refs_5_
  69.5 0.0 collective-permute-start.8
  69.5 0.2 collective-permute-done.19.refs_3_
  69.7 5.3 %shard_map.71.gain_ref = f32[2,32,128]{2,1,0:T(8,128)S(1)} custom-call(f32[168,128]{1,0:T(8,128)S(1)} %shard_map.70.refs_0_, f32[168,128]{1,0:T(8,128)S(1)} %collective-permute-done.17.refs_1_, f32[168,128]{1,0:T(8,128)S(1)} %collective-permute-done.18.refs_2_, f32[168,128]{1,0:T(8,128)S(1)} %collective-permute-done.19.refs_3_, ...), custom_call_target="tpu_custom_call" | custom-call | flops 3221225472 | bytes 655360 | tf_op jit(solution)/shard_map/pallas_call | solution.py:524
  75.0 11.0 %collective-permute-done.8.home_ref = f32[2,64,256]{2,1,0:T(8,128)S(1)} collective-permute-done((f32[2,64,256]{2,1,0:T(8,128)S(1)}, f32[2,64,256]{2,1,0:T(8,128)S(1)}, u32[]{:S(2)}, u32[]{:S(2)}) %collective-permute-start.8) | collective-permute-done | bytes 131104 | tf_op jit(solution)/shard_map/ppermute | solution.py:28
  86.1 1.7 %shard_map.72 = f32[32,2,2048]{2,1,0:T(2,128)} custom-call(f32[8,64,256]{2,1,0:T(8,128)S(1)} %get-tuple-element.30.own_ref, f32[2,64,256]{2,1,0:T(8,128)S(1)} %collective-permute-done.8.home_ref, f32[6,64,256]{2,1,0:T(8,128)S(1)} %collective-permute-done.9.rest_ref, f32[8,64,256]{2,1,0:T(8,128)S(1)} %shard_map.69.far_ref, ...), custom_call_target="tpu_custom_call" | custom-call | flops 100663296 | bytes 3145728 | tf_op jit(solution)/shard_map/pallas_call | solution.py:545
  (21 shorter events, 0.2 us)
Async XLA Ops:
  0.0 1.0 %copy-start = (f32[32,2,2048]{2,1,0:T(2,128)S(1)}, f32[32,2,2048]{2,1,0:T(2,128)}, u32[]{:S(2)}) copy-start(f32[32,2,2048]{2,1,0:T(2,128)} %ens_ref.1) | copy-start | bytes 1572868
  1.0 0.7 copy-start.1
  1.9 1.8 %collective-permute-start = (f32[4,72,256]{2,1,0:T(8,128)S(1)}, f32[4,72,256]{2,1,0:T(8,128)S(1)}, u32[]{:S(2)}, u32[]{:S(2)}) collective-permute-start(f32[4,72,256]{2,1,0:T(8,128)S(1)} %get-tuple-element.20), channel_id=1, source_target_pairs={{0,1},{1,0},{2,3},{3,2},{4,5},{5,4},{6,7},{7,6},{8,9},{9,8},{10,11... | collective-permute-start | bytes 884744 | tf_op jit(solution)/shard_map/ppermute | solution.py:28
  3.7 7.6 %collective-permute-start.1 = (f32[2,72,256]{2,1,0:T(8,128)S(1)}, f32[2,72,256]{2,1,0:T(8,128)S(1)}, u32[]{:S(2)}, u32[]{:S(2)}) collective-permute-start(f32[2,72,256]{2,1,0:T(8,128)S(1)} %get-tuple-element.21), channel_id=1, source_target_pairs={{0,2},{1,3},{2,0},{3,1},{4,6},{5,7},{6,4},{7,5},{8,10},{9,11},{10,... | collective-permute-start | bytes 442376 | tf_op jit(solution)/shard_map/ppermute | solution.py:28
  6.7 8.8 %collective-permute-start.2 = (f32[2,72,256]{2,1,0:T(8,128)S(1)}, f32[2,72,256]{2,1,0:T(8,128)S(1)}, u32[]{:S(2)}, u32[]{:S(2)}) collective-permute-start(f32[2,72,256]{2,1,0:T(8,128)S(1)} %get-tuple-element.22), channel_id=1, source_target_pairs={{0,4},{1,5},{2,6},{3,7},{4,0},{5,1},{6,2},{7,3},{8,12},{9,13},{10,... | collective-permute-start | bytes 442376 | tf_op jit(solution)/shard_map/ppermute | solution.py:28
  8.2 7.3 %collective-permute-start.3 = (f32[2,72,256]{2,1,0:T(8,128)S(1)}, f32[2,72,256]{2,1,0:T(8,128)S(1)}, u32[]{:S(2)}, u32[]{:S(2)}) collective-permute-start(f32[2,72,256]{2,1,0:T(8,128)S(1)} %get-tuple-element.23), channel_id=1, source_target_pairs={{0,6},{1,7},{2,4},{3,5},{4,2},{5,3},{6,0},{7,1},{8,14},{9,15},{10,... | collective-permute-start | bytes 442376 | tf_op jit(solution)/shard_map/ppermute | solution.py:28
  15.9 1.6 %collective-permute-start.4 = (f32[4,64,256]{2,1,0:T(8,128)S(1)}, f32[4,64,256]{2,1,0:T(8,128)S(1)}, u32[]{:S(2)}, u32[]{:S(2)}) collective-permute-start(f32[4,64,256]{2,1,0:T(8,128)S(1)} %get-tuple-element.25), channel_id=1, source_target_pairs={{0,1},{1,0},{2,3},{3,2},{4,5},{5,4},{6,7},{7,6},{8,9},{9,8},{10,11... | collective-permute-start | bytes 786440 | tf_op jit(solution)/shard_map/ppermute | solution.py:28
  17.6 6.3 %collective-permute-start.5 = (f32[2,64,256]{2,1,0:T(8,128)S(1)}, f32[2,64,256]{2,1,0:T(8,128)S(1)}, u32[]{:S(2)}, u32[]{:S(2)}) collective-permute-start(f32[2,64,256]{2,1,0:T(8,128)S(1)} %get-tuple-element.27), channel_id=1, source_target_pairs={{0,2},{1,3},{2,0},{3,1},{4,6},{5,7},{6,4},{7,5},{8,10},{9,11},{10,... | collective-permute-start | bytes 393224 | tf_op jit(solution)/shard_map/ppermute | solution.py:28
  18.9 6.4 %collective-permute-start.6 = (f32[2,64,256]{2,1,0:T(8,128)S(1)}, f32[2,64,256]{2,1,0:T(8,128)S(1)}, u32[]{:S(2)}, u32[]{:S(2)}) collective-permute-start(f32[2,64,256]{2,1,0:T(8,128)S(1)} %get-tuple-element.28), channel_id=1, source_target_pairs={{0,4},{1,5},{2,6},{3,7},{4,0},{5,1},{6,2},{7,3},{8,12},{9,13},{10,... | collective-permute-start | bytes 393224 | tf_op jit(solution)/shard_map/ppermute | solution.py:28
  19.7 7.2 %collective-permute-start.7 = (f32[2,64,256]{2,1,0:T(8,128)S(1)}, f32[2,64,256]{2,1,0:T(8,128)S(1)}, u32[]{:S(2)}, u32[]{:S(2)}) collective-permute-start(f32[2,64,256]{2,1,0:T(8,128)S(1)} %get-tuple-element.29), channel_id=1, source_target_pairs={{0,6},{1,7},{2,4},{3,5},{4,2},{5,3},{6,0},{7,1},{8,14},{9,15},{10,... | collective-permute-start | bytes 393224 | tf_op jit(solution)/shard_map/ppermute | solution.py:28
  26.9 0.7 copy-start.3
  27.6 27.2 %copy-start.2 = (f32[32,128]{1,0:T(8,128)S(1)}, f32[32,128]{1,0:T(8,128)}, u32[]{:S(2)}) copy-start(f32[32,128]{1,0:T(8,128)} %refs_7_.1) | copy-start | bytes 49156
  28.1 30.1 %collective-permute-start.11 = (f32[6,64,256]{2,1,0:T(8,128)S(1)}, f32[6,64,256]{2,1,0:T(8,128)S(1)}, u32[]{:S(2)}, u32[]{:S(2)}) collective-permute-start(f32[6,64,256]{2,1,0:T(8,128)S(1)} %get-tuple-element.31), channel_id=1, source_target_pairs={{0,16},{8,24},{16,0},{24,8},{1,17},{9,25},{17,1},{25,9},{2,18},{10... | collective-permute-start | bytes 1179656 | tf_op jit(solution)/shard_map/ppermute | solution.py:28
  30.8 27.4 %collective-permute-start.10 = (f32[2,64,256]{2,1,0:T(8,128)S(1)}, f32[2,64,256]{2,1,0:T(8,128)S(1)}, u32[]{:S(2)}, u32[]{:S(2)}) collective-permute-start(f32[2,64,256]{2,1,0:T(8,128)S(1)} %get-tuple-element.26.refs_0_), channel_id=1, source_target_pairs={{0,16},{8,24},{16,0},{24,8},{1,17},{9,25},{17,1},{25,9},{2,18},{10... | collective-permute-start | bytes 393224 | tf_op jit(solution)/shard_map/ppermute | solution.py:28
  31.1 12.8 %collective-permute-start.16 = (f32[32,128]{1,0:T(8,128)S(1)}, f32[32,128]{1,0:T(8,128)S(1)}, u32[]{:S(2)}, u32[]{:S(2)}) collective-permute-start(f32[32,128]{1,0:T(8,128)S(1)} %get-tuple-element.32.refs_0_), channel_id=1, source_target_pairs={{0,24},{8,16},{16,8},{24,0},{1,25},{9,17},{17,9},{25,1},{2,26},{10... | collective-permute-start | bytes 49160 | tf_op jit(solution)/shard_map/ppermute | solution.py:28
  34.7 20.1 %collective-permute-start.15 = (f32[32,128]{1,0:T(8,128)S(1)}, f32[32,128]{1,0:T(8,128)S(1)}, u32[]{:S(2)}, u32[]{:S(2)}) collective-permute-start(f32[32,128]{1,0:T(8,128)S(1)} %get-tuple-element.32.refs_0_), channel_id=1, source_target_pairs={{0,16},{8,24},{16,0},{24,8},{1,17},{9,25},{17,1},{25,9},{2,18},{10... | collective-permute-start | bytes 49160 | tf_op jit(solution)/shard_map/ppermute | solution.py:28
  34.7 20.1 %collective-permute-start.14 = (f32[32,128]{1,0:T(8,128)S(1)}, f32[32,128]{1,0:T(8,128)S(1)}, u32[]{:S(2)}, u32[]{:S(2)}) collective-permute-start(f32[32,128]{1,0:T(8,128)S(1)} %get-tuple-element.32.refs_0_), channel_id=1, source_target_pairs={{0,8},{8,0},{16,24},{24,16},{1,9},{9,1},{17,25},{25,17},{2,10},{10... | collective-permute-start | bytes 49160 | tf_op jit(solution)/shard_map/ppermute | solution.py:28
  54.8 0.7 copy-start.4
  54.8 0.7 copy-start.5
  55.5 5.7 %collective-permute-start.22 = (f32[168,128]{1,0:T(8,128)S(1)}, f32[168,128]{1,0:T(8,128)S(1)}, u32[]{:S(2)}, u32[]{:S(2)}) collective-permute-start(f32[168,128]{1,0:T(8,128)S(1)} %shard_map.70.refs_0_), channel_id=1, source_target_pairs={{0,6},{1,7},{2,4},{3,5},{4,2},{5,3},{6,0},{7,1},{8,14},{9,15},{10,... | collective-permute-start | bytes 258056 | tf_op jit(solution)/shard_map/ppermute | solution.py:28
  56.8 5.1 %collective-permute-start.20 = (f32[168,128]{1,0:T(8,128)S(1)}, f32[168,128]{1,0:T(8,128)S(1)}, u32[]{:S(2)}, u32[]{:S(2)}) collective-permute-start(f32[168,128]{1,0:T(8,128)S(1)} %shard_map.70.refs_0_), channel_id=1, source_target_pairs={{0,4},{1,5},{2,6},{3,7},{4,0},{5,1},{6,2},{7,3},{8,12},{9,13},{10,... | collective-permute-start | bytes 258056 | tf_op jit(solution)/shard_map/ppermute | solution.py:28
  57.5 28.6 %collective-permute-start.12 = (f32[8,64,256]{2,1,0:T(8,128)S(1)}, f32[8,64,256]{2,1,0:T(8,128)S(1)}, u32[]{:S(2)}, u32[]{:S(2)}) collective-permute-start(f32[8,64,256]{2,1,0:T(8,128)S(1)} %get-tuple-element.30.own_ref), channel_id=1, source_target_pairs={{8,16},{16,8},{9,17},{17,9},{10,18},{18,10},{11,19},{19,11},{12,20... | collective-permute-start | bytes 1572872 | tf_op jit(solution)/shard_map/ppermute | solution.py:514
  58.3 27.8 %collective-permute-start.13 = (f32[8,64,256]{2,1,0:T(8,128)S(1)}, f32[8,64,256]{2,1,0:T(8,128)S(1)}, u32[]{:S(2)}, u32[]{:S(2)}) collective-permute-start(f32[8,64,256]{2,1,0:T(8,128)S(1)} %shard_map.69.far_ref), channel_id=1, source_target_pairs={{16,24},{8,0},{17,25},{9,1},{18,26},{10,2},{19,27},{11,3},{20,28},... | collective-permute-start | bytes 1572872 | tf_op jit(solution)/shard_map/ppermute | solution.py:516
  59.6 4.6 %collective-permute-start.18 = (f32[168,128]{1,0:T(8,128)S(1)}, f32[168,128]{1,0:T(8,128)S(1)}, u32[]{:S(2)}, u32[]{:S(2)}) collective-permute-start(f32[168,128]{1,0:T(8,128)S(1)} %shard_map.70.refs_0_), channel_id=1, source_target_pairs={{0,2},{1,3},{2,0},{3,1},{4,6},{5,7},{6,4},{7,5},{8,10},{9,11},{10,... | collective-permute-start | bytes 258056 | tf_op jit(solution)/shard_map/ppermute | solution.py:28
  61.2 7.0 %collective-permute-start.17 = (f32[168,128]{1,0:T(8,128)S(1)}, f32[168,128]{1,0:T(8,128)S(1)}, u32[]{:S(2)}, u32[]{:S(2)}) collective-permute-start(f32[168,128]{1,0:T(8,128)S(1)} %shard_map.70.refs_0_), channel_id=1, source_target_pairs={{0,1},{1,0},{2,3},{3,2},{4,5},{5,4},{6,7},{7,6},{8,9},{9,8},{10,11... | collective-permute-start | bytes 258056 | tf_op jit(solution)/shard_map/ppermute | solution.py:28
  61.9 6.4 %collective-permute-start.23 = (f32[168,128]{1,0:T(8,128)S(1)}, f32[168,128]{1,0:T(8,128)S(1)}, u32[]{:S(2)}, u32[]{:S(2)}) collective-permute-start(f32[168,128]{1,0:T(8,128)S(1)} %collective-permute-done.22.refs_6_), channel_id=1, source_target_pairs={{0,1},{1,0},{2,3},{3,2},{4,5},{5,4},{6,7},{7,6},{8,9},{9,8},{10,11... | collective-permute-start | bytes 258056 | tf_op jit(solution)/shard_map/ppermute | solution.py:28
  64.1 21.9 %collective-permute-start.9 = (f32[6,64,256]{2,1,0:T(8,128)S(1)}, f32[6,64,256]{2,1,0:T(8,128)S(1)}, u32[]{:S(2)}, u32[]{:S(2)}) collective-permute-start(f32[6,64,256]{2,1,0:T(8,128)S(1)} %get-tuple-element.31), channel_id=1, source_target_pairs={{0,8},{8,0},{16,24},{24,16},{1,9},{9,1},{17,25},{25,17},{2,10},{10... | collective-permute-start | bytes 1179656 | tf_op jit(solution)/shard_map/ppermute | solution.py:28
  68.3 1.3 %collective-permute-start.21 = (f32[168,128]{1,0:T(8,128)S(1)}, f32[168,128]{1,0:T(8,128)S(1)}, u32[]{:S(2)}, u32[]{:S(2)}) collective-permute-start(f32[168,128]{1,0:T(8,128)S(1)} %collective-permute-done.20.refs_4_), channel_id=1, source_target_pairs={{0,1},{1,0},{2,3},{3,2},{4,5},{5,4},{6,7},{7,6},{8,9},{9,8},{10,11... | collective-permute-start | bytes 258056 | tf_op jit(solution)/shard_map/ppermute | solution.py:28
  68.3 1.4 %collective-permute-start.19 = (f32[168,128]{1,0:T(8,128)S(1)}, f32[168,128]{1,0:T(8,128)S(1)}, u32[]{:S(2)}, u32[]{:S(2)}) collective-permute-start(f32[168,128]{1,0:T(8,128)S(1)} %collective-permute-done.18.refs_2_), channel_id=1, source_target_pairs={{0,1},{1,0},{2,3},{3,2},{4,5},{5,4},{6,7},{7,6},{8,9},{9,8},{10,11... | collective-permute-start | bytes 258056 | tf_op jit(solution)/shard_map/ppermute | solution.py:28
  69.5 16.5 %collective-permute-start.8 = (f32[2,64,256]{2,1,0:T(8,128)S(1)}, f32[2,64,256]{2,1,0:T(8,128)S(1)}, u32[]{:S(2)}, u32[]{:S(2)}) collective-permute-start(f32[2,64,256]{2,1,0:T(8,128)S(1)} %get-tuple-element.26.refs_0_), channel_id=1, source_target_pairs={{0,8},{8,0},{16,24},{24,16},{1,9},{9,1},{17,25},{25,17},{2,10},{10... | collective-permute-start | bytes 393224 | tf_op jit(solution)/shard_map/ppermute | solution.py:28

commit v2 on v1

--- a/solution.py
+++ b/solution.py
@@ -251,10 +251,13 @@
 
 def stack_kernel(*refs, planes_dev, plane_cells):
     seen, (cell_ref, value_ref, var_ref, noise_ref, out_ref) = refs[:-5], refs[-5:]
+    group = lax.axis_index("mem")
+    mid = jnp.logical_and(group > 0, group < lax.axis_size("mem") - 1)
+    own, one, two, three = (ref[...] for ref in seen)
     row = 0
-    for ref in seen:
-        out_ref[row : row + ref.shape[0]] = ref[...]
-        row += ref.shape[0]
+    for values in (own, jnp.where(mid, two, one), jnp.where(mid, one, two), three):
+        out_ref[row : row + values.shape[0]] = values
+        row += values.shape[0]
     wanted = value_ref[...] + jnp.sqrt(var_ref[...]) * noise_ref[...]
     out_ref[row : row + wanted.shape[0]] = wanted
     base = lax.axis_index("space") * planes_dev
@@ -264,12 +267,6 @@
         place = place + jnp.where(local >= plane * plane_cells, 1.0, 0.0)
     fill = jnp.zeros((SUBLANES - 2, local.shape[1]), jnp.float32)
     out_ref[row + wanted.shape[0] :] = jnp.concatenate([var_ref[...], place, fill], axis=0)
-
-
-def merge_kernel(home_ref, rest_ref, out_ref):
-    split = home_ref.shape[0]
-    out_ref[:split] = home_ref[...]
-    out_ref[split:] = rest_ref[...]
 
 
 def solve_kernel(*refs, members, members_dev, planes_dev, pair, reach_slabs):
@@ -414,34 +411,70 @@
         gain_ref[plane] = gain[plane * members_dev : (plane + 1) * members_dev]
 
 
-def update_kernel(own_ref, home_ref, rest_ref, far_ref, middle_ref, end_ref, gain_ref, out_ref):
-    blocks, _, width = own_ref.shape
-    members_dev, planes_dev = out_ref.shape[:2]
-    split = home_ref.shape[0]
-    member_count = jnp.float32(gain_ref.shape[2])
-    me = lax.axis_index("space")
+def centred(gain_ref, plane):
+    gain = gain_ref[plane]
+    return halves(gain - jnp.mean(gain, axis=1, keepdims=True))
+
+
+def early_kernel(home_refs, rest_refs, gain_ref, part_ref, level_ref):
+    blocks, _, _ = part_ref.shape
+    planes_dev, members_dev = gain_ref.shape[:2]
+    split = home_refs[0].shape[0]
+    here = len(home_refs) * members_dev
     for plane in range(planes_dev):
-        high, low = halves(gain_ref[plane])
+        high, low = centred(gain_ref, plane)
+        high, low = high[:, :here], low[:, :here]
         both = jnp.concatenate([high, low], axis=0)
         span = slice(plane * members_dev, (plane + 1) * members_dev)
         for block in range(blocks):
-            own = own_ref[block, span, :]
-            one = home_ref[block, span, :] if block < split else rest_ref[block - split, span, :]
-            last = middle_ref[block, span, :] + end_ref[block, span, :]
-            values = jnp.concatenate([own, one, far_ref[block, span, :], last], axis=0)
-            anom = values - jnp.sum(values, axis=0, keepdims=True) / member_count
-            anom_hi, anom_lo = halves(anom)
+            refs, part = (home_refs, block) if block < split else (rest_refs, block - split)
+            parts = [ref[part, span, :] for ref in refs]
+            values = jnp.concatenate(parts, axis=0)
+            level = jnp.sum(values, axis=0, keepdims=True) / jnp.float32(here)
+            anom_hi, anom_lo = halves(values - level)
             change = mxu(both, anom_hi)
             change = change[:members_dev] + change[members_dev:] + mxu(high, anom_lo)
-            start = jnp.bitwise_xor(me, block) * width
-            out_ref[:, plane, pl.ds(pl.multiple_of(start, width), width)] = own + change
-
-
-def on_core(kernel, shapes, flops, moved, scratch=(), room=8, in_specs=None):
+            part_ref[block, span, :] = parts[0] + change
+            level_ref[block, plane : plane + 1, :] = level
+
+
+def update_kernel(part_ref, level_ref, middle_ref, outer_ref, gain_ref, out_hbm, out_ref, sems):
+    blocks, _, width = part_ref.shape
+    members_dev, planes_dev = out_hbm.shape[:2]
+    me = lax.axis_index("space")
+    factors = []
+    for plane in range(planes_dev):
+        high, low = centred(gain_ref, plane)
+        high, low = high[:, -members_dev:], low[:, -members_dev:]
+        factors.append((high, jnp.concatenate([high, low], axis=0)))
+    copies = []
+    for block in range(blocks):
+        for plane in range(planes_dev):
+            high, both = factors[plane]
+            span = slice(plane * members_dev, (plane + 1) * members_dev)
+            values = middle_ref[block, span, :] + outer_ref[block, span, :]
+            anom_hi, anom_lo = halves(values - level_ref[block, plane : plane + 1, :])
+            change = mxu(both, anom_hi)
+            change = change[:members_dev] + change[members_dev:] + mxu(high, anom_lo)
+            out_ref[block, :, plane, :] = part_ref[block, span, :] + change
+        start = jnp.bitwise_xor(me, block) * width
+        target = out_hbm.at[:, :, pl.ds(pl.multiple_of(start, width), width)]
+        copies.append(pltpu.make_async_copy(out_ref.at[block], target, sems.at[block]))
+        copies[-1].start()
+    for copy in copies:
+        copy.wait()
+
+
+def merge_kernel(home_ref, rest_ref, out_ref):
+    split = home_ref.shape[0]
+    out_ref[:split] = home_ref[...]
+    out_ref[split:] = rest_ref[...]
+
+
+def on_core(kernel, shapes, flops, moved, scratch=(), room=8, **extra):
     single = not isinstance(shapes, list)
     many = [shapes] if single else shapes
     out = [x if hasattr(x, "dtype") else jax.ShapeDtypeStruct(x, jnp.float32) for x in many]
-    extra = {} if in_specs is None else {"in_specs": in_specs}
     return pl.pallas_call(
         kernel,
         compiler_params=pltpu.CompilerParams(vmem_limit_bytes=room * 2**20),
@@ -484,8 +517,11 @@
     back = on_core(join_kernel, [(2, state_rows, width)] * hops, 1, 2 * state_bytes)(own, crossed)
     home = back[0]
     pieces = [home] + [flipped(back[n], "space", 2 * n) for n in range(1, hops)]
-    home_one = flipped(home, "mem", 1)
-    home_two = flipped(home, "mem", 2)
+    leading = [(0, 2), (3, 1), (1, 0), (2, 3)]
+    trailing = [(0, 1), (3, 2), (1, 3), (2, 0)]
+    outward = [(1, 0), (2, 3)]
+    home_lead = lax.ppermute(home, "mem", leading)
+    home_trail = lax.ppermute(home, "mem", trailing)
     observed, rest, whole = on_core(
         functools.partial(observe_kernel, plane_cells=plane_cells, **sizes),
         [
@@ -498,8 +534,8 @@
     )(*pieces, obs_cell[None])
 
     seen = [observed] + [flipped(observed, "mem", n) for n in range(1, mem_count)]
-    rest_one = flipped(rest, "mem", 1)
-    rest_two = flipped(rest, "mem", 2)
+    rest_lead = lax.ppermute(rest, "mem", leading)
+    rest_trail = lax.ppermute(rest, "mem", trailing)
     block = on_core(
         functools.partial(stack_kernel, planes_dev=planes_dev, plane_cells=plane_cells),
         (members + members_dev + SUBLANES, obs_dev),
@@ -512,8 +548,10 @@
         gathered += [near[n], flipped(near[n], "space", 1)]
 
     all_middle = lax.ppermute(whole, "mem", [(1, 2), (2, 1)])
-    far = on_core(merge_kernel, (slabs, state_rows, width), 1, 2 * state_bytes)(home_two, rest_two)
-    all_out = lax.ppermute(far, "mem", [(2, 3), (1, 0)])
+    passed = on_core(merge_kernel, (slabs, state_rows, width), 1, 2 * state_bytes)(
+        home_lead, rest_lead
+    )
+    all_out = lax.ppermute(passed, "mem", outward)
 
     pair = 2
     tiles = slabs // pair
@@ -542,9 +580,25 @@
         room=20,
     )(*gathered)
 
+    part, level = on_core(
+        lambda *refs: early_kernel(refs[0:3], refs[3:6], *refs[6:]),
+        [(slabs, state_rows, width), (slabs, SUBLANES, width)],
+        4 * ensemble.size * members,
+        4 * state_bytes,
+        room=12,
+    )(home, home_lead, home_trail, rest, rest_lead, rest_trail, gain)
     return on_core(
-        update_kernel, ensemble.shape, 6 * ensemble.size * members, 6 * state_bytes, room=12
-    )(whole, home_one, rest_one, far, all_middle, all_out, gain)
+        update_kernel,
+        ensemble.shape,
+        2 * ensemble.size * members,
+        4 * state_bytes,
+        [
+            pltpu.VMEM((slabs, members_dev, planes_dev, width), jnp.float32),
+            pltpu.SemaphoreType.DMA((slabs,)),
+        ],
+        room=12,
+        out_specs=pl.BlockSpec(memory_space=pltpu.HBM),
+    )(part, level, all_middle, all_out, gain)
 
 
 def shards(ensemble, forcing, obs_cell, obs_value, obs_var, obs_noise):

time: 88 us -> 76.3 us (0.87)
  waiting for transfers between devices: 50 us -> 37.9 us
    ppermute x22 -> x18, waiting for transfers between devices: 50 us -> 27.5 us  [flipped(): return lax.ppermute(value, axis, [(i, i ^ mask) for i in range(count)])]
    ppermute x1 -> x5, waiting for transfers between devices: 0.01 us -> 10.5 us  [the longest x1 9.65 us: replicated(): home_trail = lax.ppermute(home, 'mem', trailing)]
    ppermute x1 -> x5, starting transfers between devices: 1.29 us -> 8.64 us  [the longest x1 3.13 us: replicated(): rest_trail = lax.ppermute(rest, 'mem', trailing)]
    ppermute x22 -> x18, starting transfers between devices: 24.3 us -> 17.2 us  [flipped(): return lax.ppermute(value, axis, [(i, i ^ mask) for i in range(count)])]
    pallas_call x1 -> x2, Pallas kernels: 1.65 us -> 1.77 us  [the longest x1 1.22 us: replicated(): on_core(update_kernel, ensemble.shape, 2 * ensemble.size * members, 4 * s...]
  transfers between devices with their start and end apart: 24 -> 24, of which waited for: 14 -> 15; matrix products, arithmetic and copies ran while one was open for 0% -> 0% of each run, Pallas kernels for 6% -> 8%
where the time goes in v2:
time: 76.3 us; the launch traced here: 76 us
  waiting for transfers between devices  37.9 us (50%)
  starting transfers between devices  26.5 us (35%)
  Pallas kernels  8.4 us (11%)
  local copies, waits for them, and re-layouts  3.08 us (4%)
    ppermute x18, waiting for transfers between devices, flipped(): return lax.ppermute(value, axis, [(i, i ^ mask) for i in range(count)])  27.5 us
    ppermute x18, starting transfers between devices, flipped(): return lax.ppermute(value, axis, [(i, i ^ mask) for i in range(count)])  17.2 us
    ppermute x1, waiting for transfers between devices, replicated(): home_trail = lax.ppermute(home, 'mem', trailing)  9.65 us
    pallas_call x1, Pallas kernels, replicated(): on_core(functools.partial(solve_kernel, members=members, pair=pair, reach...  5.32 us
    ppermute x1, starting transfers between devices, replicated(): rest_trail = lax.ppermute(rest, 'mem', trailing)  3.13 us
    unnamed x12, local copies, waits for them, and re-layouts  3.08 us
    ppermute x1, starting transfers between devices, replicated(): rest_lead = lax.ppermute(rest, 'mem', leading)  2.64 us
    ppermute x1, starting transfers between devices, replicated(): home_lead = lax.ppermute(home, 'mem', leading)  1.57 us
  transfers between devices with their start and end apart: 24, of which 15 were waited for; matrix products, arithmetic and copies ran while one was open for 0% of the time, Pallas kernels for 8%

profile of v2, /device:TPU:0, one launch (start us, length us, event | category | flops | bytes accessed | tf_op | source)
XLA Modules:
  0.0 76.0 jit_solution(5701788462817658786)
XLA Ops:
  0.0 1.0 %copy-done = f32[32,2,2048]{2,1,0:T(2,128)S(1)} copy-done((f32[32,2,2048]{2,1,0:T(2,128)S(1)}, f32[32,2,2048]{2,1,0:T(2,128)}, u32[]{:S(2)}) %copy-start) | copy-done | bytes 524312
  1.0 0.7 copy-done.1
  1.8 0.2 shard_map.64
  1.9 0.6 collective-permute-start
  2.5 1.2 %collective-permute-done.got_ref.refs_1_ = f32[4,72,256]{2,1,0:T(8,128)S(1)} collective-permute-done((f32[4,72,256]{2,1,0:T(8,128)S(1)}, f32[4,72,256]{2,1,0:T(8,128)S(1)}, u32[]{:S(2)}, u32[]{:S(2)}) %collective-permute-start) | collective-permute-done | bytes 294944 | tf_op jit(solution)/shard_map/ppermute | solution.py:28
  3.7 2.9 %collective-permute-start.1 = (f32[2,72,256]{2,1,0:T(8,128)S(1)}, f32[2,72,256]{2,1,0:T(8,128)S(1)}, u32[]{:S(2)}, u32[]{:S(2)}) collective-permute-start(f32[2,72,256]{2,1,0:T(8,128)S(1)} %get-tuple-element.23), channel_id=1, source_target_pairs={{0,2},{1,3},{2,0},{3,1},{4,6},{5,7},{6,4},{7,5},{8,10},{9,11},{10,... | collective-permute-start | bytes 442376 | tf_op jit(solution)/shard_map/ppermute | solution.py:28
  6.7 1.5 %collective-permute-start.2 = (f32[2,72,256]{2,1,0:T(8,128)S(1)}, f32[2,72,256]{2,1,0:T(8,128)S(1)}, u32[]{:S(2)}, u32[]{:S(2)}) collective-permute-start(f32[2,72,256]{2,1,0:T(8,128)S(1)} %get-tuple-element.24), channel_id=1, source_target_pairs={{0,4},{1,5},{2,6},{3,7},{4,0},{5,1},{6,2},{7,3},{8,12},{9,13},{10,... | collective-permute-start | bytes 442376 | tf_op jit(solution)/shard_map/ppermute | solution.py:28
  8.2 0.0 collective-permute-start.3
  8.2 3.1 %collective-permute-done.1.refs_2_ = f32[2,72,256]{2,1,0:T(8,128)S(1)} collective-permute-done((f32[2,72,256]{2,1,0:T(8,128)S(1)}, f32[2,72,256]{2,1,0:T(8,128)S(1)}, u32[]{:S(2)}, u32[]{:S(2)}) %collective-permute-start.1) | collective-permute-done | bytes 147488 | tf_op jit(solution)/shard_map/ppermute | solution.py:28
  11.3 4.1 %collective-permute-done.2.refs_3_ = f32[2,72,256]{2,1,0:T(8,128)S(1)} collective-permute-done((f32[2,72,256]{2,1,0:T(8,128)S(1)}, f32[2,72,256]{2,1,0:T(8,128)S(1)}, u32[]{:S(2)}, u32[]{:S(2)}) %collective-permute-start.2) | collective-permute-done | bytes 147488 | tf_op jit(solution)/shard_map/ppermute | solution.py:28
  15.4 0.5 shard_map.66
  15.9 0.1 collective-permute-start.4
  16.0 1.5 %collective-permute-done.4.got_ref = f32[4,64,256]{2,1,0:T(8,128)S(1)} collective-permute-done((f32[4,64,256]{2,1,0:T(8,128)S(1)}, f32[4,64,256]{2,1,0:T(8,128)S(1)}, u32[]{:S(2)}, u32[]{:S(2)}) %collective-permute-start.4) | collective-permute-done | bytes 262176 | tf_op jit(solution)/shard_map/ppermute | solution.py:28
  17.6 1.3 %collective-permute-start.7 = (f32[2,64,256]{2,1,0:T(8,128)S(1)}, f32[2,64,256]{2,1,0:T(8,128)S(1)}, u32[]{:S(2)}, u32[]{:S(2)}) collective-permute-start(f32[2,64,256]{2,1,0:T(8,128)S(1)} %get-tuple-element.29), channel_id=1, source_target_pairs={{0,2},{1,3},{2,0},{3,1},{4,6},{5,7},{6,4},{7,5},{8,10},{9,11},{10,... | collective-permute-start | bytes 393224 | tf_op jit(solution)/shard_map/ppermute | solution.py:28
  18.9 0.8 %collective-permute-start.8 = (f32[2,64,256]{2,1,0:T(8,128)S(1)}, f32[2,64,256]{2,1,0:T(8,128)S(1)}, u32[]{:S(2)}, u32[]{:S(2)}) collective-permute-start(f32[2,64,256]{2,1,0:T(8,128)S(1)} %get-tuple-element.30), channel_id=1, source_target_pairs={{0,4},{1,5},{2,6},{3,7},{4,0},{5,1},{6,2},{7,3},{8,12},{9,13},{10,... | collective-permute-start | bytes 393224 | tf_op jit(solution)/shard_map/ppermute | solution.py:28
  19.7 1.4 %collective-permute-start.9 = (f32[2,64,256]{2,1,0:T(8,128)S(1)}, f32[2,64,256]{2,1,0:T(8,128)S(1)}, u32[]{:S(2)}, u32[]{:S(2)}) collective-permute-start(f32[2,64,256]{2,1,0:T(8,128)S(1)} %get-tuple-element.31), channel_id=1, source_target_pairs={{0,6},{1,7},{2,4},{3,5},{4,2},{5,3},{6,0},{7,1},{8,14},{9,15},{10,... | collective-permute-start | bytes 393224 | tf_op jit(solution)/shard_map/ppermute | solution.py:28
  21.1 2.7 %collective-permute-done.7.refs_1_ = f32[2,64,256]{2,1,0:T(8,128)S(1)} collective-permute-done((f32[2,64,256]{2,1,0:T(8,128)S(1)}, f32[2,64,256]{2,1,0:T(8,128)S(1)}, u32[]{:S(2)}, u32[]{:S(2)}) %collective-permute-start.7) | collective-permute-done | bytes 131104 | tf_op jit(solution)/shard_map/ppermute | solution.py:28
  23.8 1.5 %collective-permute-done.8.refs_2_ = f32[2,64,256]{2,1,0:T(8,128)S(1)} collective-permute-done((f32[2,64,256]{2,1,0:T(8,128)S(1)}, f32[2,64,256]{2,1,0:T(8,128)S(1)}, u32[]{:S(2)}, u32[]{:S(2)}) %collective-permute-start.8) | collective-permute-done | bytes 131104 | tf_op jit(solution)/shard_map/ppermute | solution.py:28
  25.3 1.6 %collective-permute-done.9.refs_3_ = f32[2,64,256]{2,1,0:T(8,128)S(1)} collective-permute-done((f32[2,64,256]{2,1,0:T(8,128)S(1)}, f32[2,64,256]{2,1,0:T(8,128)S(1)}, u32[]{:S(2)}, u32[]{:S(2)}) %collective-permute-start.9) | collective-permute-done | bytes 131104 | tf_op jit(solution)/shard_map/ppermute | solution.py:28
  26.9 0.7 copy-done.3
  27.6 0.5 shard_map.68
  28.1 2.6 %collective-permute-start.10 = (f32[6,64,256]{2,1,0:T(8,128)S(1)}, f32[6,64,256]{2,1,0:T(8,128)S(1)}, u32[]{:S(2)}, u32[]{:S(2)}) collective-permute-start(f32[6,64,256]{2,1,0:T(8,128)S(1)} %get-tuple-element.32.refs_3_), channel_id=1, source_target_pairs={{0,16},{24,8},{8,0},{16,24},{1,17},{25,9},{9,1},{17,25},{2,18},{26... | collective-permute-start | bytes 1179656 | tf_op jit(solution)/shard_map/ppermute | solution.py:537
  30.8 1.6 %collective-permute-start.5 = (f32[2,64,256]{2,1,0:T(8,128)S(1)}, f32[2,64,256]{2,1,0:T(8,128)S(1)}, u32[]{:S(2)}, u32[]{:S(2)}) collective-permute-start(f32[2,64,256]{2,1,0:T(8,128)S(1)} %get-tuple-element.28.refs_0_), channel_id=1, source_target_pairs={{0,16},{24,8},{8,0},{16,24},{1,17},{25,9},{9,1},{17,25},{2,18},{26... | collective-permute-start | bytes 393224 | tf_op jit(solution)/shard_map/ppermute | solution.py:523
  32.3 0.2 collective-permute-start.14
  32.6 1.7 %collective-permute-start.13 = (f32[32,128]{1,0:T(8,128)S(1)}, f32[32,128]{1,0:T(8,128)S(1)}, u32[]{:S(2)}, u32[]{:S(2)}) collective-permute-start(f32[32,128]{1,0:T(8,128)S(1)} %get-tuple-element.33.refs_0_), channel_id=1, source_target_pairs={{0,16},{8,24},{16,0},{24,8},{1,17},{9,25},{17,1},{25,9},{2,18},{10... | collective-permute-start | bytes 49160 | tf_op jit(solution)/shard_map/ppermute | solution.py:28
  34.2 2.5 %collective-permute-start.12 = (f32[32,128]{1,0:T(8,128)S(1)}, f32[32,128]{1,0:T(8,128)S(1)}, u32[]{:S(2)}, u32[]{:S(2)}) collective-permute-start(f32[32,128]{1,0:T(8,128)S(1)} %get-tuple-element.33.refs_0_), channel_id=1, source_target_pairs={{0,8},{8,0},{16,24},{24,16},{1,9},{9,1},{17,25},{25,17},{2,10},{10... | collective-permute-start | bytes 49160 | tf_op jit(solution)/shard_map/ppermute | solution.py:28
  36.7 7.2 %collective-permute-done.14.refs_3_ = f32[32,128]{1,0:T(8,128)S(1)} collective-permute-done((f32[32,128]{1,0:T(8,128)S(1)}, f32[32,128]{1,0:T(8,128)S(1)}, u32[]{:S(2)}, u32[]{:S(2)}) %collective-permute-start.14) | collective-permute-done | bytes 16416 | tf_op jit(solution)/shard_map/ppermute | solution.py:28
  43.9 0.7 collective-permute-done.13.refs_2_
  44.6 0.6 copy-done.4
  45.3 0.0 copy-done.5
  45.3 1.3 %collective-permute-start.20 = (f32[168,128]{1,0:T(8,128)S(1)}, f32[168,128]{1,0:T(8,128)S(1)}, u32[]{:S(2)}, u32[]{:S(2)}) collective-permute-start(f32[168,128]{1,0:T(8,128)S(1)} %shard_map.69.refs_0_), channel_id=1, source_target_pairs={{0,6},{1,7},{2,4},{3,5},{4,2},{5,3},{6,0},{7,1},{8,14},{9,15},{10,... | collective-permute-start | bytes 258056 | tf_op jit(solution)/shard_map/ppermute | solution.py:28
  46.6 0.7 collective-permute-start.18
  47.3 0.7 collective-permute-start.22
  48.0 1.3 %collective-permute-start.23 = (f32[8,64,256]{2,1,0:T(8,128)S(1)}, f32[8,64,256]{2,1,0:T(8,128)S(1)}, u32[]{:S(2)}, u32[]{:S(2)}) collective-permute-start(f32[8,64,256]{2,1,0:T(8,128)S(1)} %shard_map.72), channel_id=1, source_target_pairs={{8,0},{16,24},{9,1},{17,25},{10,2},{18,26},{11,3},{19,27},{12,4},{... | collective-permute-start | bytes 1572872 | tf_op jit(solution)/shard_map/ppermute | solution.py:554
  49.3 1.6 %collective-permute-start.16 = (f32[168,128]{1,0:T(8,128)S(1)}, f32[168,128]{1,0:T(8,128)S(1)}, u32[]{:S(2)}, u32[]{:S(2)}) collective-permute-start(f32[168,128]{1,0:T(8,128)S(1)} %shard_map.69.refs_0_), channel_id=1, source_target_pairs={{0,2},{1,3},{2,0},{3,1},{4,6},{5,7},{6,4},{7,5},{8,10},{9,11},{10,... | collective-permute-start | bytes 258056 | tf_op jit(solution)/shard_map/ppermute | solution.py:28
  51.0 1.6 %collective-permute-done.18.refs_4_ = f32[168,128]{1,0:T(8,128)S(1)} collective-permute-done((f32[168,128]{1,0:T(8,128)S(1)}, f32[168,128]{1,0:T(8,128)S(1)}, u32[]{:S(2)}, u32[]{:S(2)}) %collective-permute-start.18) | collective-permute-done | bytes 86048 | tf_op jit(solution)/shard_map/ppermute | solution.py:28
  52.6 0.0 collective-permute-start.21
  52.6 1.3 %collective-permute-done.16.refs_2_ = f32[168,128]{1,0:T(8,128)S(1)} collective-permute-done((f32[168,128]{1,0:T(8,128)S(1)}, f32[168,128]{1,0:T(8,128)S(1)}, u32[]{:S(2)}, u32[]{:S(2)}) %collective-permute-start.16) | collective-permute-done | bytes 86048 | tf_op jit(solution)/shard_map/ppermute | solution.py:28
  53.9 3.1 %collective-permute-start.11 = (f32[6,64,256]{2,1,0:T(8,128)S(1)}, f32[6,64,256]{2,1,0:T(8,128)S(1)}, u32[]{:S(2)}, u32[]{:S(2)}) collective-permute-start(f32[6,64,256]{2,1,0:T(8,128)S(1)} %get-tuple-element.32.refs_3_), channel_id=1, source_target_pairs={{0,8},{24,16},{8,24},{16,0},{1,9},{25,17},{9,25},{17,1},{2,10},{26... | collective-permute-start | bytes 1179656 | tf_op jit(solution)/shard_map/ppermute | solution.py:538
  57.0 0.5 collective-permute-start.17
  57.5 0.8 %collective-permute-done.19.refs_5_ = f32[168,128]{1,0:T(8,128)S(1)} collective-permute-done((f32[168,128]{1,0:T(8,128)S(1)}, f32[168,128]{1,0:T(8,128)S(1)}, u32[]{:S(2)}, u32[]{:S(2)}) %collective-permute-start.19) | collective-permute-done | bytes 86048 | tf_op jit(solution)/shard_map/ppermute | solution.py:28
  58.3 0.0 collective-permute-start.6
  58.3 0.2 collective-permute-done.17.refs_3_
  58.4 5.3 %shard_map.70.refs_6_.gain_ref = f32[2,32,128]{2,1,0:T(8,128)S(1)} custom-call(f32[168,128]{1,0:T(8,128)S(1)} %shard_map.69.refs_0_, f32[168,128]{1,0:T(8,128)S(1)} %collective-permute-done.15.refs_1_, f32[168,128]{1,0:T(8,128)S(1)} %collective-permute-done.16.refs_2_, f32[168,128]{1,0:T(8,128)S(1)} %collective-permute-done.17.refs_3_, ...), custom_call_target="tpu_custom_call" | custom-call | flops 3221225472 | bytes 655360 | tf_op jit(solution)/shard_map/pallas_call | solution.py:562
  63.8 9.7 %collective-permute-done.6.refs_2_ = f32[2,64,256]{2,1,0:T(8,128)S(1)} collective-permute-done((f32[2,64,256]{2,1,0:T(8,128)S(1)}, f32[2,64,256]{2,1,0:T(8,128)S(1)}, u32[]{:S(2)}, u32[]{:S(2)}) %collective-permute-start.6) | collective-permute-done | bytes 131104 | tf_op jit(solution)/shard_map/ppermute | solution.py:524
  73.4 0.6 shard_map.71
  74.0 0.8 %collective-permute-done.23.outer_ref = f32[8,64,256]{2,1,0:T(8,128)S(1)} collective-permute-done((f32[8,64,256]{2,1,0:T(8,128)S(1)}, f32[8,64,256]{2,1,0:T(8,128)S(1)}, u32[]{:S(2)}, u32[]{:S(2)}) %collective-permute-start.23) | collective-permute-done | bytes 524320 | tf_op jit(solution)/shard_map/ppermute | solution.py:554
  74.8 1.2 %shard_map.73 = f32[32,2,2048]{2,1,0:T(2,128)} custom-call(f32[8,64,256]{2,1,0:T(8,128)S(1)} %get-tuple-element.34.part_ref, f32[8,8,256]{2,1,0:T(8,128)S(1)} %get-tuple-element.35.level_ref, f32[8,64,256]{2,1,0:T(8,128)S(1)} %collective-permute-done.22.middle_ref, f32[8,64,256]{2,1,0:T(8,128)S(1)} %collective-permute-done.23.outer_ref, ...), custom_call_target="tpu_custom_call" | custom-call | flops 33554432 | bytes 2097152 | tf_op jit(solution)/shard_map/pallas_call | solution.py:590
  (22 shorter events, 0.2 us)
Async XLA Ops:
  0.0 1.0 %copy-start = (f32[32,2,2048]{2,1,0:T(2,128)S(1)}, f32[32,2,2048]{2,1,0:T(2,128)}, u32[]{:S(2)}) copy-start(f32[32,2,2048]{2,1,0:T(2,128)} %ens_ref.1) | copy-start | bytes 1572868
  1.0 0.7 copy-start.1
  1.9 1.8 %collective-permute-start = (f32[4,72,256]{2,1,0:T(8,128)S(1)}, f32[4,72,256]{2,1,0:T(8,128)S(1)}, u32[]{:S(2)}, u32[]{:S(2)}) collective-permute-start(f32[4,72,256]{2,1,0:T(8,128)S(1)} %get-tuple-element.22), channel_id=1, source_target_pairs={{0,1},{1,0},{2,3},{3,2},{4,5},{5,4},{6,7},{7,6},{8,9},{9,8},{10,11... | collective-permute-start | bytes 884744 | tf_op jit(solution)/shard_map/ppermute | solution.py:28
  3.7 7.6 %collective-permute-start.1 = (f32[2,72,256]{2,1,0:T(8,128)S(1)}, f32[2,72,256]{2,1,0:T(8,128)S(1)}, u32[]{:S(2)}, u32[]{:S(2)}) collective-permute-start(f32[2,72,256]{2,1,0:T(8,128)S(1)} %get-tuple-element.23), channel_id=1, source_target_pairs={{0,2},{1,3},{2,0},{3,1},{4,6},{5,7},{6,4},{7,5},{8,10},{9,11},{10,... | collective-permute-start | bytes 442376 | tf_op jit(solution)/shard_map/ppermute | solution.py:28
  6.7 8.8 %collective-permute-start.2 = (f32[2,72,256]{2,1,0:T(8,128)S(1)}, f32[2,72,256]{2,1,0:T(8,128)S(1)}, u32[]{:S(2)}, u32[]{:S(2)}) collective-permute-start(f32[2,72,256]{2,1,0:T(8,128)S(1)} %get-tuple-element.24), channel_id=1, source_target_pairs={{0,4},{1,5},{2,6},{3,7},{4,0},{5,1},{6,2},{7,3},{8,12},{9,13},{10,... | collective-permute-start | bytes 442376 | tf_op jit(solution)/shard_map/ppermute | solution.py:28
  8.2 7.3 %collective-permute-start.3 = (f32[2,72,256]{2,1,0:T(8,128)S(1)}, f32[2,72,256]{2,1,0:T(8,128)S(1)}, u32[]{:S(2)}, u32[]{:S(2)}) collective-permute-start(f32[2,72,256]{2,1,0:T(8,128)S(1)} %get-tuple-element.25), channel_id=1, source_target_pairs={{0,6},{1,7},{2,4},{3,5},{4,2},{5,3},{6,0},{7,1},{8,14},{9,15},{10,... | collective-permute-start | bytes 442376 | tf_op jit(solution)/shard_map/ppermute | solution.py:28
  15.9 1.6 %collective-permute-start.4 = (f32[4,64,256]{2,1,0:T(8,128)S(1)}, f32[4,64,256]{2,1,0:T(8,128)S(1)}, u32[]{:S(2)}, u32[]{:S(2)}) collective-permute-start(f32[4,64,256]{2,1,0:T(8,128)S(1)} %get-tuple-element.27), channel_id=1, source_target_pairs={{0,1},{1,0},{2,3},{3,2},{4,5},{5,4},{6,7},{7,6},{8,9},{9,8},{10,11... | collective-permute-start | bytes 786440 | tf_op jit(solution)/shard_map/ppermute | solution.py:28
  17.6 6.3 %collective-permute-start.7 = (f32[2,64,256]{2,1,0:T(8,128)S(1)}, f32[2,64,256]{2,1,0:T(8,128)S(1)}, u32[]{:S(2)}, u32[]{:S(2)}) collective-permute-start(f32[2,64,256]{2,1,0:T(8,128)S(1)} %get-tuple-element.29), channel_id=1, source_target_pairs={{0,2},{1,3},{2,0},{3,1},{4,6},{5,7},{6,4},{7,5},{8,10},{9,11},{10,... | collective-permute-start | bytes 393224 | tf_op jit(solution)/shard_map/ppermute | solution.py:28
  18.9 6.4 %collective-permute-start.8 = (f32[2,64,256]{2,1,0:T(8,128)S(1)}, f32[2,64,256]{2,1,0:T(8,128)S(1)}, u32[]{:S(2)}, u32[]{:S(2)}) collective-permute-start(f32[2,64,256]{2,1,0:T(8,128)S(1)} %get-tuple-element.30), channel_id=1, source_target_pairs={{0,4},{1,5},{2,6},{3,7},{4,0},{5,1},{6,2},{7,3},{8,12},{9,13},{10,... | collective-permute-start | bytes 393224 | tf_op jit(solution)/shard_map/ppermute | solution.py:28
  19.7 7.2 %collective-permute-start.9 = (f32[2,64,256]{2,1,0:T(8,128)S(1)}, f32[2,64,256]{2,1,0:T(8,128)S(1)}, u32[]{:S(2)}, u32[]{:S(2)}) collective-permute-start(f32[2,64,256]{2,1,0:T(8,128)S(1)} %get-tuple-element.31), channel_id=1, source_target_pairs={{0,6},{1,7},{2,4},{3,5},{4,2},{5,3},{6,0},{7,1},{8,14},{9,15},{10,... | collective-permute-start | bytes 393224 | tf_op jit(solution)/shard_map/ppermute | solution.py:28
  26.9 0.7 copy-start.3
  27.6 17.0 %copy-start.2 = (f32[32,128]{1,0:T(8,128)S(1)}, f32[32,128]{1,0:T(8,128)}, u32[]{:S(2)}) copy-start(f32[32,128]{1,0:T(8,128)} %refs_7_.1) | copy-start | bytes 49156
  28.1 19.9 %collective-permute-start.10 = (f32[6,64,256]{2,1,0:T(8,128)S(1)}, f32[6,64,256]{2,1,0:T(8,128)S(1)}, u32[]{:S(2)}, u32[]{:S(2)}) collective-permute-start(f32[6,64,256]{2,1,0:T(8,128)S(1)} %get-tuple-element.32.refs_3_), channel_id=1, source_target_pairs={{0,16},{24,8},{8,0},{16,24},{1,17},{25,9},{9,1},{17,25},{2,18},{26... | collective-permute-start | bytes 1179656 | tf_op jit(solution)/shard_map/ppermute | solution.py:537
  30.8 17.2 %collective-permute-start.5 = (f32[2,64,256]{2,1,0:T(8,128)S(1)}, f32[2,64,256]{2,1,0:T(8,128)S(1)}, u32[]{:S(2)}, u32[]{:S(2)}) collective-permute-start(f32[2,64,256]{2,1,0:T(8,128)S(1)} %get-tuple-element.28.refs_0_), channel_id=1, source_target_pairs={{0,16},{24,8},{8,0},{16,24},{1,17},{25,9},{9,1},{17,25},{2,18},{26... | collective-permute-start | bytes 393224 | tf_op jit(solution)/shard_map/ppermute | solution.py:523
  32.3 11.6 %collective-permute-start.14 = (f32[32,128]{1,0:T(8,128)S(1)}, f32[32,128]{1,0:T(8,128)S(1)}, u32[]{:S(2)}, u32[]{:S(2)}) collective-permute-start(f32[32,128]{1,0:T(8,128)S(1)} %get-tuple-element.33.refs_0_), channel_id=1, source_target_pairs={{0,24},{8,16},{16,8},{24,0},{1,25},{9,17},{17,9},{25,1},{2,26},{10... | collective-permute-start | bytes 49160 | tf_op jit(solution)/shard_map/ppermute | solution.py:28
  32.6 12.0 %collective-permute-start.13 = (f32[32,128]{1,0:T(8,128)S(1)}, f32[32,128]{1,0:T(8,128)S(1)}, u32[]{:S(2)}, u32[]{:S(2)}) collective-permute-start(f32[32,128]{1,0:T(8,128)S(1)} %get-tuple-element.33.refs_0_), channel_id=1, source_target_pairs={{0,16},{8,24},{16,0},{24,8},{1,17},{9,25},{17,1},{25,9},{2,18},{10... | collective-permute-start | bytes 49160 | tf_op jit(solution)/shard_map/ppermute | solution.py:28
  34.2 10.3 %collective-permute-start.12 = (f32[32,128]{1,0:T(8,128)S(1)}, f32[32,128]{1,0:T(8,128)S(1)}, u32[]{:S(2)}, u32[]{:S(2)}) collective-permute-start(f32[32,128]{1,0:T(8,128)S(1)} %get-tuple-element.33.refs_0_), channel_id=1, source_target_pairs={{0,8},{8,0},{16,24},{24,16},{1,9},{9,1},{17,25},{25,17},{2,10},{10... | collective-permute-start | bytes 49160 | tf_op jit(solution)/shard_map/ppermute | solution.py:28
  44.6 0.7 copy-start.4
  44.6 0.7 copy-start.5
  45.3 5.7 %collective-permute-start.20 = (f32[168,128]{1,0:T(8,128)S(1)}, f32[168,128]{1,0:T(8,128)S(1)}, u32[]{:S(2)}, u32[]{:S(2)}) collective-permute-start(f32[168,128]{1,0:T(8,128)S(1)} %shard_map.69.refs_0_), channel_id=1, source_target_pairs={{0,6},{1,7},{2,4},{3,5},{4,2},{5,3},{6,0},{7,1},{8,14},{9,15},{10,... | collective-permute-start | bytes 258056 | tf_op jit(solution)/shard_map/ppermute | solution.py:28
  46.6 6.0 %collective-permute-start.18 = (f32[168,128]{1,0:T(8,128)S(1)}, f32[168,128]{1,0:T(8,128)S(1)}, u32[]{:S(2)}, u32[]{:S(2)}) collective-permute-start(f32[168,128]{1,0:T(8,128)S(1)} %shard_map.69.refs_0_), channel_id=1, source_target_pairs={{0,4},{1,5},{2,6},{3,7},{4,0},{5,1},{6,2},{7,3},{8,12},{9,13},{10,... | collective-permute-start | bytes 258056 | tf_op jit(solution)/shard_map/ppermute | solution.py:28
  47.3 26.7 %collective-permute-start.22 = (f32[8,64,256]{2,1,0:T(8,128)S(1)}, f32[8,64,256]{2,1,0:T(8,128)S(1)}, u32[]{:S(2)}, u32[]{:S(2)}) collective-permute-start(f32[8,64,256]{2,1,0:T(8,128)S(1)} %get-tuple-element.36), channel_id=1, source_target_pairs={{8,16},{16,8},{9,17},{17,9},{10,18},{18,10},{11,19},{19,11},{12,20... | collective-permute-start | bytes 1572872 | tf_op jit(solution)/shard_map/ppermute | solution.py:550
  48.0 26.8 %collective-permute-start.23 = (f32[8,64,256]{2,1,0:T(8,128)S(1)}, f32[8,64,256]{2,1,0:T(8,128)S(1)}, u32[]{:S(2)}, u32[]{:S(2)}) collective-permute-start(f32[8,64,256]{2,1,0:T(8,128)S(1)} %shard_map.72), channel_id=1, source_target_pairs={{8,0},{16,24},{9,1},{17,25},{10,2},{18,26},{11,3},{19,27},{12,4},{... | collective-permute-start | bytes 1572872 | tf_op jit(solution)/shard_map/ppermute | solution.py:554
  49.3 4.6 %collective-permute-start.16 = (f32[168,128]{1,0:T(8,128)S(1)}, f32[168,128]{1,0:T(8,128)S(1)}, u32[]{:S(2)}, u32[]{:S(2)}) collective-permute-start(f32[168,128]{1,0:T(8,128)S(1)} %shard_map.69.refs_0_), channel_id=1, source_target_pairs={{0,2},{1,3},{2,0},{3,1},{4,6},{5,7},{6,4},{7,5},{8,10},{9,11},{10,... | collective-permute-start | bytes 258056 | tf_op jit(solution)/shard_map/ppermute | solution.py:28
  51.0 6.0 %collective-permute-start.15 = (f32[168,128]{1,0:T(8,128)S(1)}, f32[168,128]{1,0:T(8,128)S(1)}, u32[]{:S(2)}, u32[]{:S(2)}) collective-permute-start(f32[168,128]{1,0:T(8,128)S(1)} %shard_map.69.refs_0_), channel_id=1, source_target_pairs={{0,1},{1,0},{2,3},{3,2},{4,5},{5,4},{6,7},{7,6},{8,9},{9,8},{10,11... | collective-permute-start | bytes 258056 | tf_op jit(solution)/shard_map/ppermute | solution.py:28
  52.6 4.5 %collective-permute-start.21 = (f32[168,128]{1,0:T(8,128)S(1)}, f32[168,128]{1,0:T(8,128)S(1)}, u32[]{:S(2)}, u32[]{:S(2)}) collective-permute-start(f32[168,128]{1,0:T(8,128)S(1)} %collective-permute-done.20.refs_6_), channel_id=1, source_target_pairs={{0,1},{1,0},{2,3},{3,2},{4,5},{5,4},{6,7},{7,6},{8,9},{9,8},{10,11... | collective-permute-start | bytes 258056 | tf_op jit(solution)/shard_map/ppermute | solution.py:28
  53.9 19.6 %collective-permute-start.11 = (f32[6,64,256]{2,1,0:T(8,128)S(1)}, f32[6,64,256]{2,1,0:T(8,128)S(1)}, u32[]{:S(2)}, u32[]{:S(2)}) collective-permute-start(f32[6,64,256]{2,1,0:T(8,128)S(1)} %get-tuple-element.32.refs_3_), channel_id=1, source_target_pairs={{0,8},{24,16},{8,24},{16,0},{1,9},{25,17},{9,25},{17,1},{2,10},{26... | collective-permute-start | bytes 1179656 | tf_op jit(solution)/shard_map/ppermute | solution.py:538
  57.0 1.3 %collective-permute-start.19 = (f32[168,128]{1,0:T(8,128)S(1)}, f32[168,128]{1,0:T(8,128)S(1)}, u32[]{:S(2)}, u32[]{:S(2)}) collective-permute-start(f32[168,128]{1,0:T(8,128)S(1)} %collective-permute-done.18.refs_4_), channel_id=1, source_target_pairs={{0,1},{1,0},{2,3},{3,2},{4,5},{5,4},{6,7},{7,6},{8,9},{9,8},{10,11... | collective-permute-start | bytes 258056 | tf_op jit(solution)/shard_map/ppermute | solution.py:28
  57.0 1.4 %collective-permute-start.17 = (f32[168,128]{1,0:T(8,128)S(1)}, f32[168,128]{1,0:T(8,128)S(1)}, u32[]{:S(2)}, u32[]{:S(2)}) collective-permute-start(f32[168,128]{1,0:T(8,128)S(1)} %collective-permute-done.16.refs_2_), channel_id=1, source_target_pairs={{0,1},{1,0},{2,3},{3,2},{4,5},{5,4},{6,7},{7,6},{8,9},{9,8},{10,11... | collective-permute-start | bytes 258056 | tf_op jit(solution)/shard_map/ppermute | solution.py:28
  58.3 15.1 %collective-permute-start.6 = (f32[2,64,256]{2,1,0:T(8,128)S(1)}, f32[2,64,256]{2,1,0:T(8,128)S(1)}, u32[]{:S(2)}, u32[]{:S(2)}) collective-permute-start(f32[2,64,256]{2,1,0:T(8,128)S(1)} %get-tuple-element.28.refs_0_), channel_id=1, source_target_pairs={{0,8},{24,16},{8,24},{16,0},{1,9},{25,17},{9,25},{17,1},{2,10},{26... | collective-permute-start | bytes 393224 | tf_op jit(solution)/shard_map/ppermute | solution.py:524

commit v3 on v2

--- a/solution.py
+++ b/solution.py
@@ -155,11 +155,22 @@
     return -(-value // unit) * unit
 
 
-def pack_kernel(ens_ref, forcing_ref, give_ref, keep_ref):
-    members_dev, planes_dev, _ = ens_ref.shape
+def pack_kernel(*refs, count):
+    sources, refs = refs[:count], refs[count:]
+    give_ref, keep_ref, side_ref, local_ref, *targets, sems = refs
+    copies = [
+        pltpu.make_async_copy(source, target, sems.at[n])
+        for n, (source, target) in enumerate(zip(sources, targets))
+    ]
+    for copy in copies:
+        copy.start()
+    ens_ref, forcing_ref, cell_ref, value_ref, var_ref, noise_ref = targets
+    members_dev, planes_dev, cells = ens_ref.shape
     blocks, rows, width = give_ref.shape
     state_rows = planes_dev * members_dev
     me = lax.axis_index("space")
+    for copy in copies:
+        copy.wait()
     tail = jnp.zeros((rows - state_rows - planes_dev, width), jnp.float32)
     for hop in range(blocks):
         for ref, flip in ((give_ref, 1), (keep_ref, 0)):
@@ -169,6 +180,14 @@
                 top = plane * members_dev
                 ref[hop, top : top + members_dev, :] = ens_ref[:, plane, span]
             ref[hop, state_rows:, :] = jnp.concatenate([forcing_ref[:, span], tail], axis=0)
+    local = cell_ref[...] - me * (planes_dev * cells)
+    local_ref[...] = local
+    side_ref[:members_dev] = value_ref[...] + jnp.sqrt(var_ref[...]) * noise_ref[...]
+    place = jnp.zeros(local.shape, jnp.float32) + (me * planes_dev).astype(jnp.float32)
+    for plane in range(1, planes_dev):
+        place = place + jnp.where(local >= plane * cells, 1.0, 0.0)
+    fill = jnp.zeros((SUBLANES - 2, local.shape[1]), jnp.float32)
+    side_ref[members_dev:] = jnp.concatenate([var_ref[...], place, fill], axis=0)
 
 
 def join_kernel(keep_ref, got_ref, *outs):
@@ -225,7 +244,7 @@
     width = rest_ref.shape[2]
     obs_dev = local_ref.shape[1]
     me = lax.axis_index("space")
-    local = local_ref[...] - me * (planes_dev * plane_cells)
+    local = local_ref[...]
     total = jnp.zeros((3 * members_dev, obs_dev), jnp.float32)
     for hop, piece in enumerate(pieces):
         for flip in range(2):
@@ -249,24 +268,15 @@
     )
 
 
-def stack_kernel(*refs, planes_dev, plane_cells):
-    seen, (cell_ref, value_ref, var_ref, noise_ref, out_ref) = refs[:-5], refs[-5:]
+def stack_kernel(own_ref, one_ref, two_ref, three_ref, side_ref, out_ref):
     group = lax.axis_index("mem")
     mid = jnp.logical_and(group > 0, group < lax.axis_size("mem") - 1)
-    own, one, two, three = (ref[...] for ref in seen)
+    one, two = one_ref[...], two_ref[...]
+    ordered = (own_ref[...], jnp.where(mid, two, one), jnp.where(mid, one, two), three_ref[...])
     row = 0
-    for values in (own, jnp.where(mid, two, one), jnp.where(mid, one, two), three):
+    for values in (*ordered, side_ref[...]):
         out_ref[row : row + values.shape[0]] = values
         row += values.shape[0]
-    wanted = value_ref[...] + jnp.sqrt(var_ref[...]) * noise_ref[...]
-    out_ref[row : row + wanted.shape[0]] = wanted
-    base = lax.axis_index("space") * planes_dev
-    local = cell_ref[...] - base * plane_cells
-    place = jnp.zeros(local.shape, jnp.float32) + base.astype(jnp.float32)
-    for plane in range(1, planes_dev):
-        place = place + jnp.where(local >= plane * plane_cells, 1.0, 0.0)
-    fill = jnp.zeros((SUBLANES - 2, local.shape[1]), jnp.float32)
-    out_ref[row + wanted.shape[0] :] = jnp.concatenate([var_ref[...], place, fill], axis=0)
 
 
 def solve_kernel(*refs, members, members_dev, planes_dev, pair, reach_slabs):
@@ -499,9 +509,22 @@
     hops = slabs // 2
     sizes = dict(planes_dev=planes_dev, members_dev=members_dev)
 
-    give, keep = on_core(
-        pack_kernel, [(hops, sent_rows, width)] * 2, ensemble.size, 2 * state_bytes
-    )(ensemble, forcing)
+    inputs = (ensemble, forcing, obs_cell[None], obs_value[None], obs_var[None], obs_noise)
+    inputs = [pltpu.with_memory_space_constraint(x, pltpu.HBM) for x in inputs]
+    give, keep, side, local = on_core(
+        functools.partial(pack_kernel, count=len(inputs)),
+        [
+            (hops, sent_rows, width),
+            (hops, sent_rows, width),
+            (members_dev + SUBLANES, obs_dev),
+            jax.ShapeDtypeStruct((1, obs_dev), jnp.int32),
+        ],
+        ensemble.size,
+        2 * state_bytes,
+        [pltpu.VMEM(x.shape, x.dtype) for x in inputs]
+        + [pltpu.SemaphoreType.DMA((len(inputs),))],
+        in_specs=[pl.BlockSpec(memory_space=pltpu.HBM)] * len(inputs),
+    )(*inputs)
     got = flipped(give, "space", 1)
     sent = on_core(join_kernel, [(2, sent_rows, width)] * (hops - 1), 1, 2 * state_bytes)(keep, got)
     come = [flipped(sent[n - 1], "space", 2 * n) for n in range(1, hops)]
@@ -531,17 +554,14 @@
         ],
         6 * ensemble.size * obs_dev,
         state_bytes,
-    )(*pieces, obs_cell[None])
+    )(*pieces, local)
 
     seen = [observed] + [flipped(observed, "mem", n) for n in range(1, mem_count)]
     rest_lead = lax.ppermute(rest, "mem", leading)
     rest_trail = lax.ppermute(rest, "mem", trailing)
     block = on_core(
-        functools.partial(stack_kernel, planes_dev=planes_dev, plane_cells=plane_cells),
-        (members + members_dev + SUBLANES, obs_dev),
-        1,
-        8 * members * obs_dev,
-    )(*seen, obs_cell[None], obs_value[None], obs_var[None], obs_noise)
+        stack_kernel, (members + members_dev + SUBLANES, obs_dev), 1, 8 * members * obs_dev
+    )(*seen, side)
     near = [block] + [flipped(block, "space", 2 * n) for n in range(1, hops)]
     gathered = []
     for n in range(hops):

time: 76.3 us -> 74.2 us (0.972)
  local copies, waits for them, and re-layouts: 3.08 us -> 0 us
  Pallas kernels: 8.4 us -> 9.49 us
    unnamed x12 -> x0, local copies, waits for them, and re-layouts: 3.08 us -> none
    pallas_call x2, Pallas kernels: 0.2 us -> 1.3 us  [the longest x1 1.29 us: replicated(): on_core(functools.partial(pack_kernel, count=len(inputs)), [(hops, sent_r...]
where the time goes in v3:
time: 74.2 us; the launch traced here: 74 us
  waiting for transfers between devices  37.9 us (51%)
  starting transfers between devices  26.5 us (36%)
  Pallas kernels  9.49 us (13%)
    ppermute x18, waiting for transfers between devices, flipped(): return lax.ppermute(value, axis, [(i, i ^ mask) for i in range(count)])  27.5 us
    ppermute x18, starting transfers between devices, flipped(): return lax.ppermute(value, axis, [(i, i ^ mask) for i in range(count)])  17.2 us
    ppermute x1, waiting for transfers between devices, replicated(): home_trail = lax.ppermute(home, 'mem', trailing)  9.65 us
    pallas_call x1, Pallas kernels, replicated(): on_core(functools.partial(solve_kernel, members=members, pair=pair, reach...  5.32 us
    ppermute x1, starting transfers between devices, replicated(): rest_trail = lax.ppermute(rest, 'mem', trailing)  3.13 us
    ppermute x1, starting transfers between devices, replicated(): rest_lead = lax.ppermute(rest, 'mem', leading)  2.64 us
    ppermute x1, starting transfers between devices, replicated(): home_lead = lax.ppermute(home, 'mem', leading)  1.58 us
  transfers between devices with their start and end apart: 24, of which 15 were waited for; matrix products, arithmetic and copies ran while one was open for 0% of the time, Pallas kernels for 8%

profile of v3, /device:TPU:0, one launch (start us, length us, event | category | flops | bytes accessed | tf_op | source)
XLA Modules:
  0.0 74.0 jit_solution(421874618653367133)
XLA Ops:
  0.0 1.3 %shard_map.64 = (f32[4,72,256]{2,1,0:T(8,128)S(1)}, f32[4,72,256]{2,1,0:T(8,128)S(1)}, f32[40,128]{1,0:T(8,128)S(1)}, s32[1,128]{1,0:T(1,128)S(1)}) custom-call(f32[32,2,2048]{2,1,0:T(2,128)} %refs_0_.1, f32[2,2048]{1,0:T(2,128)} %refs_1_.1, s32[1,128]{1,0:T(1,128)} %bitcast.3, f32[1,128]{1,0:T(1,128)} %bitcast.4, f32[1,128]{1,0:T(1,128)} %bitcast.5, ...), custom_call_target="tpu_custom_call" | custom-call | flops 131072 | bytes 1048576 | tf_op jit(solution)/shard_map/pallas_call | solution.py:514
  1.3 0.6 collective-permute-start
  1.9 1.2 %collective-permute-done.got_ref.refs_1_ = f32[4,72,256]{2,1,0:T(8,128)S(1)} collective-permute-done((f32[4,72,256]{2,1,0:T(8,128)S(1)}, f32[4,72,256]{2,1,0:T(8,128)S(1)}, u32[]{:S(2)}, u32[]{:S(2)}) %collective-permute-start) | collective-permute-done | bytes 294944 | tf_op jit(solution)/shard_map/ppermute | solution.py:28
  3.1 2.9 %collective-permute-start.1 = (f32[2,72,256]{2,1,0:T(8,128)S(1)}, f32[2,72,256]{2,1,0:T(8,128)S(1)}, u32[]{:S(2)}, u32[]{:S(2)}) collective-permute-start(f32[2,72,256]{2,1,0:T(8,128)S(1)} %get-tuple-element.25), channel_id=1, source_target_pairs={{0,2},{1,3},{2,0},{3,1},{4,6},{5,7},{6,4},{7,5},{8,10},{9,11},{10,... | collective-permute-start | bytes 442376 | tf_op jit(solution)/shard_map/ppermute | solution.py:28
  6.0 1.5 %collective-permute-start.2 = (f32[2,72,256]{2,1,0:T(8,128)S(1)}, f32[2,72,256]{2,1,0:T(8,128)S(1)}, u32[]{:S(2)}, u32[]{:S(2)}) collective-permute-start(f32[2,72,256]{2,1,0:T(8,128)S(1)} %get-tuple-element.26), channel_id=1, source_target_pairs={{0,4},{1,5},{2,6},{3,7},{4,0},{5,1},{6,2},{7,3},{8,12},{9,13},{10,... | collective-permute-start | bytes 442376 | tf_op jit(solution)/shard_map/ppermute | solution.py:28
  7.5 0.0 collective-permute-start.3
  7.6 3.1 %collective-permute-done.1.refs_2_ = f32[2,72,256]{2,1,0:T(8,128)S(1)} collective-permute-done((f32[2,72,256]{2,1,0:T(8,128)S(1)}, f32[2,72,256]{2,1,0:T(8,128)S(1)}, u32[]{:S(2)}, u32[]{:S(2)}) %collective-permute-start.1) | collective-permute-done | bytes 147488 | tf_op jit(solution)/shard_map/ppermute | solution.py:28
  10.7 4.1 %collective-permute-done.2.refs_3_ = f32[2,72,256]{2,1,0:T(8,128)S(1)} collective-permute-done((f32[2,72,256]{2,1,0:T(8,128)S(1)}, f32[2,72,256]{2,1,0:T(8,128)S(1)}, u32[]{:S(2)}, u32[]{:S(2)}) %collective-permute-start.2) | collective-permute-done | bytes 147488 | tf_op jit(solution)/shard_map/ppermute | solution.py:28
  14.8 0.5 shard_map.66
  15.3 0.1 collective-permute-start.4
  15.4 1.5 %collective-permute-done.4.got_ref = f32[4,64,256]{2,1,0:T(8,128)S(1)} collective-permute-done((f32[4,64,256]{2,1,0:T(8,128)S(1)}, f32[4,64,256]{2,1,0:T(8,128)S(1)}, u32[]{:S(2)}, u32[]{:S(2)}) %collective-permute-start.4) | collective-permute-done | bytes 262176 | tf_op jit(solution)/shard_map/ppermute | solution.py:28
  16.9 1.3 %collective-permute-start.7 = (f32[2,64,256]{2,1,0:T(8,128)S(1)}, f32[2,64,256]{2,1,0:T(8,128)S(1)}, u32[]{:S(2)}, u32[]{:S(2)}) collective-permute-start(f32[2,64,256]{2,1,0:T(8,128)S(1)} %get-tuple-element.31), channel_id=1, source_target_pairs={{0,2},{1,3},{2,0},{3,1},{4,6},{5,7},{6,4},{7,5},{8,10},{9,11},{10,... | collective-permute-start | bytes 393224 | tf_op jit(solution)/shard_map/ppermute | solution.py:28
  18.2 0.8 %collective-permute-start.8 = (f32[2,64,256]{2,1,0:T(8,128)S(1)}, f32[2,64,256]{2,1,0:T(8,128)S(1)}, u32[]{:S(2)}, u32[]{:S(2)}) collective-permute-start(f32[2,64,256]{2,1,0:T(8,128)S(1)} %get-tuple-element.32), channel_id=1, source_target_pairs={{0,4},{1,5},{2,6},{3,7},{4,0},{5,1},{6,2},{7,3},{8,12},{9,13},{10,... | collective-permute-start | bytes 393224 | tf_op jit(solution)/shard_map/ppermute | solution.py:28
  19.0 1.4 %collective-permute-start.9 = (f32[2,64,256]{2,1,0:T(8,128)S(1)}, f32[2,64,256]{2,1,0:T(8,128)S(1)}, u32[]{:S(2)}, u32[]{:S(2)}) collective-permute-start(f32[2,64,256]{2,1,0:T(8,128)S(1)} %get-tuple-element.33), channel_id=1, source_target_pairs={{0,6},{1,7},{2,4},{3,5},{4,2},{5,3},{6,0},{7,1},{8,14},{9,15},{10,... | collective-permute-start | bytes 393224 | tf_op jit(solution)/shard_map/ppermute | solution.py:28
  20.5 2.7 %collective-permute-done.7.refs_1_ = f32[2,64,256]{2,1,0:T(8,128)S(1)} collective-permute-done((f32[2,64,256]{2,1,0:T(8,128)S(1)}, f32[2,64,256]{2,1,0:T(8,128)S(1)}, u32[]{:S(2)}, u32[]{:S(2)}) %collective-permute-start.7) | collective-permute-done | bytes 131104 | tf_op jit(solution)/shard_map/ppermute | solution.py:28
  23.2 1.5 %collective-permute-done.8.refs_2_ = f32[2,64,256]{2,1,0:T(8,128)S(1)} collective-permute-done((f32[2,64,256]{2,1,0:T(8,128)S(1)}, f32[2,64,256]{2,1,0:T(8,128)S(1)}, u32[]{:S(2)}, u32[]{:S(2)}) %collective-permute-start.8) | collective-permute-done | bytes 131104 | tf_op jit(solution)/shard_map/ppermute | solution.py:28
  24.7 1.6 %collective-permute-done.9.refs_3_ = f32[2,64,256]{2,1,0:T(8,128)S(1)} collective-permute-done((f32[2,64,256]{2,1,0:T(8,128)S(1)}, f32[2,64,256]{2,1,0:T(8,128)S(1)}, u32[]{:S(2)}, u32[]{:S(2)}) %collective-permute-start.9) | collective-permute-done | bytes 131104 | tf_op jit(solution)/shard_map/ppermute | solution.py:28
  26.3 0.5 shard_map.68
  26.8 2.6 %collective-permute-start.10 = (f32[6,64,256]{2,1,0:T(8,128)S(1)}, f32[6,64,256]{2,1,0:T(8,128)S(1)}, u32[]{:S(2)}, u32[]{:S(2)}) collective-permute-start(f32[6,64,256]{2,1,0:T(8,128)S(1)} %get-tuple-element.35.refs_3_), channel_id=1, source_target_pairs={{0,16},{24,8},{8,0},{16,24},{1,17},{25,9},{9,1},{17,25},{2,18},{26... | collective-permute-start | bytes 1179656 | tf_op jit(solution)/shard_map/ppermute | solution.py:560
  29.4 1.6 %collective-permute-start.5 = (f32[2,64,256]{2,1,0:T(8,128)S(1)}, f32[2,64,256]{2,1,0:T(8,128)S(1)}, u32[]{:S(2)}, u32[]{:S(2)}) collective-permute-start(f32[2,64,256]{2,1,0:T(8,128)S(1)} %get-tuple-element.30.refs_0_), channel_id=1, source_target_pairs={{0,16},{24,8},{8,0},{16,24},{1,17},{25,9},{9,1},{17,25},{2,18},{26... | collective-permute-start | bytes 393224 | tf_op jit(solution)/shard_map/ppermute | solution.py:546
  31.0 0.2 collective-permute-start.14
  31.2 1.7 %collective-permute-start.13 = (f32[32,128]{1,0:T(8,128)S(1)}, f32[32,128]{1,0:T(8,128)S(1)}, u32[]{:S(2)}, u32[]{:S(2)}) collective-permute-start(f32[32,128]{1,0:T(8,128)S(1)} %get-tuple-element.36.own_ref), channel_id=1, source_target_pairs={{0,16},{8,24},{16,0},{24,8},{1,17},{9,25},{17,1},{25,9},{2,18},{10... | collective-permute-start | bytes 49160 | tf_op jit(solution)/shard_map/ppermute | solution.py:28
  32.9 2.5 %collective-permute-start.12 = (f32[32,128]{1,0:T(8,128)S(1)}, f32[32,128]{1,0:T(8,128)S(1)}, u32[]{:S(2)}, u32[]{:S(2)}) collective-permute-start(f32[32,128]{1,0:T(8,128)S(1)} %get-tuple-element.36.own_ref), channel_id=1, source_target_pairs={{0,8},{8,0},{16,24},{24,16},{1,9},{9,1},{17,25},{25,17},{2,10},{10... | collective-permute-start | bytes 49160 | tf_op jit(solution)/shard_map/ppermute | solution.py:28
  35.4 7.2 %collective-permute-done.14.three_ref = f32[32,128]{1,0:T(8,128)S(1)} collective-permute-done((f32[32,128]{1,0:T(8,128)S(1)}, f32[32,128]{1,0:T(8,128)S(1)}, u32[]{:S(2)}, u32[]{:S(2)}) %collective-permute-start.14) | collective-permute-done | bytes 16416 | tf_op jit(solution)/shard_map/ppermute | solution.py:28
  42.6 0.7 collective-permute-done.13.two_ref
  43.3 0.0 collective-permute-done.12.one_ref
  43.3 1.3 %collective-permute-start.20 = (f32[168,128]{1,0:T(8,128)S(1)}, f32[168,128]{1,0:T(8,128)S(1)}, u32[]{:S(2)}, u32[]{:S(2)}) collective-permute-start(f32[168,128]{1,0:T(8,128)S(1)} %shard_map.69.refs_0_), channel_id=1, source_target_pairs={{0,6},{1,7},{2,4},{3,5},{4,2},{5,3},{6,0},{7,1},{8,14},{9,15},{10,... | collective-permute-start | bytes 258056 | tf_op jit(solution)/shard_map/ppermute | solution.py:28
  44.6 0.7 collective-permute-start.18
  45.3 0.7 collective-permute-start.22
  46.0 0.0 collective-permute-done.10.refs_4_.rest_ref
  46.0 1.3 %collective-permute-start.23 = (f32[8,64,256]{2,1,0:T(8,128)S(1)}, f32[8,64,256]{2,1,0:T(8,128)S(1)}, u32[]{:S(2)}, u32[]{:S(2)}) collective-permute-start(f32[8,64,256]{2,1,0:T(8,128)S(1)} %shard_map.72), channel_id=1, source_target_pairs={{8,0},{16,24},{9,1},{17,25},{10,2},{18,26},{11,3},{19,27},{12,4},{... | collective-permute-start | bytes 1572872 | tf_op jit(solution)/shard_map/ppermute | solution.py:574
  47.3 1.6 %collective-permute-start.16 = (f32[168,128]{1,0:T(8,128)S(1)}, f32[168,128]{1,0:T(8,128)S(1)}, u32[]{:S(2)}, u32[]{:S(2)}) collective-permute-start(f32[168,128]{1,0:T(8,128)S(1)} %shard_map.69.refs_0_), channel_id=1, source_target_pairs={{0,2},{1,3},{2,0},{3,1},{4,6},{5,7},{6,4},{7,5},{8,10},{9,11},{10,... | collective-permute-start | bytes 258056 | tf_op jit(solution)/shard_map/ppermute | solution.py:28
  49.0 1.6 %collective-permute-done.18.refs_4_ = f32[168,128]{1,0:T(8,128)S(1)} collective-permute-done((f32[168,128]{1,0:T(8,128)S(1)}, f32[168,128]{1,0:T(8,128)S(1)}, u32[]{:S(2)}, u32[]{:S(2)}) %collective-permute-start.18) | collective-permute-done | bytes 86048 | tf_op jit(solution)/shard_map/ppermute | solution.py:28
  50.6 0.0 collective-permute-start.21
  50.6 1.3 %collective-permute-done.16.refs_2_ = f32[168,128]{1,0:T(8,128)S(1)} collective-permute-done((f32[168,128]{1,0:T(8,128)S(1)}, f32[168,128]{1,0:T(8,128)S(1)}, u32[]{:S(2)}, u32[]{:S(2)}) %collective-permute-start.16) | collective-permute-done | bytes 86048 | tf_op jit(solution)/shard_map/ppermute | solution.py:28
  51.9 3.1 %collective-permute-start.11 = (f32[6,64,256]{2,1,0:T(8,128)S(1)}, f32[6,64,256]{2,1,0:T(8,128)S(1)}, u32[]{:S(2)}, u32[]{:S(2)}) collective-permute-start(f32[6,64,256]{2,1,0:T(8,128)S(1)} %get-tuple-element.35.refs_3_), channel_id=1, source_target_pairs={{0,8},{24,16},{8,24},{16,0},{1,9},{25,17},{9,25},{17,1},{2,10},{26... | collective-permute-start | bytes 1179656 | tf_op jit(solution)/shard_map/ppermute | solution.py:561
  55.0 0.0 collective-permute-done.15.refs_1_
  55.0 0.0 collective-permute-start.19
  55.0 0.5 collective-permute-start.17
  55.5 0.8 %collective-permute-done.19.refs_5_ = f32[168,128]{1,0:T(8,128)S(1)} collective-permute-done((f32[168,128]{1,0:T(8,128)S(1)}, f32[168,128]{1,0:T(8,128)S(1)}, u32[]{:S(2)}, u32[]{:S(2)}) %collective-permute-start.19) | collective-permute-done | bytes 86048 | tf_op jit(solution)/shard_map/ppermute | solution.py:28
  56.3 0.0 collective-permute-start.6
  56.3 0.2 collective-permute-done.17.refs_3_
  56.5 5.3 %shard_map.70.refs_6_.gain_ref = f32[2,32,128]{2,1,0:T(8,128)S(1)} custom-call(f32[168,128]{1,0:T(8,128)S(1)} %shard_map.69.refs_0_, f32[168,128]{1,0:T(8,128)S(1)} %collective-permute-done.15.refs_1_, f32[168,128]{1,0:T(8,128)S(1)} %collective-permute-done.16.refs_2_, f32[168,128]{1,0:T(8,128)S(1)} %collective-permute-done.17.refs_3_, ...), custom_call_target="tpu_custom_call" | custom-call | flops 3221225472 | bytes 655360 | tf_op jit(solution)/shard_map/pallas_call | solution.py:582
  61.8 9.6 %collective-permute-done.6.refs_2_ = f32[2,64,256]{2,1,0:T(8,128)S(1)} collective-permute-done((f32[2,64,256]{2,1,0:T(8,128)S(1)}, f32[2,64,256]{2,1,0:T(8,128)S(1)}, u32[]{:S(2)}, u32[]{:S(2)}) %collective-permute-start.6) | collective-permute-done | bytes 131104 | tf_op jit(solution)/shard_map/ppermute | solution.py:547
  71.4 0.6 shard_map.71
  72.0 0.0 collective-permute-done.22.middle_ref
  72.0 0.8 %collective-permute-done.23.outer_ref = f32[8,64,256]{2,1,0:T(8,128)S(1)} collective-permute-done((f32[8,64,256]{2,1,0:T(8,128)S(1)}, f32[8,64,256]{2,1,0:T(8,128)S(1)}, u32[]{:S(2)}, u32[]{:S(2)}) %collective-permute-start.23) | collective-permute-done | bytes 524320 | tf_op jit(solution)/shard_map/ppermute | solution.py:574
  72.8 1.2 %shard_map.73 = f32[32,2,2048]{2,1,0:T(2,128)} custom-call(f32[8,64,256]{2,1,0:T(8,128)S(1)} %get-tuple-element.38.part_ref, f32[8,8,256]{2,1,0:T(8,128)S(1)} %get-tuple-element.39.level_ref, f32[8,64,256]{2,1,0:T(8,128)S(1)} %collective-permute-done.22.middle_ref, f32[8,64,256]{2,1,0:T(8,128)S(1)} %collective-permute-done.23.outer_ref, ...), custom_call_target="tpu_custom_call" | custom-call | flops 33554432 | bytes 2097152 | tf_op jit(solution)/shard_map/pallas_call | solution.py:610
  (10 shorter events, 0.1 us)
Async XLA Ops:
  1.3 1.8 %collective-permute-start = (f32[4,72,256]{2,1,0:T(8,128)S(1)}, f32[4,72,256]{2,1,0:T(8,128)S(1)}, u32[]{:S(2)}, u32[]{:S(2)}) collective-permute-start(f32[4,72,256]{2,1,0:T(8,128)S(1)} %get-tuple-element.24), channel_id=1, source_target_pairs={{0,1},{1,0},{2,3},{3,2},{4,5},{5,4},{6,7},{7,6},{8,9},{9,8},{10,11... | collective-permute-start | bytes 884744 | tf_op jit(solution)/shard_map/ppermute | solution.py:28
  3.1 7.6 %collective-permute-start.1 = (f32[2,72,256]{2,1,0:T(8,128)S(1)}, f32[2,72,256]{2,1,0:T(8,128)S(1)}, u32[]{:S(2)}, u32[]{:S(2)}) collective-permute-start(f32[2,72,256]{2,1,0:T(8,128)S(1)} %get-tuple-element.25), channel_id=1, source_target_pairs={{0,2},{1,3},{2,0},{3,1},{4,6},{5,7},{6,4},{7,5},{8,10},{9,11},{10,... | collective-permute-start | bytes 442376 | tf_op jit(solution)/shard_map/ppermute | solution.py:28
  6.0 8.8 %collective-permute-start.2 = (f32[2,72,256]{2,1,0:T(8,128)S(1)}, f32[2,72,256]{2,1,0:T(8,128)S(1)}, u32[]{:S(2)}, u32[]{:S(2)}) collective-permute-start(f32[2,72,256]{2,1,0:T(8,128)S(1)} %get-tuple-element.26), channel_id=1, source_target_pairs={{0,4},{1,5},{2,6},{3,7},{4,0},{5,1},{6,2},{7,3},{8,12},{9,13},{10,... | collective-permute-start | bytes 442376 | tf_op jit(solution)/shard_map/ppermute | solution.py:28
  7.5 7.3 %collective-permute-start.3 = (f32[2,72,256]{2,1,0:T(8,128)S(1)}, f32[2,72,256]{2,1,0:T(8,128)S(1)}, u32[]{:S(2)}, u32[]{:S(2)}) collective-permute-start(f32[2,72,256]{2,1,0:T(8,128)S(1)} %get-tuple-element.27), channel_id=1, source_target_pairs={{0,6},{1,7},{2,4},{3,5},{4,2},{5,3},{6,0},{7,1},{8,14},{9,15},{10,... | collective-permute-start | bytes 442376 | tf_op jit(solution)/shard_map/ppermute | solution.py:28
  15.3 1.6 %collective-permute-start.4 = (f32[4,64,256]{2,1,0:T(8,128)S(1)}, f32[4,64,256]{2,1,0:T(8,128)S(1)}, u32[]{:S(2)}, u32[]{:S(2)}) collective-permute-start(f32[4,64,256]{2,1,0:T(8,128)S(1)} %get-tuple-element.29), channel_id=1, source_target_pairs={{0,1},{1,0},{2,3},{3,2},{4,5},{5,4},{6,7},{7,6},{8,9},{9,8},{10,11... | collective-permute-start | bytes 786440 | tf_op jit(solution)/shard_map/ppermute | solution.py:28
  16.9 6.3 %collective-permute-start.7 = (f32[2,64,256]{2,1,0:T(8,128)S(1)}, f32[2,64,256]{2,1,0:T(8,128)S(1)}, u32[]{:S(2)}, u32[]{:S(2)}) collective-permute-start(f32[2,64,256]{2,1,0:T(8,128)S(1)} %get-tuple-element.31), channel_id=1, source_target_pairs={{0,2},{1,3},{2,0},{3,1},{4,6},{5,7},{6,4},{7,5},{8,10},{9,11},{10,... | collective-permute-start | bytes 393224 | tf_op jit(solution)/shard_map/ppermute | solution.py:28
  18.2 6.4 %collective-permute-start.8 = (f32[2,64,256]{2,1,0:T(8,128)S(1)}, f32[2,64,256]{2,1,0:T(8,128)S(1)}, u32[]{:S(2)}, u32[]{:S(2)}) collective-permute-start(f32[2,64,256]{2,1,0:T(8,128)S(1)} %get-tuple-element.32), channel_id=1, source_target_pairs={{0,4},{1,5},{2,6},{3,7},{4,0},{5,1},{6,2},{7,3},{8,12},{9,13},{10,... | collective-permute-start | bytes 393224 | tf_op jit(solution)/shard_map/ppermute | solution.py:28
  19.0 7.2 %collective-permute-start.9 = (f32[2,64,256]{2,1,0:T(8,128)S(1)}, f32[2,64,256]{2,1,0:T(8,128)S(1)}, u32[]{:S(2)}, u32[]{:S(2)}) collective-permute-start(f32[2,64,256]{2,1,0:T(8,128)S(1)} %get-tuple-element.33), channel_id=1, source_target_pairs={{0,6},{1,7},{2,4},{3,5},{4,2},{5,3},{6,0},{7,1},{8,14},{9,15},{10,... | collective-permute-start | bytes 393224 | tf_op jit(solution)/shard_map/ppermute | solution.py:28
  26.8 19.2 %collective-permute-start.10 = (f32[6,64,256]{2,1,0:T(8,128)S(1)}, f32[6,64,256]{2,1,0:T(8,128)S(1)}, u32[]{:S(2)}, u32[]{:S(2)}) collective-permute-start(f32[6,64,256]{2,1,0:T(8,128)S(1)} %get-tuple-element.35.refs_3_), channel_id=1, source_target_pairs={{0,16},{24,8},{8,0},{16,24},{1,17},{25,9},{9,1},{17,25},{2,18},{26... | collective-permute-start | bytes 1179656 | tf_op jit(solution)/shard_map/ppermute | solution.py:560
  29.4 16.5 %collective-permute-start.5 = (f32[2,64,256]{2,1,0:T(8,128)S(1)}, f32[2,64,256]{2,1,0:T(8,128)S(1)}, u32[]{:S(2)}, u32[]{:S(2)}) collective-permute-start(f32[2,64,256]{2,1,0:T(8,128)S(1)} %get-tuple-element.30.refs_0_), channel_id=1, source_target_pairs={{0,16},{24,8},{8,0},{16,24},{1,17},{25,9},{9,1},{17,25},{2,18},{26... | collective-permute-start | bytes 393224 | tf_op jit(solution)/shard_map/ppermute | solution.py:546
  31.0 11.6 %collective-permute-start.14 = (f32[32,128]{1,0:T(8,128)S(1)}, f32[32,128]{1,0:T(8,128)S(1)}, u32[]{:S(2)}, u32[]{:S(2)}) collective-permute-start(f32[32,128]{1,0:T(8,128)S(1)} %get-tuple-element.36.own_ref), channel_id=1, source_target_pairs={{0,24},{8,16},{16,8},{24,0},{1,25},{9,17},{17,9},{25,1},{2,26},{10... | collective-permute-start | bytes 49160 | tf_op jit(solution)/shard_map/ppermute | solution.py:28
  31.2 12.0 %collective-permute-start.13 = (f32[32,128]{1,0:T(8,128)S(1)}, f32[32,128]{1,0:T(8,128)S(1)}, u32[]{:S(2)}, u32[]{:S(2)}) collective-permute-start(f32[32,128]{1,0:T(8,128)S(1)} %get-tuple-element.36.own_ref), channel_id=1, source_target_pairs={{0,16},{8,24},{16,0},{24,8},{1,17},{9,25},{17,1},{25,9},{2,18},{10... | collective-permute-start | bytes 49160 | tf_op jit(solution)/shard_map/ppermute | solution.py:28
  32.9 10.4 %collective-permute-start.12 = (f32[32,128]{1,0:T(8,128)S(1)}, f32[32,128]{1,0:T(8,128)S(1)}, u32[]{:S(2)}, u32[]{:S(2)}) collective-permute-start(f32[32,128]{1,0:T(8,128)S(1)} %get-tuple-element.36.own_ref), channel_id=1, source_target_pairs={{0,8},{8,0},{16,24},{24,16},{1,9},{9,1},{17,25},{25,17},{2,10},{10... | collective-permute-start | bytes 49160 | tf_op jit(solution)/shard_map/ppermute | solution.py:28
  43.3 5.7 %collective-permute-start.20 = (f32[168,128]{1,0:T(8,128)S(1)}, f32[168,128]{1,0:T(8,128)S(1)}, u32[]{:S(2)}, u32[]{:S(2)}) collective-permute-start(f32[168,128]{1,0:T(8,128)S(1)} %shard_map.69.refs_0_), channel_id=1, source_target_pairs={{0,6},{1,7},{2,4},{3,5},{4,2},{5,3},{6,0},{7,1},{8,14},{9,15},{10,... | collective-permute-start | bytes 258056 | tf_op jit(solution)/shard_map/ppermute | solution.py:28
  44.6 6.0 %collective-permute-start.18 = (f32[168,128]{1,0:T(8,128)S(1)}, f32[168,128]{1,0:T(8,128)S(1)}, u32[]{:S(2)}, u32[]{:S(2)}) collective-permute-start(f32[168,128]{1,0:T(8,128)S(1)} %shard_map.69.refs_0_), channel_id=1, source_target_pairs={{0,4},{1,5},{2,6},{3,7},{4,0},{5,1},{6,2},{7,3},{8,12},{9,13},{10,... | collective-permute-start | bytes 258056 | tf_op jit(solution)/shard_map/ppermute | solution.py:28
  45.3 26.7 %collective-permute-start.22 = (f32[8,64,256]{2,1,0:T(8,128)S(1)}, f32[8,64,256]{2,1,0:T(8,128)S(1)}, u32[]{:S(2)}, u32[]{:S(2)}) collective-permute-start(f32[8,64,256]{2,1,0:T(8,128)S(1)} %get-tuple-element.40), channel_id=1, source_target_pairs={{8,16},{16,8},{9,17},{17,9},{10,18},{18,10},{11,19},{19,11},{12,20... | collective-permute-start | bytes 1572872 | tf_op jit(solution)/shard_map/ppermute | solution.py:570
  46.0 26.8 %collective-permute-start.23 = (f32[8,64,256]{2,1,0:T(8,128)S(1)}, f32[8,64,256]{2,1,0:T(8,128)S(1)}, u32[]{:S(2)}, u32[]{:S(2)}) collective-permute-start(f32[8,64,256]{2,1,0:T(8,128)S(1)} %shard_map.72), channel_id=1, source_target_pairs={{8,0},{16,24},{9,1},{17,25},{10,2},{18,26},{11,3},{19,27},{12,4},{... | collective-permute-start | bytes 1572872 | tf_op jit(solution)/shard_map/ppermute | solution.py:574
  47.3 4.6 %collective-permute-start.16 = (f32[168,128]{1,0:T(8,128)S(1)}, f32[168,128]{1,0:T(8,128)S(1)}, u32[]{:S(2)}, u32[]{:S(2)}) collective-permute-start(f32[168,128]{1,0:T(8,128)S(1)} %shard_map.69.refs_0_), channel_id=1, source_target_pairs={{0,2},{1,3},{2,0},{3,1},{4,6},{5,7},{6,4},{7,5},{8,10},{9,11},{10,... | collective-permute-start | bytes 258056 | tf_op jit(solution)/shard_map/ppermute | solution.py:28
  49.0 6.0 %collective-permute-start.15 = (f32[168,128]{1,0:T(8,128)S(1)}, f32[168,128]{1,0:T(8,128)S(1)}, u32[]{:S(2)}, u32[]{:S(2)}) collective-permute-start(f32[168,128]{1,0:T(8,128)S(1)} %shard_map.69.refs_0_), channel_id=1, source_target_pairs={{0,1},{1,0},{2,3},{3,2},{4,5},{5,4},{6,7},{7,6},{8,9},{9,8},{10,11... | collective-permute-start | bytes 258056 | tf_op jit(solution)/shard_map/ppermute | solution.py:28
  50.6 4.5 %collective-permute-start.21 = (f32[168,128]{1,0:T(8,128)S(1)}, f32[168,128]{1,0:T(8,128)S(1)}, u32[]{:S(2)}, u32[]{:S(2)}) collective-permute-start(f32[168,128]{1,0:T(8,128)S(1)} %collective-permute-done.20.refs_6_), channel_id=1, source_target_pairs={{0,1},{1,0},{2,3},{3,2},{4,5},{5,4},{6,7},{7,6},{8,9},{9,8},{10,11... | collective-permute-start | bytes 258056 | tf_op jit(solution)/shard_map/ppermute | solution.py:28
  51.9 19.6 %collective-permute-start.11 = (f32[6,64,256]{2,1,0:T(8,128)S(1)}, f32[6,64,256]{2,1,0:T(8,128)S(1)}, u32[]{:S(2)}, u32[]{:S(2)}) collective-permute-start(f32[6,64,256]{2,1,0:T(8,128)S(1)} %get-tuple-element.35.refs_3_), channel_id=1, source_target_pairs={{0,8},{24,16},{8,24},{16,0},{1,9},{25,17},{9,25},{17,1},{2,10},{26... | collective-permute-start | bytes 1179656 | tf_op jit(solution)/shard_map/ppermute | solution.py:561
  55.0 1.3 %collective-permute-start.19 = (f32[168,128]{1,0:T(8,128)S(1)}, f32[168,128]{1,0:T(8,128)S(1)}, u32[]{:S(2)}, u32[]{:S(2)}) collective-permute-start(f32[168,128]{1,0:T(8,128)S(1)} %collective-permute-done.18.refs_4_), channel_id=1, source_target_pairs={{0,1},{1,0},{2,3},{3,2},{4,5},{5,4},{6,7},{7,6},{8,9},{9,8},{10,11... | collective-permute-start | bytes 258056 | tf_op jit(solution)/shard_map/ppermute | solution.py:28
  55.0 1.4 %collective-permute-start.17 = (f32[168,128]{1,0:T(8,128)S(1)}, f32[168,128]{1,0:T(8,128)S(1)}, u32[]{:S(2)}, u32[]{:S(2)}) collective-permute-start(f32[168,128]{1,0:T(8,128)S(1)} %collective-permute-done.16.refs_2_), channel_id=1, source_target_pairs={{0,1},{1,0},{2,3},{3,2},{4,5},{5,4},{6,7},{7,6},{8,9},{9,8},{10,11... | collective-permute-start | bytes 258056 | tf_op jit(solution)/shard_map/ppermute | solution.py:28
  56.3 15.1 %collective-permute-start.6 = (f32[2,64,256]{2,1,0:T(8,128)S(1)}, f32[2,64,256]{2,1,0:T(8,128)S(1)}, u32[]{:S(2)}, u32[]{:S(2)}) collective-permute-start(f32[2,64,256]{2,1,0:T(8,128)S(1)} %get-tuple-element.30.refs_0_), channel_id=1, source_target_pairs={{0,8},{24,16},{8,24},{16,0},{1,9},{25,17},{9,25},{17,1},{2,10},{26... | collective-permute-start | bytes 393224 | tf_op jit(solution)/shard_map/ppermute | solution.py:547

commit v4 on v3

--- a/solution.py
+++ b/solution.py
@@ -166,20 +166,12 @@
         copy.start()
     ens_ref, forcing_ref, cell_ref, value_ref, var_ref, noise_ref = targets
     members_dev, planes_dev, cells = ens_ref.shape
-    blocks, rows, width = give_ref.shape
-    state_rows = planes_dev * members_dev
+    blocks, rows, _ = give_ref.shape
+    strips = cells // (2 * blocks * LANES)
+    state_rows = strips * planes_dev * members_dev
     me = lax.axis_index("space")
-    for copy in copies:
+    for copy in copies[1:]:
         copy.wait()
-    tail = jnp.zeros((rows - state_rows - planes_dev, width), jnp.float32)
-    for hop in range(blocks):
-        for ref, flip in ((give_ref, 1), (keep_ref, 0)):
-            first = jnp.bitwise_xor(me, 2 * hop + flip) * width
-            span = pl.ds(pl.multiple_of(first, width), width)
-            for plane in range(planes_dev):
-                top = plane * members_dev
-                ref[hop, top : top + members_dev, :] = ens_ref[:, plane, span]
-            ref[hop, state_rows:, :] = jnp.concatenate([forcing_ref[:, span], tail], axis=0)
     local = cell_ref[...] - me * (planes_dev * cells)
     local_ref[...] = local
     side_ref[:members_dev] = value_ref[...] + jnp.sqrt(var_ref[...]) * noise_ref[...]
@@ -188,38 +180,69 @@
         place = place + jnp.where(local >= plane * cells, 1.0, 0.0)
     fill = jnp.zeros((SUBLANES - 2, local.shape[1]), jnp.float32)
     side_ref[members_dev:] = jnp.concatenate([var_ref[...], place, fill], axis=0)
+    copies[0].wait()
+    tail = jnp.zeros((rows - state_rows - strips * planes_dev, LANES), jnp.float32)
+    for hop in range(blocks):
+        for ref, flip in ((give_ref, 1), (keep_ref, 0)):
+            first = jnp.bitwise_xor(me, 2 * hop + flip) * (strips * LANES)
+            drive = []
+            for strip in range(strips):
+                lanes = pl.ds(pl.multiple_of(first + strip * LANES, LANES), LANES)
+                for plane in range(planes_dev):
+                    top = (strip * planes_dev + plane) * members_dev
+                    ref[hop, top : top + members_dev, :] = ens_ref[:, plane, lanes]
+                drive.append(forcing_ref[:, lanes])
+            ref[hop, state_rows:, :] = jnp.concatenate(drive + [tail], axis=0)
+
+
+def join_sent_kernel(keep_ref, got_ref, *outs, state_rows, drive_rows):
+    both = (keep_ref, got_ref)
+    for hop, out in enumerate(outs):
+        for n, ref in enumerate(both):
+            out[n * state_rows : (n + 1) * state_rows, :] = ref[hop + 1, :state_rows]
+        drive = [ref[hop + 1, state_rows : state_rows + drive_rows] for ref in both]
+        spare = out.shape[0] - 2 * (state_rows + drive_rows)
+        if spare:
+            drive.append(jnp.zeros((spare, LANES), jnp.float32))
+        out[2 * state_rows :, :] = jnp.concatenate(drive, axis=0)
 
 
 def join_kernel(keep_ref, got_ref, *outs):
-    skip = keep_ref.shape[0] - len(outs)
     for hop, out in enumerate(outs):
-        out[0] = keep_ref[hop + skip]
-        out[1] = got_ref[hop + skip]
+        out[0] = keep_ref[hop]
+        out[1] = got_ref[hop]
 
 
 def forecast_kernel(*refs, planes_dev, members_dev, slabs):
     keep_ref, got_ref, others = refs[0], refs[1], refs[2 : 1 + slabs // 2]
     own_ref, cross_ref, grid_ref = refs[1 + slabs // 2 :]
-    width = own_ref.shape[2]
-    state_rows = planes_dev * members_dev
+    strips = own_ref.shape[2] // LANES
+    strip_rows = planes_dev * members_dev
+    state_rows, drive_rows = strips * strip_rows, strips * planes_dev
     count = slabs * planes_dev
     me = lax.axis_index("space")
     grid_ref[me] = keep_ref[0]
     grid_ref[jnp.bitwise_xor(me, 1)] = got_ref[0]
     for hop, other in enumerate(others):
         for flip in range(2):
-            grid_ref[jnp.bitwise_xor(me, 2 * hop + 2 + flip)] = other[flip]
-    for lane in range(0, width, LANES):
-        lanes = slice(lane, lane + LANES)
+            slab = jnp.bitwise_xor(me, 2 * hop + 2 + flip)
+            grid_ref[slab, :state_rows] = other[flip * state_rows : (flip + 1) * state_rows]
+            first = 2 * state_rows + flip * drive_rows
+            grid_ref[slab, state_rows : state_rows + drive_rows] = other[first : first + drive_rows]
+    for strip in range(strips):
         drive = []
         for plane in range(count):
-            row = state_rows + plane % planes_dev
-            drive.append(grid_ref[plane // planes_dev, row : row + 1, lanes])
+            row = state_rows + strip * planes_dev + plane % planes_dev
+            drive.append(grid_ref[plane // planes_dev, row : row + 1, :])
         for member in range(0, members_dev, SUBLANES):
-            column = []
-            for plane in range(count):
-                top = (plane % planes_dev) * members_dev + member
-                column.append(grid_ref[plane // planes_dev, top : top + SUBLANES, lanes])
+            tops = [
+                strip * strip_rows + (plane % planes_dev) * members_dev + member
+                for plane in range(count)
+            ]
+            column = [
+                grid_ref[plane // planes_dev, tops[plane] : tops[plane] + SUBLANES, :]
+                for plane in range(count)
+            ]
             for _ in range(FSTEPS):
                 column = [
                     column[n]
@@ -232,11 +255,14 @@
                     for n in range(count)
                 ]
             for plane in range(count):
-                top = (plane % planes_dev) * members_dev + member
-                grid_ref[plane // planes_dev, top : top + SUBLANES, lanes] = column[plane]
+                top = tops[plane]
+                grid_ref[plane // planes_dev, top : top + SUBLANES, :] = column[plane]
     for hop in range(slabs // 2):
-        own_ref[hop] = grid_ref[jnp.bitwise_xor(me, 2 * hop), :state_rows]
-        cross_ref[hop] = grid_ref[jnp.bitwise_xor(me, 2 * hop + 1), :state_rows]
+        for ref, flip in ((own_ref, 0), (cross_ref, 1)):
+            slab = jnp.bitwise_xor(me, 2 * hop + flip)
+            for strip in range(strips):
+                rows = slice(strip * strip_rows, (strip + 1) * strip_rows)
+                ref[hop, :, strip * LANES : (strip + 1) * LANES] = grid_ref[slab, rows]
 
 
 def observe_kernel(*refs, planes_dev, members_dev, plane_cells):
@@ -504,7 +530,10 @@
     reach_slabs = min(8, slabs // 4)
     width = plane_cells // slabs
     state_rows = planes_dev * members_dev
-    sent_rows = round_up(state_rows + planes_dev, SUBLANES)
+    strips = width // LANES
+    strip_rows, drive_rows = strips * state_rows, strips * planes_dev
+    held_rows = round_up(strip_rows + drive_rows, SUBLANES)
+    sent_rows = 2 * strip_rows + round_up(2 * drive_rows, SUBLANES)
     state_bytes = 4 * ensemble.size
     hops = slabs // 2
     sizes = dict(planes_dev=planes_dev, members_dev=members_dev)
@@ -514,8 +543,8 @@
     give, keep, side, local = on_core(
         functools.partial(pack_kernel, count=len(inputs)),
         [
-            (hops, sent_rows, width),
-            (hops, sent_rows, width),
+            (hops, held_rows, LANES),
+            (hops, held_rows, LANES),
             (members_dev + SUBLANES, obs_dev),
             jax.ShapeDtypeStruct((1, obs_dev), jnp.int32),
         ],
@@ -526,14 +555,19 @@
         in_specs=[pl.BlockSpec(memory_space=pltpu.HBM)] * len(inputs),
     )(*inputs)
     got = flipped(give, "space", 1)
-    sent = on_core(join_kernel, [(2, sent_rows, width)] * (hops - 1), 1, 2 * state_bytes)(keep, got)
+    sent = on_core(
+        functools.partial(join_sent_kernel, state_rows=strip_rows, drive_rows=drive_rows),
+        [(sent_rows, LANES)] * (hops - 1),
+        1,
+        2 * state_bytes,
+    )(keep, got)
     come = [flipped(sent[n - 1], "space", 2 * n) for n in range(1, hops)]
     own, cross = on_core(
         functools.partial(forecast_kernel, slabs=slabs, **sizes),
         [(hops, state_rows, width)] * 2,
         24 * ensemble.size,
         2 * state_bytes,
-        scratch=[pltpu.VMEM((slabs, sent_rows, width), jnp.float32)],
+        scratch=[pltpu.VMEM((slabs, held_rows, LANES), jnp.float32)],
     )(keep, got, *come)
 
     crossed = flipped(cross, "space", 1)

time: 74.2 us -> 74 us (level)
  no operation moved by 1% of the time
where the time goes in v4:
time: 74 us; the launch traced here: 73.7 us
  waiting for transfers between devices  37.4 us (51%)
  starting transfers between devices  26.5 us (36%)
  Pallas kernels  9.74 us (13%)
    ppermute x18, waiting for transfers between devices, flipped(): return lax.ppermute(value, axis, [(i, i ^ mask) for i in range(count)])  26.9 us
    ppermute x18, starting transfers between devices, flipped(): return lax.ppermute(value, axis, [(i, i ^ mask) for i in range(count)])  17.2 us
    ppermute x1, waiting for transfers between devices, replicated(): home_trail = lax.ppermute(home, 'mem', trailing)  9.64 us
    pallas_call x1, Pallas kernels, replicated(): on_core(functools.partial(solve_kernel, members=members, pair=pair, reach...  5.32 us
    ppermute x1, starting transfers between devices, replicated(): rest_trail = lax.ppermute(rest, 'mem', trailing)  3.13 us
    ppermute x1, starting transfers between devices, replicated(): rest_lead = lax.ppermute(rest, 'mem', leading)  2.64 us
    ppermute x1, starting transfers between devices, replicated(): home_lead = lax.ppermute(home, 'mem', leading)  1.58 us
    pallas_call x1, Pallas kernels, replicated(): on_core(functools.partial(pack_kernel, count=len(inputs)), [(hops, held_r...  1.53 us
  transfers between devices with their start and end apart: 24, of which 15 were waited for; matrix products, arithmetic and copies ran while one was open for 0% of the time, Pallas kernels for 8%

profile of v4, /device:TPU:0, one launch (start us, length us, event | category | flops | bytes accessed | tf_op | source)
XLA Modules:
  0.0 73.7 jit_solution(4452205595239147155)
XLA Ops:
  0.0 1.5 %shard_map.64 = (f32[4,136,128]{2,1,0:T(8,128)S(1)}, f32[4,136,128]{2,1,0:T(8,128)S(1)}, f32[40,128]{1,0:T(8,128)S(1)}, s32[1,128]{1,0:T(1,128)S(1)}) custom-call(f32[32,2,2048]{2,1,0:T(2,128)} %refs_0_.1, f32[2,2048]{1,0:T(2,128)} %refs_1_.1, s32[1,128]{1,0:T(1,128)} %bitcast.3, f32[1,128]{1,0:T(1,128)} %bitcast.4, f32[1,128]{1,0:T(1,128)} %bitcast.5, ...), custom_call_target="tpu_custom_call" | custom-call | flops 131072 | bytes 1048576 | tf_op jit(solution)/shard_map/pallas_call | solution.py:543
  1.5 0.6 collective-permute-start
  2.1 1.2 %collective-permute-done.got_ref.refs_1_ = f32[4,136,128]{2,1,0:T(8,128)S(1)} collective-permute-done((f32[4,136,128]{2,1,0:T(8,128)S(1)}, f32[4,136,128]{2,1,0:T(8,128)S(1)}, u32[]{:S(2)}, u32[]{:S(2)}) %collective-permute-start) | collective-permute-done | bytes 278560 | tf_op jit(solution)/shard_map/ppermute | solution.py:28
  3.3 2.9 %collective-permute-start.1 = (f32[264,128]{1,0:T(8,128)S(1)}, f32[264,128]{1,0:T(8,128)S(1)}, u32[]{:S(2)}, u32[]{:S(2)}) collective-permute-start(f32[264,128]{1,0:T(8,128)S(1)} %get-tuple-element.25), channel_id=1, source_target_pairs={{0,2},{1,3},{2,0},{3,1},{4,6},{5,7},{6,4},{7,5},{8,10},{9,11},{10,... | collective-permute-start | bytes 405512 | tf_op jit(solution)/shard_map/ppermute | solution.py:28
  6.2 1.5 %collective-permute-start.2 = (f32[264,128]{1,0:T(8,128)S(1)}, f32[264,128]{1,0:T(8,128)S(1)}, u32[]{:S(2)}, u32[]{:S(2)}) collective-permute-start(f32[264,128]{1,0:T(8,128)S(1)} %get-tuple-element.26), channel_id=1, source_target_pairs={{0,4},{1,5},{2,6},{3,7},{4,0},{5,1},{6,2},{7,3},{8,12},{9,13},{10,... | collective-permute-start | bytes 405512 | tf_op jit(solution)/shard_map/ppermute | solution.py:28
  7.7 0.0 collective-permute-start.3
  7.8 2.6 %collective-permute-done.1.refs_2_ = f32[264,128]{1,0:T(8,128)S(1)} collective-permute-done((f32[264,128]{1,0:T(8,128)S(1)}, f32[264,128]{1,0:T(8,128)S(1)}, u32[]{:S(2)}, u32[]{:S(2)}) %collective-permute-start.1) | collective-permute-done | bytes 135200 | tf_op jit(solution)/shard_map/ppermute | solution.py:28
  10.4 4.1 %collective-permute-done.2.refs_3_ = f32[264,128]{1,0:T(8,128)S(1)} collective-permute-done((f32[264,128]{1,0:T(8,128)S(1)}, f32[264,128]{1,0:T(8,128)S(1)}, u32[]{:S(2)}, u32[]{:S(2)}) %collective-permute-start.2) | collective-permute-done | bytes 135200 | tf_op jit(solution)/shard_map/ppermute | solution.py:28
  14.5 0.0 collective-permute-done.3.refs_4_
  14.5 0.5 shard_map.66
  15.0 0.1 collective-permute-start.4
  15.1 1.5 %collective-permute-done.4.got_ref = f32[4,64,256]{2,1,0:T(8,128)S(1)} collective-permute-done((f32[4,64,256]{2,1,0:T(8,128)S(1)}, f32[4,64,256]{2,1,0:T(8,128)S(1)}, u32[]{:S(2)}, u32[]{:S(2)}) %collective-permute-start.4) | collective-permute-done | bytes 262176 | tf_op jit(solution)/shard_map/ppermute | solution.py:28
  16.6 1.3 %collective-permute-start.7 = (f32[2,64,256]{2,1,0:T(8,128)S(1)}, f32[2,64,256]{2,1,0:T(8,128)S(1)}, u32[]{:S(2)}, u32[]{:S(2)}) collective-permute-start(f32[2,64,256]{2,1,0:T(8,128)S(1)} %get-tuple-element.31), channel_id=1, source_target_pairs={{0,2},{1,3},{2,0},{3,1},{4,6},{5,7},{6,4},{7,5},{8,10},{9,11},{10,... | collective-permute-start | bytes 393224 | tf_op jit(solution)/shard_map/ppermute | solution.py:28
  17.9 0.8 %collective-permute-start.8 = (f32[2,64,256]{2,1,0:T(8,128)S(1)}, f32[2,64,256]{2,1,0:T(8,128)S(1)}, u32[]{:S(2)}, u32[]{:S(2)}) collective-permute-start(f32[2,64,256]{2,1,0:T(8,128)S(1)} %get-tuple-element.32), channel_id=1, source_target_pairs={{0,4},{1,5},{2,6},{3,7},{4,0},{5,1},{6,2},{7,3},{8,12},{9,13},{10,... | collective-permute-start | bytes 393224 | tf_op jit(solution)/shard_map/ppermute | solution.py:28
  18.7 1.4 %collective-permute-start.9 = (f32[2,64,256]{2,1,0:T(8,128)S(1)}, f32[2,64,256]{2,1,0:T(8,128)S(1)}, u32[]{:S(2)}, u32[]{:S(2)}) collective-permute-start(f32[2,64,256]{2,1,0:T(8,128)S(1)} %get-tuple-element.33), channel_id=1, source_target_pairs={{0,6},{1,7},{2,4},{3,5},{4,2},{5,3},{6,0},{7,1},{8,14},{9,15},{10,... | collective-permute-start | bytes 393224 | tf_op jit(solution)/shard_map/ppermute | solution.py:28
  20.2 2.7 %collective-permute-done.7.refs_1_ = f32[2,64,256]{2,1,0:T(8,128)S(1)} collective-permute-done((f32[2,64,256]{2,1,0:T(8,128)S(1)}, f32[2,64,256]{2,1,0:T(8,128)S(1)}, u32[]{:S(2)}, u32[]{:S(2)}) %collective-permute-start.7) | collective-permute-done | bytes 131104 | tf_op jit(solution)/shard_map/ppermute | solution.py:28
  22.9 1.5 %collective-permute-done.8.refs_2_ = f32[2,64,256]{2,1,0:T(8,128)S(1)} collective-permute-done((f32[2,64,256]{2,1,0:T(8,128)S(1)}, f32[2,64,256]{2,1,0:T(8,128)S(1)}, u32[]{:S(2)}, u32[]{:S(2)}) %collective-permute-start.8) | collective-permute-done | bytes 131104 | tf_op jit(solution)/shard_map/ppermute | solution.py:28
  24.4 1.6 %collective-permute-done.9.refs_3_ = f32[2,64,256]{2,1,0:T(8,128)S(1)} collective-permute-done((f32[2,64,256]{2,1,0:T(8,128)S(1)}, f32[2,64,256]{2,1,0:T(8,128)S(1)}, u32[]{:S(2)}, u32[]{:S(2)}) %collective-permute-start.9) | collective-permute-done | bytes 131104 | tf_op jit(solution)/shard_map/ppermute | solution.py:28
  26.0 0.5 shard_map.68
  26.5 2.6 %collective-permute-start.10 = (f32[6,64,256]{2,1,0:T(8,128)S(1)}, f32[6,64,256]{2,1,0:T(8,128)S(1)}, u32[]{:S(2)}, u32[]{:S(2)}) collective-permute-start(f32[6,64,256]{2,1,0:T(8,128)S(1)} %get-tuple-element.35.refs_3_), channel_id=1, source_target_pairs={{0,16},{24,8},{8,0},{16,24},{1,17},{25,9},{9,1},{17,25},{2,18},{26... | collective-permute-start | bytes 1179656 | tf_op jit(solution)/shard_map/ppermute | solution.py:594
  29.1 1.6 %collective-permute-start.5 = (f32[2,64,256]{2,1,0:T(8,128)S(1)}, f32[2,64,256]{2,1,0:T(8,128)S(1)}, u32[]{:S(2)}, u32[]{:S(2)}) collective-permute-start(f32[2,64,256]{2,1,0:T(8,128)S(1)} %get-tuple-element.30.refs_0_), channel_id=1, source_target_pairs={{0,16},{24,8},{8,0},{16,24},{1,17},{25,9},{9,1},{17,25},{2,18},{26... | collective-permute-start | bytes 393224 | tf_op jit(solution)/shard_map/ppermute | solution.py:580
  30.7 0.2 collective-permute-start.14
  30.9 1.7 %collective-permute-start.13 = (f32[32,128]{1,0:T(8,128)S(1)}, f32[32,128]{1,0:T(8,128)S(1)}, u32[]{:S(2)}, u32[]{:S(2)}) collective-permute-start(f32[32,128]{1,0:T(8,128)S(1)} %get-tuple-element.36.own_ref), channel_id=1, source_target_pairs={{0,16},{8,24},{16,0},{24,8},{1,17},{9,25},{17,1},{25,9},{2,18},{10... | collective-permute-start | bytes 49160 | tf_op jit(solution)/shard_map/ppermute | solution.py:28
  32.6 2.5 %collective-permute-start.12 = (f32[32,128]{1,0:T(8,128)S(1)}, f32[32,128]{1,0:T(8,128)S(1)}, u32[]{:S(2)}, u32[]{:S(2)}) collective-permute-start(f32[32,128]{1,0:T(8,128)S(1)} %get-tuple-element.36.own_ref), channel_id=1, source_target_pairs={{0,8},{8,0},{16,24},{24,16},{1,9},{9,1},{17,25},{25,17},{2,10},{10... | collective-permute-start | bytes 49160 | tf_op jit(solution)/shard_map/ppermute | solution.py:28
  35.1 7.2 %collective-permute-done.14.three_ref = f32[32,128]{1,0:T(8,128)S(1)} collective-permute-done((f32[32,128]{1,0:T(8,128)S(1)}, f32[32,128]{1,0:T(8,128)S(1)}, u32[]{:S(2)}, u32[]{:S(2)}) %collective-permute-start.14) | collective-permute-done | bytes 16416 | tf_op jit(solution)/shard_map/ppermute | solution.py:28
  42.3 0.7 collective-permute-done.13.two_ref
  43.0 1.3 %collective-permute-start.20 = (f32[168,128]{1,0:T(8,128)S(1)}, f32[168,128]{1,0:T(8,128)S(1)}, u32[]{:S(2)}, u32[]{:S(2)}) collective-permute-start(f32[168,128]{1,0:T(8,128)S(1)} %shard_map.69.refs_0_), channel_id=1, source_target_pairs={{0,6},{1,7},{2,4},{3,5},{4,2},{5,3},{6,0},{7,1},{8,14},{9,15},{10,... | collective-permute-start | bytes 258056 | tf_op jit(solution)/shard_map/ppermute | solution.py:28
  44.3 0.7 collective-permute-start.18
  45.0 0.7 collective-permute-start.22
  45.7 0.0 collective-permute-done.10.refs_4_.rest_ref
  45.7 1.3 %collective-permute-start.23 = (f32[8,64,256]{2,1,0:T(8,128)S(1)}, f32[8,64,256]{2,1,0:T(8,128)S(1)}, u32[]{:S(2)}, u32[]{:S(2)}) collective-permute-start(f32[8,64,256]{2,1,0:T(8,128)S(1)} %shard_map.72), channel_id=1, source_target_pairs={{8,0},{16,24},{9,1},{17,25},{10,2},{18,26},{11,3},{19,27},{12,4},{... | collective-permute-start | bytes 1572872 | tf_op jit(solution)/shard_map/ppermute | solution.py:608
  47.0 1.6 %collective-permute-start.16 = (f32[168,128]{1,0:T(8,128)S(1)}, f32[168,128]{1,0:T(8,128)S(1)}, u32[]{:S(2)}, u32[]{:S(2)}) collective-permute-start(f32[168,128]{1,0:T(8,128)S(1)} %shard_map.69.refs_0_), channel_id=1, source_target_pairs={{0,2},{1,3},{2,0},{3,1},{4,6},{5,7},{6,4},{7,5},{8,10},{9,11},{10,... | collective-permute-start | bytes 258056 | tf_op jit(solution)/shard_map/ppermute | solution.py:28
  48.7 0.0 collective-permute-start.15
  48.7 1.6 %collective-permute-done.18.refs_4_ = f32[168,128]{1,0:T(8,128)S(1)} collective-permute-done((f32[168,128]{1,0:T(8,128)S(1)}, f32[168,128]{1,0:T(8,128)S(1)}, u32[]{:S(2)}, u32[]{:S(2)}) %collective-permute-start.18) | collective-permute-done | bytes 86048 | tf_op jit(solution)/shard_map/ppermute | solution.py:28
  50.3 0.0 collective-permute-start.21
  50.3 1.3 %collective-permute-done.16.refs_2_ = f32[168,128]{1,0:T(8,128)S(1)} collective-permute-done((f32[168,128]{1,0:T(8,128)S(1)}, f32[168,128]{1,0:T(8,128)S(1)}, u32[]{:S(2)}, u32[]{:S(2)}) %collective-permute-start.16) | collective-permute-done | bytes 86048 | tf_op jit(solution)/shard_map/ppermute | solution.py:28
  51.6 3.1 %collective-permute-start.11 = (f32[6,64,256]{2,1,0:T(8,128)S(1)}, f32[6,64,256]{2,1,0:T(8,128)S(1)}, u32[]{:S(2)}, u32[]{:S(2)}) collective-permute-start(f32[6,64,256]{2,1,0:T(8,128)S(1)} %get-tuple-element.35.refs_3_), channel_id=1, source_target_pairs={{0,8},{24,16},{8,24},{16,0},{1,9},{25,17},{9,25},{17,1},{2,10},{26... | collective-permute-start | bytes 1179656 | tf_op jit(solution)/shard_map/ppermute | solution.py:595
  54.7 0.0 collective-permute-done.15.refs_1_
  54.7 0.0 collective-permute-start.19
  54.7 0.5 collective-permute-start.17
  55.2 0.8 %collective-permute-done.19.refs_5_ = f32[168,128]{1,0:T(8,128)S(1)} collective-permute-done((f32[168,128]{1,0:T(8,128)S(1)}, f32[168,128]{1,0:T(8,128)S(1)}, u32[]{:S(2)}, u32[]{:S(2)}) %collective-permute-start.19) | collective-permute-done | bytes 86048 | tf_op jit(solution)/shard_map/ppermute | solution.py:28
  56.0 0.0 collective-permute-start.6
  56.0 0.2 collective-permute-done.17.refs_3_
  56.1 5.3 %shard_map.70.refs_6_.gain_ref = f32[2,32,128]{2,1,0:T(8,128)S(1)} custom-call(f32[168,128]{1,0:T(8,128)S(1)} %shard_map.69.refs_0_, f32[168,128]{1,0:T(8,128)S(1)} %collective-permute-done.15.refs_1_, f32[168,128]{1,0:T(8,128)S(1)} %collective-permute-done.16.refs_2_, f32[168,128]{1,0:T(8,128)S(1)} %collective-permute-done.17.refs_3_, ...), custom_call_target="tpu_custom_call" | custom-call | flops 3221225472 | bytes 655360 | tf_op jit(solution)/shard_map/pallas_call | solution.py:616
  61.5 9.6 %collective-permute-done.6.refs_2_ = f32[2,64,256]{2,1,0:T(8,128)S(1)} collective-permute-done((f32[2,64,256]{2,1,0:T(8,128)S(1)}, f32[2,64,256]{2,1,0:T(8,128)S(1)}, u32[]{:S(2)}, u32[]{:S(2)}) %collective-permute-start.6) | collective-permute-done | bytes 131104 | tf_op jit(solution)/shard_map/ppermute | solution.py:581
  71.1 0.6 shard_map.71
  71.7 0.8 %collective-permute-done.23.outer_ref = f32[8,64,256]{2,1,0:T(8,128)S(1)} collective-permute-done((f32[8,64,256]{2,1,0:T(8,128)S(1)}, f32[8,64,256]{2,1,0:T(8,128)S(1)}, u32[]{:S(2)}, u32[]{:S(2)}) %collective-permute-start.23) | collective-permute-done | bytes 524320 | tf_op jit(solution)/shard_map/ppermute | solution.py:608
  72.5 1.2 %shard_map.73 = f32[32,2,2048]{2,1,0:T(2,128)} custom-call(f32[8,64,256]{2,1,0:T(8,128)S(1)} %get-tuple-element.38.part_ref, f32[8,8,256]{2,1,0:T(8,128)S(1)} %get-tuple-element.39.level_ref, f32[8,64,256]{2,1,0:T(8,128)S(1)} %collective-permute-done.22.middle_ref, f32[8,64,256]{2,1,0:T(8,128)S(1)} %collective-permute-done.23.outer_ref, ...), custom_call_target="tpu_custom_call" | custom-call | flops 33554432 | bytes 2097152 | tf_op jit(solution)/shard_map/pallas_call | solution.py:644
  (10 shorter events, 0.1 us)
Async XLA Ops:
  1.5 1.7 %collective-permute-start = (f32[4,136,128]{2,1,0:T(8,128)S(1)}, f32[4,136,128]{2,1,0:T(8,128)S(1)}, u32[]{:S(2)}, u32[]{:S(2)}) collective-permute-start(f32[4,136,128]{2,1,0:T(8,128)S(1)} %get-tuple-element.24), channel_id=1, source_target_pairs={{0,1},{1,0},{2,3},{3,2},{4,5},{5,4},{6,7},{7,6},{8,9},{9,8},{10,11... | collective-permute-start | bytes 835592 | tf_op jit(solution)/shard_map/ppermute | solution.py:28
  3.3 7.1 %collective-permute-start.1 = (f32[264,128]{1,0:T(8,128)S(1)}, f32[264,128]{1,0:T(8,128)S(1)}, u32[]{:S(2)}, u32[]{:S(2)}) collective-permute-start(f32[264,128]{1,0:T(8,128)S(1)} %get-tuple-element.25), channel_id=1, source_target_pairs={{0,2},{1,3},{2,0},{3,1},{4,6},{5,7},{6,4},{7,5},{8,10},{9,11},{10,... | collective-permute-start | bytes 405512 | tf_op jit(solution)/shard_map/ppermute | solution.py:28
  6.2 8.2 %collective-permute-start.2 = (f32[264,128]{1,0:T(8,128)S(1)}, f32[264,128]{1,0:T(8,128)S(1)}, u32[]{:S(2)}, u32[]{:S(2)}) collective-permute-start(f32[264,128]{1,0:T(8,128)S(1)} %get-tuple-element.26), channel_id=1, source_target_pairs={{0,4},{1,5},{2,6},{3,7},{4,0},{5,1},{6,2},{7,3},{8,12},{9,13},{10,... | collective-permute-start | bytes 405512 | tf_op jit(solution)/shard_map/ppermute | solution.py:28
  7.7 6.7 %collective-permute-start.3 = (f32[264,128]{1,0:T(8,128)S(1)}, f32[264,128]{1,0:T(8,128)S(1)}, u32[]{:S(2)}, u32[]{:S(2)}) collective-permute-start(f32[264,128]{1,0:T(8,128)S(1)} %get-tuple-element.27), channel_id=1, source_target_pairs={{0,6},{1,7},{2,4},{3,5},{4,2},{5,3},{6,0},{7,1},{8,14},{9,15},{10,... | collective-permute-start | bytes 405512 | tf_op jit(solution)/shard_map/ppermute | solution.py:28
  15.0 1.6 %collective-permute-start.4 = (f32[4,64,256]{2,1,0:T(8,128)S(1)}, f32[4,64,256]{2,1,0:T(8,128)S(1)}, u32[]{:S(2)}, u32[]{:S(2)}) collective-permute-start(f32[4,64,256]{2,1,0:T(8,128)S(1)} %get-tuple-element.29), channel_id=1, source_target_pairs={{0,1},{1,0},{2,3},{3,2},{4,5},{5,4},{6,7},{7,6},{8,9},{9,8},{10,11... | collective-permute-start | bytes 786440 | tf_op jit(solution)/shard_map/ppermute | solution.py:28
  16.6 6.3 %collective-permute-start.7 = (f32[2,64,256]{2,1,0:T(8,128)S(1)}, f32[2,64,256]{2,1,0:T(8,128)S(1)}, u32[]{:S(2)}, u32[]{:S(2)}) collective-permute-start(f32[2,64,256]{2,1,0:T(8,128)S(1)} %get-tuple-element.31), channel_id=1, source_target_pairs={{0,2},{1,3},{2,0},{3,1},{4,6},{5,7},{6,4},{7,5},{8,10},{9,11},{10,... | collective-permute-start | bytes 393224 | tf_op jit(solution)/shard_map/ppermute | solution.py:28
  17.9 6.4 %collective-permute-start.8 = (f32[2,64,256]{2,1,0:T(8,128)S(1)}, f32[2,64,256]{2,1,0:T(8,128)S(1)}, u32[]{:S(2)}, u32[]{:S(2)}) collective-permute-start(f32[2,64,256]{2,1,0:T(8,128)S(1)} %get-tuple-element.32), channel_id=1, source_target_pairs={{0,4},{1,5},{2,6},{3,7},{4,0},{5,1},{6,2},{7,3},{8,12},{9,13},{10,... | collective-permute-start | bytes 393224 | tf_op jit(solution)/shard_map/ppermute | solution.py:28
  18.7 7.2 %collective-permute-start.9 = (f32[2,64,256]{2,1,0:T(8,128)S(1)}, f32[2,64,256]{2,1,0:T(8,128)S(1)}, u32[]{:S(2)}, u32[]{:S(2)}) collective-permute-start(f32[2,64,256]{2,1,0:T(8,128)S(1)} %get-tuple-element.33), channel_id=1, source_target_pairs={{0,6},{1,7},{2,4},{3,5},{4,2},{5,3},{6,0},{7,1},{8,14},{9,15},{10,... | collective-permute-start | bytes 393224 | tf_op jit(solution)/shard_map/ppermute | solution.py:28
  26.5 19.2 %collective-permute-start.10 = (f32[6,64,256]{2,1,0:T(8,128)S(1)}, f32[6,64,256]{2,1,0:T(8,128)S(1)}, u32[]{:S(2)}, u32[]{:S(2)}) collective-permute-start(f32[6,64,256]{2,1,0:T(8,128)S(1)} %get-tuple-element.35.refs_3_), channel_id=1, source_target_pairs={{0,16},{24,8},{8,0},{16,24},{1,17},{25,9},{9,1},{17,25},{2,18},{26... | collective-permute-start | bytes 1179656 | tf_op jit(solution)/shard_map/ppermute | solution.py:594
  29.1 16.5 %collective-permute-start.5 = (f32[2,64,256]{2,1,0:T(8,128)S(1)}, f32[2,64,256]{2,1,0:T(8,128)S(1)}, u32[]{:S(2)}, u32[]{:S(2)}) collective-permute-start(f32[2,64,256]{2,1,0:T(8,128)S(1)} %get-tuple-element.30.refs_0_), channel_id=1, source_target_pairs={{0,16},{24,8},{8,0},{16,24},{1,17},{25,9},{9,1},{17,25},{2,18},{26... | collective-permute-start | bytes 393224 | tf_op jit(solution)/shard_map/ppermute | solution.py:580
  30.7 11.6 %collective-permute-start.14 = (f32[32,128]{1,0:T(8,128)S(1)}, f32[32,128]{1,0:T(8,128)S(1)}, u32[]{:S(2)}, u32[]{:S(2)}) collective-permute-start(f32[32,128]{1,0:T(8,128)S(1)} %get-tuple-element.36.own_ref), channel_id=1, source_target_pairs={{0,24},{8,16},{16,8},{24,0},{1,25},{9,17},{17,9},{25,1},{2,26},{10... | collective-permute-start | bytes 49160 | tf_op jit(solution)/shard_map/ppermute | solution.py:28
  30.9 12.0 %collective-permute-start.13 = (f32[32,128]{1,0:T(8,128)S(1)}, f32[32,128]{1,0:T(8,128)S(1)}, u32[]{:S(2)}, u32[]{:S(2)}) collective-permute-start(f32[32,128]{1,0:T(8,128)S(1)} %get-tuple-element.36.own_ref), channel_id=1, source_target_pairs={{0,16},{8,24},{16,0},{24,8},{1,17},{9,25},{17,1},{25,9},{2,18},{10... | collective-permute-start | bytes 49160 | tf_op jit(solution)/shard_map/ppermute | solution.py:28
  32.6 10.4 %collective-permute-start.12 = (f32[32,128]{1,0:T(8,128)S(1)}, f32[32,128]{1,0:T(8,128)S(1)}, u32[]{:S(2)}, u32[]{:S(2)}) collective-permute-start(f32[32,128]{1,0:T(8,128)S(1)} %get-tuple-element.36.own_ref), channel_id=1, source_target_pairs={{0,8},{8,0},{16,24},{24,16},{1,9},{9,1},{17,25},{25,17},{2,10},{10... | collective-permute-start | bytes 49160 | tf_op jit(solution)/shard_map/ppermute | solution.py:28
  43.0 5.7 %collective-permute-start.20 = (f32[168,128]{1,0:T(8,128)S(1)}, f32[168,128]{1,0:T(8,128)S(1)}, u32[]{:S(2)}, u32[]{:S(2)}) collective-permute-start(f32[168,128]{1,0:T(8,128)S(1)} %shard_map.69.refs_0_), channel_id=1, source_target_pairs={{0,6},{1,7},{2,4},{3,5},{4,2},{5,3},{6,0},{7,1},{8,14},{9,15},{10,... | collective-permute-start | bytes 258056 | tf_op jit(solution)/shard_map/ppermute | solution.py:28
  44.3 6.0 %collective-permute-start.18 = (f32[168,128]{1,0:T(8,128)S(1)}, f32[168,128]{1,0:T(8,128)S(1)}, u32[]{:S(2)}, u32[]{:S(2)}) collective-permute-start(f32[168,128]{1,0:T(8,128)S(1)} %shard_map.69.refs_0_), channel_id=1, source_target_pairs={{0,4},{1,5},{2,6},{3,7},{4,0},{5,1},{6,2},{7,3},{8,12},{9,13},{10,... | collective-permute-start | bytes 258056 | tf_op jit(solution)/shard_map/ppermute | solution.py:28
  45.0 26.7 %collective-permute-start.22 = (f32[8,64,256]{2,1,0:T(8,128)S(1)}, f32[8,64,256]{2,1,0:T(8,128)S(1)}, u32[]{:S(2)}, u32[]{:S(2)}) collective-permute-start(f32[8,64,256]{2,1,0:T(8,128)S(1)} %get-tuple-element.40), channel_id=1, source_target_pairs={{8,16},{16,8},{9,17},{17,9},{10,18},{18,10},{11,19},{19,11},{12,20... | collective-permute-start | bytes 1572872 | tf_op jit(solution)/shard_map/ppermute | solution.py:604
  45.7 26.8 %collective-permute-start.23 = (f32[8,64,256]{2,1,0:T(8,128)S(1)}, f32[8,64,256]{2,1,0:T(8,128)S(1)}, u32[]{:S(2)}, u32[]{:S(2)}) collective-permute-start(f32[8,64,256]{2,1,0:T(8,128)S(1)} %shard_map.72), channel_id=1, source_target_pairs={{8,0},{16,24},{9,1},{17,25},{10,2},{18,26},{11,3},{19,27},{12,4},{... | collective-permute-start | bytes 1572872 | tf_op jit(solution)/shard_map/ppermute | solution.py:608
  47.0 4.6 %collective-permute-start.16 = (f32[168,128]{1,0:T(8,128)S(1)}, f32[168,128]{1,0:T(8,128)S(1)}, u32[]{:S(2)}, u32[]{:S(2)}) collective-permute-start(f32[168,128]{1,0:T(8,128)S(1)} %shard_map.69.refs_0_), channel_id=1, source_target_pairs={{0,2},{1,3},{2,0},{3,1},{4,6},{5,7},{6,4},{7,5},{8,10},{9,11},{10,... | collective-permute-start | bytes 258056 | tf_op jit(solution)/shard_map/ppermute | solution.py:28
  48.7 6.0 %collective-permute-start.15 = (f32[168,128]{1,0:T(8,128)S(1)}, f32[168,128]{1,0:T(8,128)S(1)}, u32[]{:S(2)}, u32[]{:S(2)}) collective-permute-start(f32[168,128]{1,0:T(8,128)S(1)} %shard_map.69.refs_0_), channel_id=1, source_target_pairs={{0,1},{1,0},{2,3},{3,2},{4,5},{5,4},{6,7},{7,6},{8,9},{9,8},{10,11... | collective-permute-start | bytes 258056 | tf_op jit(solution)/shard_map/ppermute | solution.py:28
  50.3 4.5 %collective-permute-start.21 = (f32[168,128]{1,0:T(8,128)S(1)}, f32[168,128]{1,0:T(8,128)S(1)}, u32[]{:S(2)}, u32[]{:S(2)}) collective-permute-start(f32[168,128]{1,0:T(8,128)S(1)} %collective-permute-done.20.refs_6_), channel_id=1, source_target_pairs={{0,1},{1,0},{2,3},{3,2},{4,5},{5,4},{6,7},{7,6},{8,9},{9,8},{10,11... | collective-permute-start | bytes 258056 | tf_op jit(solution)/shard_map/ppermute | solution.py:28
  51.6 19.6 %collective-permute-start.11 = (f32[6,64,256]{2,1,0:T(8,128)S(1)}, f32[6,64,256]{2,1,0:T(8,128)S(1)}, u32[]{:S(2)}, u32[]{:S(2)}) collective-permute-start(f32[6,64,256]{2,1,0:T(8,128)S(1)} %get-tuple-element.35.refs_3_), channel_id=1, source_target_pairs={{0,8},{24,16},{8,24},{16,0},{1,9},{25,17},{9,25},{17,1},{2,10},{26... | collective-permute-start | bytes 1179656 | tf_op jit(solution)/shard_map/ppermute | solution.py:595
  54.7 1.3 %collective-permute-start.19 = (f32[168,128]{1,0:T(8,128)S(1)}, f32[168,128]{1,0:T(8,128)S(1)}, u32[]{:S(2)}, u32[]{:S(2)}) collective-permute-start(f32[168,128]{1,0:T(8,128)S(1)} %collective-permute-done.18.refs_4_), channel_id=1, source_target_pairs={{0,1},{1,0},{2,3},{3,2},{4,5},{5,4},{6,7},{7,6},{8,9},{9,8},{10,11... | collective-permute-start | bytes 258056 | tf_op jit(solution)/shard_map/ppermute | solution.py:28
  54.7 1.4 %collective-permute-start.17 = (f32[168,128]{1,0:T(8,128)S(1)}, f32[168,128]{1,0:T(8,128)S(1)}, u32[]{:S(2)}, u32[]{:S(2)}) collective-permute-start(f32[168,128]{1,0:T(8,128)S(1)} %collective-permute-done.16.refs_2_), channel_id=1, source_target_pairs={{0,1},{1,0},{2,3},{3,2},{4,5},{5,4},{6,7},{7,6},{8,9},{9,8},{10,11... | collective-permute-start | bytes 258056 | tf_op jit(solution)/shard_map/ppermute | solution.py:28
  56.0 15.1 %collective-permute-start.6 = (f32[2,64,256]{2,1,0:T(8,128)S(1)}, f32[2,64,256]{2,1,0:T(8,128)S(1)}, u32[]{:S(2)}, u32[]{:S(2)}) collective-permute-start(f32[2,64,256]{2,1,0:T(8,128)S(1)} %get-tuple-element.30.refs_0_), channel_id=1, source_target_pairs={{0,8},{24,16},{8,24},{16,0},{1,9},{25,17},{9,25},{17,1},{2,10},{26... | collective-permute-start | bytes 393224 | tf_op jit(solution)/shard_map/ppermute | solution.py:581
